TPU v7x, 32 devices: a whole 2x2x4 slice. The times are simulated.
32 devices in a mesh: grp: 2 (over y), pts: 4 (over z), col: 2 (over x), sub: 2 (over core).
Axes of the slice: x: 2, y: 2, z: 4, core: 2. Of those that a mesh axis runs over, the one named last changes fastest.
Arguments:
- points: bfloat16 [32768, 256], P(('grp', 'pts', 'sub')), parts along dimension 0, may hold values from -12 to 12
- weights: bfloat16 [32768, 128], P(('grp', 'pts', 'sub')), parts along dimension 0, may hold values from -0.046875 to 0.046875
- tile_rows: int32 [4, 8, 128], P(('grp', 'col'), ('pts', 'sub')), parts along dimension 0, may hold values from 0 to 2047, as said below
- tile_count: int32 [4, 8], P(('grp', 'col')), parts along dimension 0, may hold values from 1 to 128, 512 in all within a row
- sketch_pick: int32 [4, 256], P(('grp', 'col')), parts along dimension 0, may hold values from 0 to 511, as said below
- block_targets: bfloat16 [4, 1024, 128], P(('grp', 'col'), ('pts', 'sub')), parts along dimension 0, may hold values from -4 to 4
- core_inv: float32 [1024, 512], P('grp'), parts along dimension 0, as said below
Outputs:
- block_grad: float32 [4, 1024, 128], P(('grp', 'col'), ('pts', 'sub')), parts along dimension 0
- direction: float32 [4, 1024, 128], P(('grp', 'col'), ('pts', 'sub')), parts along dimension 0
There are 2 independent parts, one for each index of `grp`. A program takes and returns all parts, laid end to end along the dimension named above; each array names one. Nothing has to cross between parts.
Inputs may be any that keep to these rules, and one draw needn't show every extreme that they name: For each owner o, the 256 entries tile_rows[:, o, :] are distinct; only slots below tile_count are used. `tile_count`: each row of 8 counts sums to 512, and its largest count is 128. `sketch_pick`: the entries of one row are distinct. `core_inv`: A full-rank matrix.
All inputs are finite; a program needn't handle non-finite values.
Results may differ from a plain program's by a relative error of at most 0.0003.
Values may be sent and summed in bfloat16 or wider, within the bound.
No kernel may reach another device: no remote copies, remote signals or barrier semaphores. Data moves between devices by JAX's collectives and lax.ppermute only.
A program may use at most 64 MiB of HBM per device.

v0:
```python
import math

import jax
import jax.numpy as jnp
from jax import lax
from jax.sharding import PartitionSpec as P

RIDGE_COEF = 50.0
HIGHEST_PREC = lax.Precision.HIGHEST


def sq_norms(values):
    widened = values.astype(jnp.float32)
    return jnp.sum(widened * widened, axis=1)


def kernel_block(left_x, left_sq, right_x, right_sq):
    inner_prods = jnp.einsum("ik,jk->ij", left_x, right_x, preferred_element_type=jnp.float32)
    dist_sq = left_sq[:, None] + right_sq[None, :] - 2.0 * inner_prods
    return jnp.exp(-dist_sq / left_x.shape[1])


def pick_entry(table, position):
    return jnp.sum(jnp.where(jnp.arange(table.shape[0]) == position, table, 0))


def per_device(points, weights, tile_rows, tile_count, sketch_pick, block_targets, core_inv):
    slot_cap = tile_rows.shape[2]
    counts = tile_count[0]
    owner_total = counts.shape[0]
    live_total = owner_total * slot_cap // 2
    owner_idx = lax.axis_index(("pts", "sub"))
    offsets = jnp.cumsum(counts) - counts
    own_count = pick_entry(counts, owner_idx)
    slot_ids = jnp.arange(slot_cap, dtype=jnp.int32)
    used_float = (slot_ids < own_count).astype(jnp.float32)[:, None]
    own_rows = tile_rows[0, 0]
    own_x = jnp.where(used_float > 0, jnp.take(points, own_rows, axis=0), 0)
    own_alpha = jnp.take(weights, own_rows, axis=0).astype(jnp.float32)
    tile_x = lax.all_gather(own_x, ("pts", "sub"), axis=0, tiled=True)
    tile_sq = sq_norms(tile_x)
    slab_sq = sq_norms(points)
    slab_total = points.shape[0]
    slab_step = math.gcd(slab_total, 512)
    rank_ids = jnp.arange(live_total, dtype=jnp.int32)
    owner_of = jnp.sum((offsets[None, :] <= rank_ids[:, None]).astype(jnp.int32), axis=1) - 1
    owner_onehot = owner_of[:, None] == jnp.arange(owner_total)[None, :]
    live_slot = (
        owner_of * slot_cap
        + rank_ids
        - jnp.sum(jnp.where(owner_onehot, offsets[None, :], 0), axis=1)
    )

    def add_block(block_idx, running):
        slab_x = lax.dynamic_slice_in_dim(points, block_idx * slab_step, slab_step, 0)
        slab_w = lax.dynamic_slice_in_dim(weights, block_idx * slab_step, slab_step, 0).astype(
            jnp.float32
        )
        block_sq = lax.dynamic_slice_in_dim(slab_sq, block_idx * slab_step, slab_step, 0)
        kern_vals = kernel_block(tile_x, tile_sq, slab_x, block_sq)
        return running + jnp.dot(kern_vals, slab_w, precision=HIGHEST_PREC)

    start_sum = jnp.zeros((tile_x.shape[0], weights.shape[1]), jnp.float32)
    slab_part = lax.psum_scatter(
        lax.fori_loop(0, slab_total // slab_step, add_block, start_sum),
        ("pts", "sub"),
        scatter_dimension=0,
        tiled=True,
    )
    targets = block_targets[0].astype(jnp.float32)
    block_grad = used_float * (slab_part + RIDGE_COEF * own_alpha - targets)
    sketch_slot = jnp.take(live_slot, sketch_pick[0], axis=0)
    sketch_local = jnp.take(tile_x, sketch_slot, axis=0)
    sketch_x = lax.all_gather(sketch_local, "col", axis=0, tiled=True)
    sketch_kern = used_float * kernel_block(own_x, sq_norms(own_x), sketch_x, sq_norms(sketch_x))
    local_proj = jnp.dot(sketch_kern.T, block_grad, precision=HIGHEST_PREC)
    projected = lax.psum(local_proj, ("pts", "col", "sub"))
    weighted = jnp.dot(core_inv, projected, precision=HIGHEST_PREC)
    direction = used_float * (block_grad - jnp.dot(sketch_kern, weighted, precision=HIGHEST_PREC))
    return (block_grad[None], direction[None])


def solution(mesh):
    in_specs = (
        P(("grp", "pts", "sub"), None),
        P(("grp", "pts", "sub"), None),
        P(("grp", "col"), ("pts", "sub"), None),
        P(("grp", "col"), None),
        P(("grp", "col"), None),
        P(("grp", "col"), ("pts", "sub"), None),
        P("grp", None),
    )
    out_specs = (P(("grp", "col"), ("pts", "sub"), None), P(("grp", "col"), ("pts", "sub"), None))
    return jax.shard_map(
        per_device, mesh=mesh, in_specs=in_specs, out_specs=out_specs, check_vma=False
    )
```

profile of v0, /device:TPU:0, one launch (start us, length us, event | category | flops | bytes accessed | tf_op | source)
XLA Modules:
  0.0 187.9 jit_solution(5780408351962476899)
XLA Ops:
  7.2 0.0 copy-start
  7.2 0.0 reduce-scatter.2.cloned.1.call-start
  7.2 0.7 fusion.30
  8.0 1.6 multiply_reduce_fusion
  9.6 2.1 %gather_fusion = bf16[128,256]{1,0:T(8,128)(2,1)S(1)} fusion(bf16[2048,256]{1,0:T(8,128)(2,1)} %param.9, s32[1024]{0:T(1024)S(1)} %pad_clamp_fusion.2), kind=kCustom, calls=%fused_computation | custom fusion | bytes 131584 | tf_op jit(solution)/shard_map/jit(_take)/gather | solution.py:38
  11.7 1.3 fusion.29
  13.0 1.3 compare_and_fusion.1
  14.3 0.2 multiply_reduce_fusion.3
  14.5 16.5 %all_gather.6 = bf16[1024,256]{1,0:T(8,128)(2,1)S(1)} all-gather(bf16[128,256]{1,0:T(8,128)(2,1)S(1)} %get-tuple-element.166), channel_id=1, replica_groups=mesh['grp'=2,'pts'=4,'col'=2,'sub'=2] {'pts','sub'}, dimensions={0}, use_global_device_ids=true | all-gather | bytes 589824 | tf_op jit(solution)/shard_map/all_gather | solution.py:40
  31.0 0.2 multiply_reduce_fusion.1
  31.2 0.6 copy-done.1
  31.8 22.2 %while.14 = (s32[]{:T(128)}, f32[1024,128]{1,0:T(8,128)}, f32[1024]{0:T(1024)S(1)}, f32[2048]{0:T(1024)S(1)}, bf16[2048,256]{1,0:T(8,128)(2,1)}, /*index=5*/bf16...) while((s32[]{:T(128)}, f32[1024,128]{1,0:T(8,128)}, ...), condition=%wide.region_4.5_spmd.clone, body=%wide.region_3.4_spmd.clone.sunk | while | flops 1076625408 | bytes 6170809 | solution.py:65
  31.8 1.6 fusion.52
  33.4 0.1 dynamic_slice.33
  33.5 3.7 %fusion.53 = f32[1024,128]{1,0:T(8,128)} fusion(f32[512,1024]{1,0:T(8,128)S(1)} %fusion.52, f32[512]{0:T(512)S(1)} %dynamic_slice.33, f32[1024]{0:T(1024)S(1)} %get-tuple-element.236, f32[1024,128]{1,0:T(8,128)} %get-tuple-element.224, pred[]{:T(512)S(6)} %compare.3, bf16[2048,128]{1,0:T(8,128)(2,1)} %get-tuple-element.240, s32[]{:T(128)S(6)} %select_n.155), kind=kOutput, calls=%fused_computation.11.clone.1 | convolution fusion | flops 808189952 | bytes 3282949 | tf_op jit(solution)/shard_map/while/body/eval_jaxpr/dot_general | solution.py:61
  37.2 1.6 fusion.52
  38.8 0.1 dynamic_slice.33
  38.9 3.9 %fusion.53 = f32[1024,128]{1,0:T(8,128)} fusion(f32[512,1024]{1,0:T(8,128)S(1)} %fusion.52, f32[512]{0:T(512)S(1)} %dynamic_slice.33, f32[1024]{0:T(1024)S(1)} %get-tuple-element.236, f32[1024,128]{1,0:T(8,128)} %get-tuple-element.224, pred[]{:T(512)S(6)} %compare.3, bf16[2048,128]{1,0:T(8,128)(2,1)} %get-tuple-element.240, s32[]{:T(128)S(6)} %select_n.155), kind=kOutput, calls=%fused_computation.11.clone.1 | convolution fusion | flops 808189952 | bytes 3282949 | tf_op jit(solution)/shard_map/while/body/eval_jaxpr/dot_general | solution.py:61
  42.8 1.6 fusion.52
  44.4 0.1 dynamic_slice.33
  44.5 3.9 %fusion.53 = f32[1024,128]{1,0:T(8,128)} fusion(f32[512,1024]{1,0:T(8,128)S(1)} %fusion.52, f32[512]{0:T(512)S(1)} %dynamic_slice.33, f32[1024]{0:T(1024)S(1)} %get-tuple-element.236, f32[1024,128]{1,0:T(8,128)} %get-tuple-element.224, pred[]{:T(512)S(6)} %compare.3, bf16[2048,128]{1,0:T(8,128)(2,1)} %get-tuple-element.240, s32[]{:T(128)S(6)} %select_n.155), kind=kOutput, calls=%fused_computation.11.clone.1 | convolution fusion | flops 808189952 | bytes 3282949 | tf_op jit(solution)/shard_map/while/body/eval_jaxpr/dot_general | solution.py:61
  48.4 1.6 fusion.52
  50.0 0.1 dynamic_slice.33
  50.1 3.9 %fusion.53 = f32[1024,128]{1,0:T(8,128)} fusion(f32[512,1024]{1,0:T(8,128)S(1)} %fusion.52, f32[512]{0:T(512)S(1)} %dynamic_slice.33, f32[1024]{0:T(1024)S(1)} %get-tuple-element.236, f32[1024,128]{1,0:T(8,128)} %get-tuple-element.224, pred[]{:T(512)S(6)} %compare.3, bf16[2048,128]{1,0:T(8,128)(2,1)} %get-tuple-element.240, s32[]{:T(128)S(6)} %select_n.155), kind=kOutput, calls=%fused_computation.11.clone.1 | convolution fusion | flops 808189952 | bytes 3282949 | tf_op jit(solution)/shard_map/while/body/eval_jaxpr/dot_general | solution.py:61
  54.0 0.0 reduce-scatter.2.cloned.1.call-update
  54.0 0.0 all-reduce.2.cloned.1.call-start
  54.1 0.0 copy-done.6
  54.1 0.2 reduce-window_clone.1
  54.3 0.1 convert_reduce_fusion
  54.4 0.1 select_reduce_fusion
  54.5 0.0 copy-done.5
  54.5 1.9 %gather_fusion.2 = s32[256]{0:T(256)S(1)} fusion(s32[512]{0:T(512)S(1)} %add_subtract_fusion, s32[1024]{0:T(1024)S(1)} %pad_clamp_fusion.1), kind=kCustom, calls=%fused_computation.2 | custom fusion | bytes 3072 | tf_op jit(solution)/shard_map/jit(_take)/gather | solution.py:72
  56.5 1.8 gather_fusion.1
  58.2 0.0 copy-done.2
  58.3 1.2 gather_fusion.3
  59.4 0.1 broadcast_select_fusion
  59.5 6.4 %all_gather.7 = bf16[512,256]{1,0:T(8,128)(2,1)S(1)} all-gather(bf16[256,256]{1,0:T(8,128)(2,1)S(1)} %broadcast_select_fusion), channel_id=1, replica_groups=mesh['grp'=2,'pts'=4,'col'=2,'sub'=2] {'col'}, dimensions={0}, use_global_device_ids=true | all-gather | bytes 393216 | tf_op jit(solution)/shard_map/all_gather | solution.py:74
  65.9 0.6 compare_convert_fusion
  66.6 0.1 multiply_reduce_fusion.2
  66.8 0.3 fusion.25
  67.0 19.5 %reduce-scatter.2.cloned.1.call-done = f32[128,128]{1,0:T(8,128)} async-done(((f32[1024,128]{1,0:T(8,128)}), f32[128,128]{1,0:T(8,128)}) %reduce-scatter.2.cloned.1.call-update) | async-done | bytes 65552 | tf_op jit(solution)/shard_map/reduce_scatter | solution.py:64
  86.5 0.9 fusion.28
  87.4 0.0 copy-start.3
  87.4 1.3 fusion.31
  88.7 0.0 all-reduce.2.cloned.1.call-update
  88.7 89.1 %all-reduce.2.cloned.1.call-done = f32[512,128]{1,0:T(8,128)} async-done(((f32[512,128]{1,0:T(8,128)}), f32[512,128]{1,0:T(8,128)}) %all-reduce.2.cloned.1.call-update) | async-done | bytes 262160 | tf_op jit(solution)/shard_map/psum | solution.py:77
  177.8 2.2 %fusion.32 = f32[128,512]{1,0:T(8,128)S(1)} fusion(f32[512,128]{1,0:T(8,128)} %all-reduce.2.cloned.1.call-done, f32[512,512]{1,0:T(8,128)S(1)} %copy-done), kind=kOutput, calls=%fused_computation.66 | convolution fusion | flops 402653184 | bytes 1572864 | tf_op jit(solution)/shard_map/dot_general | solution.py:78
  180.1 1.0 fusion.27
  (18 shorter events, 0.1 us)
Async XLA Ops:
  7.2 170.7 %copy-start = (f32[512,512]{1,0:T(8,128)S(1)}, f32[512,512]{1,0:T(8,128)}, u32[]{:S(2)}) copy-start(f32[512,512]{1,0:T(8,128)} %param.15) | copy-start | bytes 3145732
  7.2 79.3 %reduce-scatter.2.cloned.1.call-start = ((), (), s32[]{:S(2)}) async-start(), calls=%async_computation.1 | async-start | bytes 589824 | tf_op jit(solution)/shard_map/reduce_scatter | solution.py:64
  31.0 0.8 copy-start.1
  31.8 22.3 %copy-start.6 = (s32[1,8]{1,0:T(1,128)S(1)}, s32[1,8]{1,0:T(1,128)}, u32[]{:S(2)}) copy-start(s32[1,8]{1,0:T(1,128)} %param.12) | copy-start | bytes 100
  31.8 22.7 %copy-start.5 = (s32[1,256]{1,0:T(1,128)S(1)}, s32[1,256]{1,0:T(1,128)}, u32[]{:S(2)}) copy-start(s32[1,256]{1,0:T(1,128)} %param.13) | copy-start | bytes 3076
  54.0 4.2 %copy-start.2 = (bf16[1024,256]{1,0:T(8,128)(2,1)S(1)}, bf16[1024,256]{1,0:T(8,128)(2,1)}, u32[]{:S(2)}) copy-start(bf16[1024,256]{1,0:T(8,128)(2,1)} %get-tuple-element.247) | copy-start | bytes 1572868
  54.0 123.8 %all-reduce.2.cloned.1.call-start = ((), (), s32[]{:S(2)}) async-start(), calls=%async_computation.2 | async-start | bytes 524288 | tf_op jit(solution)/shard_map/psum | solution.py:77
  54.3 32.2 %copy-start.4 = (bf16[1,128,128]{2,1,0:T(8,128)(2,1)S(1)}, bf16[1,128,128]{2,1,0:T(8,128)(2,1)}, u32[]{:S(2)}) copy-start(bf16[1,128,128]{2,1,0:T(8,128)(2,1)} %param.14) | copy-start | bytes 98308
  87.4 93.7 %copy-start.3 = (f32[128,128]{1,0:T(8,128)}, f32[128,128]{1,0:T(8,128)S(1)}, u32[]{:S(2)}) copy-start(f32[128,128]{1,0:T(8,128)S(1)} %fusion.28) | copy-start | bytes 196612
Sparse Core Ops, SparseCore 0:
  54.2 32.2 reduce-scatter.1
  89.9 87.9 all-reduce.1
where the time goes:
time: 188 us
  waiting for transfers between devices  109 us (58%)
  matrix products  26.7 us (14%)
  blocking collectives  22.9 us (12%)
  between operations  14.2 us (8%)
  local copies, waits for them, and re-layouts  7.9 us (4%)
  other arithmetic  7.55 us (4%)
    psum x1, waiting for transfers between devices, per_device(): projected = lax.psum(local_proj, ('pts', 'col', 'sub'))  89.1 us
    reduce_scatter x1, waiting for transfers between devices, per_device(): lax.psum_scatter(lax.fori_loop(0, slab_total // slab_step, add_block, sta...  19.5 us
    all_gather x1, blocking collectives, per_device(): tile_x = lax.all_gather(own_x, ('pts', 'sub'), axis=0, tiled=True)  16.5 us
    dot_general x4, matrix products, add_block(): return running + jnp.dot(kern_vals, slab_w, precision=HIGHEST_PREC)  15.5 us
    dot_general x5, matrix products, kernel_block(): jnp.einsum('ik,jk->ij', left_x, right_x, preferred_element_type=jnp.float32)  6.63 us
    all_gather x1, blocking collectives, per_device(): sketch_x = lax.all_gather(sketch_local, 'col', axis=0, tiled=True)  6.42 us
  transfers between devices with their start and end apart: 2, of which 2 were waited for; matrix products, arithmetic and copies ran while one was open for 3% of the time, Pallas kernels for 0%

commit v1 on v0

v1 whole, which is shorter than its diff:
```python
import math

import jax
import jax.numpy as jnp
from jax import lax
from jax.experimental import pallas as pl
from jax.experimental.pallas import tpu as pltpu
from jax.sharding import PartitionSpec as P

RIDGE_COEF = 50.0
LOG2E = 1.4426950408889634
HIGHEST_PREC = lax.Precision.HIGHEST


def sq_norms(values):
    widened = values.astype(jnp.float32)
    return jnp.sum(widened * widened, axis=1)


def kernel_block(left_x, right_x):
    scale = LOG2E / left_x.shape[1]
    inner_prods = jnp.einsum("ik,jk->ij", left_x, right_x, preferred_element_type=jnp.float32)
    return jnp.exp2(
        inner_prods * (2.0 * scale)
        - (sq_norms(left_x) * scale)[:, None]
        - (sq_norms(right_x) * scale)[None, :]
    )


def hop(values, axis, size, step):
    return lax.ppermute(values, axis, [(j, j ^ step) for j in range(size)])


def slab_kernel(n_blocks, half_rows, scalars, *refs):
    blocks = refs[:n_blocks]
    slabs, slab_sqs, slab_ws, shifts = refs[n_blocks : n_blocks + 4]
    part_ref, live_ref, rows, sums = refs[n_blocks + 4 :]
    cap, width = blocks[0].shape
    scale = LOG2E / width

    def place(target, values, rel):
        off, count = scalars[rel], scalars[n_blocks + rel]
        skew = lax.rem(off, 8)
        slot = lax.broadcasted_iota(jnp.int32, (cap + 8, 1), 0)
        kept = (slot >= skew) & (slot < skew + count)
        tail = jnp.zeros((8, values.shape[1]), jnp.float32)
        moved = pltpu.roll(jnp.concatenate([values, tail], axis=0), skew, 0)
        here = pl.ds(pl.multiple_of(off - skew, 8), cap + 8)
        target[here, :] = jnp.where(kept, moved, target[here, :])

    for rel in range(n_blocks):
        place(rows, blocks[rel][...].astype(jnp.float32), rel)
    live_ref[...] = rows[: live_ref.shape[0], :].astype(live_ref.dtype)
    start = pl.multiple_of(scalars[2 * n_blocks] * half_rows, half_rows)
    mine = rows[pl.ds(start, half_rows), :]
    mine_sq = jnp.sum(mine * mine, axis=1, keepdims=True) * scale
    mine_x = mine.astype(jnp.bfloat16)
    sums[...] = jnp.zeros_like(sums)
    for rel in range(shifts.shape[0]):
        place(sums, shifts[rel], rel)
    total = sums[pl.ds(start, half_rows), :]
    step = math.gcd(slabs.shape[1], 512)
    for which in range(slabs.shape[0]):
        for at in range(0, slabs.shape[1], step):
            inner = lax.dot_general(
                mine_x,
                slabs[which, at : at + step, :],
                (((1,), (1,)), ((), ())),
                preferred_element_type=jnp.float32,
            )
            kern = jnp.exp2(
                inner * (2.0 * scale) - mine_sq - slab_sqs[which, :, at : at + step]
            )
            high = kern.astype(jnp.bfloat16)
            low = (kern - high.astype(jnp.float32)).astype(jnp.bfloat16)
            slab_w = slab_ws[which, at : at + step, :]
            total = total + jnp.dot(high, slab_w, preferred_element_type=jnp.float32)
            total = total + jnp.dot(low, slab_w, preferred_element_type=jnp.float32)
    part_ref[...] = total


def make_device(mesh):
    n_pts, n_col, n_sub = mesh.shape["pts"], mesh.shape["col"], mesh.shape["sub"]

    def per_device(points, weights, tile_rows, tile_count, sketch_pick, block_targets, core_inv):
        cap = tile_rows.shape[2]
        width, outs = points.shape[1], weights.shape[1]
        scale = LOG2E / width
        counts = tile_count[0]
        owners = counts.shape[0]
        live = owners * cap // 2
        half = live // n_sub
        pts_at, sub_at, col_at = lax.axis_index("pts"), lax.axis_index("sub"), lax.axis_index("col")
        own_at = pts_at * n_sub + sub_at
        offsets = jnp.cumsum(counts) - counts
        rel_owner = own_at ^ jnp.arange(owners, dtype=jnp.int32)
        rel_hot = rel_owner[:, None] == jnp.arange(owners)[None, :]
        rel_off = jnp.sum(jnp.where(rel_hot, offsets[None, :], 0), axis=1)
        rel_cnt = jnp.sum(jnp.where(rel_hot, counts[None, :], 0), axis=1)
        scalars = jnp.concatenate([rel_off, rel_cnt, sub_at[None].astype(jnp.int32)])
        used = (jnp.arange(cap) < rel_cnt[0]).astype(jnp.float32)[:, None]

        row_hot = (tile_rows[0, 0][:, None] == jnp.arange(points.shape[0])[None, :]).astype(points.dtype)
        own_x = jnp.dot(row_hot, points, preferred_element_type=jnp.float32).astype(points.dtype)
        far = [own_x] + [hop(own_x, "pts", n_pts, i) for i in range(1, n_pts)]
        blocks = []
        for block in far:
            blocks += [block] + [hop(block, "sub", n_sub, i) for i in range(1, n_sub)]

        own_alpha = jnp.dot(row_hot, weights, preferred_element_type=jnp.float32)
        shift = RIDGE_COEF * own_alpha - block_targets[0].astype(jnp.float32)
        shifts = jnp.stack([shift] + [hop(shift, "sub", n_sub, i) for i in range(1, n_sub)])
        slabs = jnp.stack([points] + [hop(points, "sub", n_sub, i) for i in range(1, n_sub)])
        slab_ws = jnp.stack([weights] + [hop(weights, "sub", n_sub, i) for i in range(1, n_sub)])
        wide = slabs.astype(jnp.float32)
        slab_sqs = (jnp.sum(wide * wide, axis=2) * scale)[:, None, :]

        vmem = pl.BlockSpec(memory_space=pltpu.VMEM)
        part, live_x = pl.pallas_call(
            lambda *refs: slab_kernel(owners, half, *refs),
            out_shape=(
                jax.ShapeDtypeStruct((half, outs), jnp.float32),
                jax.ShapeDtypeStruct((live, width), points.dtype),
            ),
            in_specs=[pl.BlockSpec(memory_space=pltpu.SMEM)] + [vmem] * (owners + 4),
            out_specs=(vmem, vmem),
            scratch_shapes=[
                pltpu.VMEM((live + cap + 8, width), jnp.float32),
                pltpu.VMEM((live + cap + 8, outs), jnp.float32),
            ],
            name="slab",
        )(scalars, *blocks, slabs, slab_sqs, slab_ws, shifts)

        step = 1
        while step < n_pts:
            part = part + hop(part, "pts", n_pts, step)
            step *= 2

        pick_hot = (sketch_pick[0][:, None] == jnp.arange(live)[None, :]).astype(points.dtype)
        sketch_own = jnp.dot(pick_hot, live_x, preferred_element_type=jnp.float32).astype(points.dtype)
        mine_x = lax.dynamic_slice_in_dim(live_x, sub_at * half, half, 0)
        peer_x = [lax.dynamic_slice_in_dim(live_x, (sub_at ^ i) * half, half, 0) for i in range(n_sub)]
        sent = jnp.concatenate([mine_x, sketch_own], axis=0)
        got = [hop(sent, "col", n_col, i) for i in range(1, n_col)]
        rows_all = list(peer_x)
        for block in got:
            rows_all += [block[:half]] + [hop(block[:half], "sub", n_sub, i) for i in range(1, n_sub)]
        rows_all = jnp.concatenate(rows_all, axis=0)
        sketch_rel = jnp.stack([sketch_own] + [block[half:] for block in got])
        sketch_x = jnp.take(sketch_rel, col_at ^ jnp.arange(n_col), axis=0).reshape(-1, width)

        sketch_kern = used * kernel_block(own_x, sketch_x)
        sketch_all = kernel_block(rows_all, sketch_x)
        mixed = jnp.dot(sketch_kern, core_inv, precision=HIGHEST_PREC)
        gram = jnp.dot(mixed, sketch_all.T, precision=HIGHEST_PREC)

        tile_part = [part] + [hop(part, "sub", n_sub, i) for i in range(1, n_sub)]
        grads = list(tile_part)
        for i in range(1, n_col):
            other = hop(part, "col", n_col, i)
            grads += [other] + [hop(other, "sub", n_sub, j) for j in range(1, n_sub)]
        grads_all = jnp.concatenate(grads, axis=0)
        in_order = jnp.take(jnp.stack(tile_part), sub_at ^ jnp.arange(n_sub), axis=0).reshape(live, outs)
        in_order = jnp.concatenate([in_order, jnp.zeros((cap, outs), jnp.float32)], axis=0)
        block_grad = used * lax.dynamic_slice_in_dim(in_order, rel_off[0], cap, 0)
        direction = used * (block_grad - jnp.dot(gram, grads_all, precision=HIGHEST_PREC))
        return (block_grad[None], direction[None])

    return per_device


def solution(mesh):
    in_specs = (
        P(("grp", "pts", "sub"), None),
        P(("grp", "pts", "sub"), None),
        P(("grp", "col"), ("pts", "sub"), None),
        P(("grp", "col"), None),
        P(("grp", "col"), None),
        P(("grp", "col"), ("pts", "sub"), None),
        P("grp", None),
    )
    out_specs = (P(("grp", "col"), ("pts", "sub"), None), P(("grp", "col"), ("pts", "sub"), None))
    return jax.shard_map(
        make_device(mesh), mesh=mesh, in_specs=in_specs, out_specs=out_specs, check_vma=False
    )
```

time: 188 us -> 57.6 us (0.31)
  waiting for transfers between devices: 109 us -> 16.1 us
  blocking collectives: 22.9 us -> 0 us
  matrix products: 26.7 us -> 9.79 us
  between operations: 14.2 us -> 1.15 us
  starting transfers between devices: 0.08 us -> 10.8 us
  Pallas kernels: 0 us -> 6.19 us
  local copies, waits for them, and re-layouts: 7.9 us -> 3.66 us
  other arithmetic: 7.55 us -> 9.62 us
    psum x1 -> x0, waiting for transfers between devices: 89.1 us -> none  [per_device(): projected = lax.psum(local_proj, ('pts', 'col', 'sub'))]
    all_gather x2 -> x0, blocking collectives: 22.9 us -> none  [the longest x1 16.5 us: per_device(): tile_x = lax.all_gather(own_x, ('pts', 'sub'), axis=0, tiled=True)]
    reduce_scatter x1 -> x0, waiting for transfers between devices: 19.5 us -> none  [per_device(): lax.psum_scatter(lax.fori_loop(0, slab_total // slab_step, add_block, sta...]
    ppermute x0 -> x17, waiting for transfers between devices: none -> 16.1 us  [hop(): return lax.ppermute(values, axis, [(j, j ^ step) for j in range(size)])]
    dot_general x7 -> x6, matrix products: 20 us -> 9.07 us  [the longest x1 2.64 us: per_device(): gram = jnp.dot(mixed, sketch_all.T, precision=HIGHEST_PREC)]
    ppermute x0 -> x17, starting transfers between devices: none -> 10.8 us  [hop(): return lax.ppermute(values, axis, [(j, j ^ step) for j in range(size)])]
    pallas_call x0 -> x1, Pallas kernels: none -> 6.19 us  [per_device(): pl.pallas_call(lambda *refs: slab_kernel(owners, half, *refs), out_shape=...]
    dot_general x5 -> x2, matrix products: 6.63 us -> 0.72 us  [kernel_block(): jnp.einsum('ik,jk->ij', left_x, right_x, preferred_element_type=jnp.float32)]
  transfers between devices with their start and end apart: 2 -> 17, of which waited for: 2 -> 4; matrix products, arithmetic and copies ran while one was open for 3% -> 34% of each run, Pallas kernels for 0% -> 0%
where the time goes in v1:
time: 57.6 us; the launch traced here: 57.4 us
  waiting for transfers between devices  16.1 us (28%)
  starting transfers between devices  10.8 us (19%)
  matrix products  9.79 us (17%)
  other arithmetic  9.62 us (17%)
  Pallas kernels  6.19 us (11%)
  local copies, waits for them, and re-layouts  3.66 us (6%)
  between operations  1.15 us (2%)
    ppermute x17, waiting for transfers between devices, hop(): return lax.ppermute(values, axis, [(j, j ^ step) for j in range(size)])  16.1 us
    ppermute x17, starting transfers between devices, hop(): return lax.ppermute(values, axis, [(j, j ^ step) for j in range(size)])  10.8 us
    pallas_call x1, Pallas kernels, per_device(): pl.pallas_call(lambda *refs: slab_kernel(owners, half, *refs), out_shape=...  6.19 us
    dot_general x1, matrix products, per_device(): gram = jnp.dot(mixed, sketch_all.T, precision=HIGHEST_PREC)  2.64 us
    another operation x1, other arithmetic, per_device(): jnp.stack([weights] + [hop(weights, 'sub', n_sub, i) for i in range(1, n_...  2.26 us
    dot_general x1, matrix products, per_device(): jnp.dot(row_hot, points, preferred_element_type=jnp.float32)  1.81 us
    another operation x1, other arithmetic, per_device(): jnp.stack([points] + [hop(points, 'sub', n_sub, i) for i in range(1, n_su...  1.51 us
    dot_general x1, matrix products, per_device(): own_alpha = jnp.dot(row_hot, weights, preferred_element_type=jnp.float32)  1.4 us
  transfers between devices with their start and end apart: 17, of which 4 were waited for; matrix products, arithmetic and copies ran while one was open for 34% of the time, Pallas kernels for 0%

profile of v1, /device:TPU:0, one launch (start us, length us, event | category | flops | bytes accessed | tf_op | source)
XLA Modules:
  0.0 57.4 jit_solution(786335876831665097)
XLA Ops:
  0.6 0.0 copy-start
  0.7 1.8 %multiply_reduce_fusion.3 = (f32[128]{0:T(128)S(1)}, bf16[128,256]{1,0:T(8,128)(2,1)S(1)}) fusion(bf16[2048,256]{1,0:T(8,128)(2,1)} %param.7, s32[128]{0:T(128)} %bitcast.67), kind=kOutput, calls=%fused_computation.51 | convolution fusion | flops 134610816 | bytes 1115136 | tf_op jit(solution)/shard_map/dot_general | solution.py:104
  2.5 3.1 %collective-permute-start.1 = (bf16[128,256]{1,0:T(8,128)(2,1)S(1)}, bf16[128,256]{1,0:T(8,128)(2,1)S(1)}, u32[]{:S(2)}, u32[]{:S(2)}) collective-permute-start(bf16[128,256]{1,0:T(8,128)(2,1)S(1)} %get-tuple-element.13.refs_1_), channel_id=1, source_target_pairs={{0,4},{4,0},{8,12},{12,8},{1,5},{5,1},{9,13},{13,9},{2,6},{6,2},{1... | collective-permute-start | bytes 196616 | tf_op jit(solution)/shard_map/ppermute | solution.py:31
  5.6 2.6 %collective-permute-start.3 = (bf16[128,256]{1,0:T(8,128)(2,1)S(1)}, bf16[128,256]{1,0:T(8,128)(2,1)S(1)}, u32[]{:S(2)}, u32[]{:S(2)}) collective-permute-start(bf16[128,256]{1,0:T(8,128)(2,1)S(1)} %get-tuple-element.13.refs_1_), channel_id=1, source_target_pairs={{0,8},{4,12},{8,0},{12,4},{1,9},{5,13},{9,1},{13,5},{2,10},{6,14},... | collective-permute-start | bytes 196616 | tf_op jit(solution)/shard_map/ppermute | solution.py:31
  8.2 0.5 collective-permute-start.8
  8.7 1.4 %fusion.13 = f32[128,128]{1,0:T(8,128)S(1)} fusion(bf16[2048,128]{1,0:T(8,128)(2,1)} %param.8, s32[128]{0:T(128)} %bitcast.68, bf16[1,128,128]{2,1,0:T(8,128)(2,1)} %param.12), kind=kOutput, calls=%fused_computation.22 | convolution fusion | flops 67420160 | bytes 623104 | tf_op jit(solution)/shard_map/dot_general | solution.py:110
  10.1 0.1 collective-permute-start.9
  10.2 0.2 reduce-window_clone.1
  10.4 0.2 select_reduce_fusion.1
  10.6 0.5 compare_and_fusion
  11.1 0.6 %broadcast_multiply_fusion.2 = f32[128]{0:T(128)} fusion(f32[128]{0:T(128)S(1)} %get-tuple-element.12), kind=kLoop, calls=%fused_computation.77 | loop fusion | flops 128 | bytes 1024 | tf_op jit(solution)/shard_map/mul | solution.py:25
  11.7 0.6 %pad_add_fusion.refs_0_ = s32[17]{0:T(128)} fusion(s32[1]{0:T(128)} %bitcast.3, s32[8]{0:T(128)S(1)} %get-tuple-element.6, s32[8]{0:T(128)S(1)} %get-tuple-element.7), kind=kLoop, calls=%fused_computation.74 | loop fusion | flops 34 | bytes 136 | tf_op jit(solution)/shard_map/concatenate | solution.py:100
  12.3 0.7 %pad_maximum_fusion.6.refs_12_ = f32[2,128,128]{2,1,0:T(8,128)} fusion(f32[1,128,128]{2,1,0:T(8,128)S(1)} %bitcast.58, f32[1,128,128]{2,1,0:T(8,128)S(1)} %bitcast.57), kind=kLoop, calls=%fused_computation.50 | loop fusion | flops 32768 | bytes 262144 | tf_op jit(solution)/shard_map/stack | solution.py:112
  13.0 0.5 collective-permute-start
  13.5 0.1 collective-permute-start.2
  13.5 5.0 %collective-permute-done.5.refs_7_ = bf16[128,256]{1,0:T(8,128)(2,1)S(1)} collective-permute-done((bf16[128,256]{1,0:T(8,128)(2,1)S(1)}, bf16[128,256]{1,0:T(8,128)(2,1)S(1)}, u32[]{:S(2)}, u32[]{:S(2)}) %collective-permute-start.5) | collective-permute-done | bytes 65568 | tf_op jit(solution)/shard_map/ppermute | solution.py:31
  18.6 0.5 collective-permute-start.6
  19.1 2.3 %pad_maximum_fusion.1.refs_11_ = bf16[2,2048,128]{2,1,0:T(8,128)(2,1)} fusion(bf16[1,2048,128]{2,1,0:T(8,128)(2,1)} %bitcast.8, bf16[1,2048,128]{2,1,0:T(8,128)(2,1)} %bitcast.55), kind=kLoop, calls=%fused_computation.23 | loop fusion | flops 524288 | bytes 2097152 | tf_op jit(solution)/shard_map/stack | solution.py:114
  21.4 0.6 %multiply_reduce_fusion = f32[2,2048]{1,0:T(2,128)S(1)} fusion(bf16[1,2048,256]{2,1,0:T(8,128)(2,1)S(1)} %bitcast.51, bf16[1,2048,256]{2,1,0:T(8,128)(2,1)S(1)} %bitcast.49), kind=kLoop, calls=%fused_computation.2 | loop fusion | flops 4190208 | bytes 2113536 | tf_op jit(solution)/shard_map/reduce_sum | solution.py:116
  22.1 1.5 %pad_maximum_fusion.refs_9_ = bf16[2,2048,256]{2,1,0:T(8,128)(2,1)} fusion(bf16[1,2048,256]{2,1,0:T(8,128)(2,1)S(1)} %bitcast.52, bf16[1,2048,256]{2,1,0:T(8,128)(2,1)S(1)} %bitcast.50), kind=kLoop, calls=%fused_computation.3 | loop fusion | flops 1048576 | bytes 4194304 | tf_op jit(solution)/shard_map/stack | solution.py:113
  23.6 0.6 %mul.116.refs_10_ = f32[2,1,2048]{2,1,0:T(1,128)} reshape(f32[2,2048]{1,0:T(2,128)S(1)} %broadcast_multiply_fusion) | data formatting | bytes 32768 | tf_op jit(solution)/shard_map/mul | solution.py:116
  24.2 0.6 %copy-done.9 = bf16[128,256]{1,0:T(8,128)(2,1)} copy-done((bf16[128,256]{1,0:T(8,128)(2,1)}, bf16[128,256]{1,0:T(8,128)(2,1)S(1)}, u32[]{:S(2)}) %copy-start.9) | copy-done | bytes 65560
  24.9 6.2 %slab.1 = (f32[256,128]{1,0:T(8,128)}, bf16[512,256]{1,0:T(8,128)(2,1)}) custom-call(s32[17]{0:T(128)} %pad_add_fusion.refs_0_, bf16[128,256]{1,0:T(8,128)(2,1)} %copy-done.2, bf16[128,256]{1,0:T(8,128)(2,1)} %copy-done.7, bf16[128,256]{1,0:T(8,128)(2,1)} %copy-done.4, bf16[128,256]{1,0:T(8,128)(2,1)} %copy-done.8, bf16[128,256]{1,0:T(8,128)(2,1)} %copy-done.5, ...), custom_call_target="tpu_custom_call" | custom-call | tf_op jit(solution)/shard_map/slab/pallas_call | solution.py:119
  31.1 1.2 %convolution_convert_fusion = bf16[256,256]{1,0:T(8,128)(2,1)S(1)} fusion(bf16[512,256]{1,0:T(8,128)(2,1)} %get-tuple-element.5, s32[256]{0:T(256)S(1)} %bitcast.66), kind=kOutput, calls=%fused_computation.16 | convolution fusion | flops 67305472 | bytes 394240 | tf_op jit(solution)/shard_map/dot_general | solution.py:140
  32.3 1.0 %constant_dynamic-slice_fusion = (bf16[256,256]{1,0:T(8,128)(2,1)S(1)}, bf16[256,256]{1,0:T(8,128)(2,1)S(1)}) fusion(bf16[512,256]{1,0:T(8,128)(2,1)} %get-tuple-element.5, s32[]{:T(128)S(6)} %select_n.72, s32[]{:T(128)S(6)} %select_n.68), kind=kLoop, calls=%fused_computation.70 | loop fusion | bytes 524296 | tf_op jit(solution)/shard_map/dynamic_slice | solution.py:142
  33.4 1.6 %collective-permute-start.13 = (bf16[512,256]{1,0:T(8,128)(2,1)S(1)}, bf16[512,256]{1,0:T(8,128)(2,1)S(1)}, u32[]{:S(2)}, u32[]{:S(2)}) collective-permute-start(bf16[512,256]{1,0:T(8,128)(2,1)S(1)} %pad_maximum_fusion.4), channel_id=1, source_target_pairs={{0,2},{2,0},{1,3},{3,1},{4,6},{6,4},{5,7},{7,5},{8,10},{10,8},{9,1... | collective-permute-start | bytes 786440 | tf_op jit(solution)/shard_map/ppermute | solution.py:31
  34.9 1.8 %collective-permute-done.10 = f32[256,128]{1,0:T(8,128)S(1)} collective-permute-done((f32[256,128]{1,0:T(8,128)}, f32[256,128]{1,0:T(8,128)S(1)}, u32[]{:S(2)}, u32[]{:S(2)}) %collective-permute-start.10) | collective-permute-done | bytes 131104 | tf_op jit(solution)/shard_map/ppermute | solution.py:31
  36.7 0.9 %add.53 = f32[256,128]{1,0:T(8,128)S(1)} add(f32[256,128]{1,0:T(8,128)} %get-tuple-element.4, f32[256,128]{1,0:T(8,128)S(1)} %collective-permute-done.10) | non-fusion elementwise | flops 32768 | bytes 393216 | tf_op jit(solution)/shard_map/add | solution.py:136
  37.7 0.1 collective-permute-start.11
  37.9 0.1 broadcast_in_dim.78
  38.0 0.1 broadcast_in_dim.86
  38.1 7.9 %collective-permute-done.11 = f32[256,128]{1,0:T(8,128)S(1)} collective-permute-done((f32[256,128]{1,0:T(8,128)S(1)}, f32[256,128]{1,0:T(8,128)S(1)}, u32[]{:S(2)}, u32[]{:S(2)}) %collective-permute-start.11) | collective-permute-done | bytes 131104 | tf_op jit(solution)/shard_map/ppermute | solution.py:31
  46.1 0.1 collective-permute-start.12
  46.1 1.6 %collective-permute-start.15 = (f32[256,128]{1,0:T(8,128)S(1)}, f32[256,128]{1,0:T(8,128)S(1)}, u32[]{:S(2)}, u32[]{:S(2)}) collective-permute-start(f32[256,128]{1,0:T(8,128)S(1)} %add.54), channel_id=1, source_target_pairs={{0,2},{2,0},{1,3},{3,1},{4,6},{6,4},{5,7},{7,5},{8,10},{10,8},{9,1... | collective-permute-start | bytes 393224 | tf_op jit(solution)/shard_map/ppermute | solution.py:31
  47.8 0.6 gather_fusion.1
  48.3 0.2 multiply_reduce_fusion.2
  48.6 0.1 bitcast_select_fusion
  48.7 0.2 collective-permute-start.14
  48.9 0.3 fusion.10
  49.2 0.7 %fusion.38 = f32[128,512]{1,0:T(8,128)S(1)} fusion(f32[128,512]{1,0:T(8,128)S(1)} %fusion.10, f32[512,512]{1,0:T(8,128)S(1)} %copy-done), kind=kOutput, calls=%fused_computation.83 | convolution fusion | flops 402653184 | bytes 1572864 | tf_op jit(solution)/shard_map/dot_general | solution.py:154
  50.0 0.6 gather_fusion
  50.5 0.1 bitcast_select_fusion.1
  50.7 1.3 %collective-permute-done.15 = f32[256,128]{1,0:T(8,128)S(1)} collective-permute-done((f32[256,128]{1,0:T(8,128)S(1)}, f32[256,128]{1,0:T(8,128)S(1)}, u32[]{:S(2)}, u32[]{:S(2)}) %collective-permute-start.15) | collective-permute-done | bytes 131104 | tf_op jit(solution)/shard_map/ppermute | solution.py:31
  52.0 0.7 %fusion.30 = f32[1,128,128]{2,1,0:T(8,128)} fusion(s32[]{:T(128)S(6)} %select_n.66, f32[512,128]{1,0:T(8,128)S(1)} %bitcast_select_fusion.1, f32[128]{0:T(128)S(1)} %compare_convert_fusion), kind=kLoop, calls=%fused_computation.54 | loop fusion | flops 16384 | bytes 328196 | tf_op jit(solution)/shard_map/broadcast_in_dim | solution.py:167
  52.8 0.2 multiply_reduce_fusion.1
  53.0 0.5 fusion.28
  53.4 2.6 %fusion = f32[128,1024]{1,0:T(8,128)S(1)} fusion(f32[128,512]{1,0:T(8,128)S(1)} %fusion.38, f32[1024,512]{1,0:T(8,128)S(1)} %fusion.28, f32[512]{0:T(512)S(1)} %bitcast.60, f32[1024]{0:T(1024)S(1)} %broadcast_multiply_fusion.1), kind=kOutput, calls=%fused_computation.4 | convolution fusion | flops 807403520 | bytes 2889728 | tf_op jit(solution)/shard_map/dot_general | solution.py:155
  56.1 1.3 %fusion.12 = f32[1,128,128]{2,1,0:T(8,128)} fusion(f32[128,1024]{1,0:T(8,128)S(1)} %fusion, f32[256,128]{1,0:T(8,128)S(1)} %collective-permute-done.16, f32[256,128]{1,0:T(8,128)S(1)} %collective-permute-done.15, f32[256,128]{1,0:T(8,128)S(1)} %collective-permute-done.12, f32[256,128]{1,0:T(8,128)S(1)} %add.54, s32[]{:T(128)S(6)} %select_n.66, ...), kind=kOutput, calls=%fused_computation.20 | convolution fusion | flops 201768960 | bytes 1376772 | tf_op jit(solution)/shard_map/dot_general | solution.py:166
  (62 shorter events, 0.3 us)
Async XLA Ops:
  0.6 48.6 %copy-start = (f32[512,512]{1,0:T(8,128)S(1)}, f32[512,512]{1,0:T(8,128)}, u32[]{:S(2)}) copy-start(f32[512,512]{1,0:T(8,128)} %param.13) | copy-start | bytes 3145732
  0.6 9.6 %copy-start.10 = (s32[1,8]{1,0:T(1,128)S(1)}, s32[1,8]{1,0:T(1,128)}, u32[]{:S(2)}) copy-start(s32[1,8]{1,0:T(1,128)} %param.10) | copy-start | bytes 100
  0.7 20.7 %copy-start.1 = (bf16[2048,256]{1,0:T(8,128)(2,1)S(1)}, bf16[2048,256]{1,0:T(8,128)(2,1)}, u32[]{:S(2)}) copy-start(bf16[2048,256]{1,0:T(8,128)(2,1)} %param.7) | copy-start | bytes 3145732
  2.5 19.5 %copy-start.2 = (bf16[128,256]{1,0:T(8,128)(2,1)}, bf16[128,256]{1,0:T(8,128)(2,1)S(1)}, u32[]{:S(2)}) copy-start(bf16[128,256]{1,0:T(8,128)(2,1)S(1)} %get-tuple-element.13.refs_1_) | copy-start | bytes 196612
  2.5 10.5 %collective-permute-start.1 = (bf16[128,256]{1,0:T(8,128)(2,1)S(1)}, bf16[128,256]{1,0:T(8,128)(2,1)S(1)}, u32[]{:S(2)}, u32[]{:S(2)}) collective-permute-start(bf16[128,256]{1,0:T(8,128)(2,1)S(1)} %get-tuple-element.13.refs_1_), channel_id=1, source_target_pairs={{0,4},{4,0},{8,12},{12,8},{1,5},{5,1},{9,13},{13,9},{2,6},{6,2},{1... | collective-permute-start | bytes 196616 | tf_op jit(solution)/shard_map/ppermute | solution.py:31
  5.6 7.8 %collective-permute-start.3 = (bf16[128,256]{1,0:T(8,128)(2,1)S(1)}, bf16[128,256]{1,0:T(8,128)(2,1)S(1)}, u32[]{:S(2)}, u32[]{:S(2)}) collective-permute-start(bf16[128,256]{1,0:T(8,128)(2,1)S(1)} %get-tuple-element.13.refs_1_), channel_id=1, source_target_pairs={{0,8},{4,12},{8,0},{12,4},{1,9},{5,13},{9,1},{13,5},{2,10},{6,14},... | collective-permute-start | bytes 196616 | tf_op jit(solution)/shard_map/ppermute | solution.py:31
  8.2 13.2 %collective-permute-start.7 = (bf16[2048,256]{1,0:T(8,128)(2,1)}, bf16[2048,256]{1,0:T(8,128)(2,1)S(1)}, u32[]{:S(2)}, u32[]{:S(2)}) collective-permute-start(bf16[2048,256]{1,0:T(8,128)(2,1)} %param.7), channel_id=1, source_target_pairs={{0,1},{1,0},{2,3},{3,2},{4,5},{5,4},{6,7},{7,6},{8,9},{9,8},{10,11... | collective-permute-start | bytes 3145736 | tf_op jit(solution)/shard_map/ppermute | solution.py:31
  8.2 10.4 %collective-permute-start.8 = (bf16[2048,128]{1,0:T(8,128)(2,1)}, bf16[2048,128]{1,0:T(8,128)(2,1)}, u32[]{:S(2)}, u32[]{:S(2)}) collective-permute-start(bf16[2048,128]{1,0:T(8,128)(2,1)} %param.8), channel_id=1, source_target_pairs={{0,1},{1,0},{2,3},{3,2},{4,5},{5,4},{6,7},{7,6},{8,9},{9,8},{10,11... | collective-permute-start | bytes 1572872 | tf_op jit(solution)/shard_map/ppermute | solution.py:31
  10.1 2.2 %collective-permute-start.9 = (f32[128,128]{1,0:T(8,128)S(1)}, f32[128,128]{1,0:T(8,128)S(1)}, u32[]{:S(2)}, u32[]{:S(2)}) collective-permute-start(f32[128,128]{1,0:T(8,128)S(1)} %fusion.13), channel_id=1, source_target_pairs={{0,1},{1,0},{2,3},{3,2},{4,5},{5,4},{6,7},{7,6},{8,9},{9,8},{10,11... | collective-permute-start | bytes 196616 | tf_op jit(solution)/shard_map/ppermute | solution.py:31
  12.3 6.3 %collective-permute-start.5 = (bf16[128,256]{1,0:T(8,128)(2,1)S(1)}, bf16[128,256]{1,0:T(8,128)(2,1)S(1)}, u32[]{:S(2)}, u32[]{:S(2)}) collective-permute-start(bf16[128,256]{1,0:T(8,128)(2,1)S(1)} %get-tuple-element.13.refs_1_), channel_id=1, source_target_pairs={{0,12},{4,8},{8,4},{12,0},{1,13},{5,9},{9,5},{13,1},{2,14},{6,10},... | collective-permute-start | bytes 196616 | tf_op jit(solution)/shard_map/ppermute | solution.py:31
  13.0 9.0 %copy-start.4 = (bf16[128,256]{1,0:T(8,128)(2,1)}, bf16[128,256]{1,0:T(8,128)(2,1)S(1)}, u32[]{:S(2)}) copy-start(bf16[128,256]{1,0:T(8,128)(2,1)S(1)} %collective-permute-done.1.refs_3_) | copy-start | bytes 196612
  13.0 11.2 %collective-permute-start = (bf16[128,256]{1,0:T(8,128)(2,1)S(1)}, bf16[128,256]{1,0:T(8,128)(2,1)S(1)}, u32[]{:S(2)}, u32[]{:S(2)}) collective-permute-start(bf16[128,256]{1,0:T(8,128)(2,1)S(1)} %get-tuple-element.13.refs_1_), channel_id=1, source_target_pairs={{0,1},{1,0},{2,3},{3,2},{4,5},{5,4},{6,7},{7,6},{8,9},{9,8},{10,11... | collective-permute-start | bytes 196616 | tf_op jit(solution)/shard_map/ppermute | solution.py:31
  13.5 8.6 %copy-start.5 = (bf16[128,256]{1,0:T(8,128)(2,1)}, bf16[128,256]{1,0:T(8,128)(2,1)S(1)}, u32[]{:S(2)}) copy-start(bf16[128,256]{1,0:T(8,128)(2,1)S(1)} %collective-permute-done.3.refs_5_) | copy-start | bytes 196612
  13.5 10.7 %collective-permute-start.2 = (bf16[128,256]{1,0:T(8,128)(2,1)S(1)}, bf16[128,256]{1,0:T(8,128)(2,1)S(1)}, u32[]{:S(2)}, u32[]{:S(2)}) collective-permute-start(bf16[128,256]{1,0:T(8,128)(2,1)S(1)} %collective-permute-done.1.refs_3_), channel_id=1, source_target_pairs={{0,1},{1,0},{2,3},{3,2},{4,5},{5,4},{6,7},{7,6},{8,9},{9,8},{10,11... | collective-permute-start | bytes 196616 | tf_op jit(solution)/shard_map/ppermute | solution.py:31
  18.6 3.5 %copy-start.6 = (bf16[128,256]{1,0:T(8,128)(2,1)}, bf16[128,256]{1,0:T(8,128)(2,1)S(1)}, u32[]{:S(2)}) copy-start(bf16[128,256]{1,0:T(8,128)(2,1)S(1)} %collective-permute-done.5.refs_7_) | copy-start | bytes 196612
  18.6 5.6 %collective-permute-start.4 = (bf16[128,256]{1,0:T(8,128)(2,1)S(1)}, bf16[128,256]{1,0:T(8,128)(2,1)S(1)}, u32[]{:S(2)}, u32[]{:S(2)}) collective-permute-start(bf16[128,256]{1,0:T(8,128)(2,1)S(1)} %collective-permute-done.3.refs_5_), channel_id=1, source_target_pairs={{0,1},{1,0},{2,3},{3,2},{4,5},{5,4},{6,7},{7,6},{8,9},{9,8},{10,11... | collective-permute-start | bytes 196616 | tf_op jit(solution)/shard_map/ppermute | solution.py:31
  18.6 6.3 %collective-permute-start.6 = (bf16[128,256]{1,0:T(8,128)(2,1)S(1)}, bf16[128,256]{1,0:T(8,128)(2,1)}, u32[]{:S(2)}, u32[]{:S(2)}) collective-permute-start(bf16[128,256]{1,0:T(8,128)(2,1)S(1)} %collective-permute-done.5.refs_7_), channel_id=1, source_target_pairs={{0,1},{1,0},{2,3},{3,2},{4,5},{5,4},{6,7},{7,6},{8,9},{9,8},{10,11... | collective-permute-start | bytes 196616 | tf_op jit(solution)/shard_map/ppermute | solution.py:31
  23.6 7.5 %copy-start.12 = (s32[1,256]{1,0:T(1,128)S(1)}, s32[1,256]{1,0:T(1,128)}, u32[]{:S(2)}) copy-start(s32[1,256]{1,0:T(1,128)} %param.11) | copy-start | bytes 3076
  24.2 13.7 %copy-start.11 = (pred[2]{0:T(512)(128)(4,1)S(1)}, pred[2]{0:T(512)(128)(4,1)}, u32[]{:S(2)}) copy-start(pred[2]{0:T(512)(128)(4,1)} %get-tuple-element.15) | copy-start | bytes 10
  24.2 0.7 %copy-start.7 = (bf16[128,256]{1,0:T(8,128)(2,1)}, bf16[128,256]{1,0:T(8,128)(2,1)S(1)}, u32[]{:S(2)}) copy-start(bf16[128,256]{1,0:T(8,128)(2,1)S(1)} %collective-permute-done.refs_2_) | copy-start | bytes 196612
  24.2 0.7 %copy-start.8 = (bf16[128,256]{1,0:T(8,128)(2,1)}, bf16[128,256]{1,0:T(8,128)(2,1)S(1)}, u32[]{:S(2)}) copy-start(bf16[128,256]{1,0:T(8,128)(2,1)S(1)} %collective-permute-done.2.refs_4_) | copy-start | bytes 196612
  24.2 0.6 %copy-start.9 = (bf16[128,256]{1,0:T(8,128)(2,1)}, bf16[128,256]{1,0:T(8,128)(2,1)S(1)}, u32[]{:S(2)}) copy-start(bf16[128,256]{1,0:T(8,128)(2,1)S(1)} %collective-permute-done.4.refs_6_) | copy-start | bytes 196612
  31.0 5.7 %collective-permute-start.10 = (f32[256,128]{1,0:T(8,128)}, f32[256,128]{1,0:T(8,128)S(1)}, u32[]{:S(2)}, u32[]{:S(2)}) collective-permute-start(f32[256,128]{1,0:T(8,128)} %get-tuple-element.4), channel_id=1, source_target_pairs={{0,4},{4,0},{8,12},{12,8},{1,5},{5,1},{9,13},{13,9},{2,6},{6,2},{1... | collective-permute-start | bytes 393224 | tf_op jit(solution)/shard_map/ppermute | solution.py:31
  32.3 16.6 %copy-start.3 = (bf16[128,256]{1,0:T(8,128)(2,1)S(1)}, bf16[128,256]{1,0:T(8,128)(2,1)}, u32[]{:S(2)}) copy-start(bf16[128,256]{1,0:T(8,128)(2,1)} %copy-done.2) | copy-start | bytes 196612
  32.3 16.6 %copy-start.13 = (f32[128]{0:T(128)S(1)}, f32[128]{0:T(128)}, u32[]{:S(2)}) copy-start(f32[128]{0:T(128)} %broadcast_multiply_fusion.2) | copy-start | bytes 1540
  33.4 14.3 %collective-permute-start.13 = (bf16[512,256]{1,0:T(8,128)(2,1)S(1)}, bf16[512,256]{1,0:T(8,128)(2,1)S(1)}, u32[]{:S(2)}, u32[]{:S(2)}) collective-permute-start(bf16[512,256]{1,0:T(8,128)(2,1)S(1)} %pad_maximum_fusion.4), channel_id=1, source_target_pairs={{0,2},{2,0},{1,3},{3,1},{4,6},{6,4},{5,7},{7,5},{8,10},{10,8},{9,1... | collective-permute-start | bytes 786440 | tf_op jit(solution)/shard_map/ppermute | solution.py:31
  37.7 8.4 %collective-permute-start.11 = (f32[256,128]{1,0:T(8,128)S(1)}, f32[256,128]{1,0:T(8,128)S(1)}, u32[]{:S(2)}, u32[]{:S(2)}) collective-permute-start(f32[256,128]{1,0:T(8,128)S(1)} %add.53), channel_id=1, source_target_pairs={{0,8},{4,12},{8,0},{12,4},{1,9},{5,13},{9,1},{13,5},{2,10},{6,14},... | collective-permute-start | bytes 393224 | tf_op jit(solution)/shard_map/ppermute | solution.py:31
  46.1 3.9 %collective-permute-start.12 = (f32[256,128]{1,0:T(8,128)S(1)}, f32[256,128]{1,0:T(8,128)S(1)}, u32[]{:S(2)}, u32[]{:S(2)}) collective-permute-start(f32[256,128]{1,0:T(8,128)S(1)} %add.54), channel_id=1, source_target_pairs={{0,1},{1,0},{2,3},{3,2},{4,5},{5,4},{6,7},{7,6},{8,9},{9,8},{10,11... | collective-permute-start | bytes 393224 | tf_op jit(solution)/shard_map/ppermute | solution.py:31
  46.1 5.9 %collective-permute-start.15 = (f32[256,128]{1,0:T(8,128)S(1)}, f32[256,128]{1,0:T(8,128)S(1)}, u32[]{:S(2)}, u32[]{:S(2)}) collective-permute-start(f32[256,128]{1,0:T(8,128)S(1)} %add.54), channel_id=1, source_target_pairs={{0,2},{2,0},{1,3},{3,1},{4,6},{6,4},{5,7},{7,5},{8,10},{10,8},{9,1... | collective-permute-start | bytes 393224 | tf_op jit(solution)/shard_map/ppermute | solution.py:31
  48.7 4.0 %collective-permute-start.14 = (bf16[256,256]{1,0:T(8,128)(2,1)S(1)}, bf16[256,256]{1,0:T(8,128)(2,1)S(1)}, u32[]{:S(2)}, u32[]{:S(2)}) collective-permute-start(bf16[256,256]{1,0:T(8,128)(2,1)S(1)} %get-tuple-element.10), channel_id=1, source_target_pairs={{0,1},{1,0},{2,3},{3,2},{4,5},{5,4},{6,7},{7,6},{8,9},{9,8},{10,11... | collective-permute-start | bytes 393224 | tf_op jit(solution)/shard_map/ppermute | solution.py:31
  52.0 4.1 %collective-permute-start.16 = (f32[256,128]{1,0:T(8,128)S(1)}, f32[256,128]{1,0:T(8,128)S(1)}, u32[]{:S(2)}, u32[]{:S(2)}) collective-permute-start(f32[256,128]{1,0:T(8,128)S(1)} %collective-permute-done.15), channel_id=1, source_target_pairs={{0,1},{1,0},{2,3},{3,2},{4,5},{5,4},{6,7},{7,6},{8,9},{9,8},{10,11... | collective-permute-start | bytes 393224 | tf_op jit(solution)/shard_map/ppermute | solution.py:31

commit v2 on v0

v2 whole, which is shorter than its diff:
```python
import math

import jax
import jax.numpy as jnp
from jax import lax
from jax.experimental import pallas as pl
from jax.experimental.pallas import tpu as pltpu
from jax.sharding import PartitionSpec as P

RIDGE_COEF = 50.0
LOG2E = 1.4426950408889634
VMEM_LIMIT = 24 << 20
ROWS_ROWS = (((1,), (1,)), ((), ()))
VMEM = pl.BlockSpec(memory_space=pltpu.VMEM)
SMEM = pl.BlockSpec(memory_space=pltpu.SMEM)


def split(values):
    high = values.astype(jnp.bfloat16)
    return high, (values - high.astype(jnp.float32)).astype(jnp.bfloat16)


def dot(left, right, dims=(((1,), (0,)), ((), ()))):
    return lax.dot_general(left, right, dims, preferred_element_type=jnp.float32)


def dot_parts(left, right, dims=(((1,), (0,)), ((), ()))):
    return dot(left[0], right[0], dims) + (dot(left[0], right[1], dims) + dot(left[1], right[0], dims))


def row_sq(points, scale):
    wide = points.astype(jnp.float32)
    high, low = split(wide * wide)
    ones = jnp.ones((8, points.shape[1]), jnp.bfloat16)
    return (dot(ones, high, ROWS_ROWS) + dot(ones, low, ROWS_ROWS))[:1] * scale


def col_sq(points, scale):
    wide = points.astype(jnp.float32)
    return jnp.sum(wide * wide, axis=1, keepdims=True) * scale


def as_column(row):
    lanes = 128
    square = [
        jnp.transpose(jnp.broadcast_to(row[:, at : at + lanes], (lanes, lanes)))[:, :1]
        for at in range(0, row.shape[1], lanes)
    ]
    return jnp.concatenate(square, axis=0)


def owner_span(counts, owner):
    off = jnp.int32(0)
    count = jnp.int32(0)
    for at in range(counts.shape[1]):
        here = counts[0, at]
        off = off + jnp.where(at < owner, here, 0)
        count = count + jnp.where(at == owner, here, 0)
    return off, count


def own_kernel(rows_ref, points_ref, own_ref):
    total, width = points_ref.shape
    cap = own_ref.shape[0]
    step = math.gcd(total, 256)
    row_ids = as_column(rows_ref[...])
    own = jnp.zeros((cap, width), jnp.float32)
    for at in range(0, total, step):
        slot = lax.broadcasted_iota(jnp.int32, (cap, step), 1) + at
        hot = (row_ids == slot).astype(jnp.float32).astype(jnp.bfloat16)
        own = own + dot(hot, points_ref[at : at + step, :])
    own_ref[...] = own.astype(own_ref.dtype)


def prep_kernel(rows_ref, points_ref, weights_ref, targets_ref, shift_ref, sq_ref):
    total, width = points_ref.shape
    cap = targets_ref.shape[0]
    step = math.gcd(total, 256)
    row_ids = as_column(rows_ref[...])
    alpha = jnp.zeros((cap, weights_ref.shape[1]), jnp.float32)
    for at in range(0, total, step):
        slot = lax.broadcasted_iota(jnp.int32, (cap, step), 1) + at
        hot = (row_ids == slot).astype(jnp.float32).astype(jnp.bfloat16)
        alpha = alpha + dot(hot, weights_ref[at : at + step, :])
        sq_ref[:, at : at + step] = row_sq(points_ref[at : at + step, :], LOG2E / width)
    shift_ref[...] = RIDGE_COEF * alpha - targets_ref[...].astype(jnp.float32)


def slab_kernel(n_blocks, n_sub, half, counts, *refs):
    blocks, refs = refs[:n_blocks], refs[n_blocks:]
    slabs, slab_sqs = refs[:n_sub], refs[n_sub : 2 * n_sub]
    slab_ws, shifts = refs[2 * n_sub : 3 * n_sub], refs[3 * n_sub : 4 * n_sub]
    part_ref, live_ref, rows, sums = refs[4 * n_sub :]
    cap, width = blocks[0].shape
    scale = LOG2E / width
    sub_at = lax.axis_index("sub")
    own_at = lax.axis_index("pts") * n_sub + sub_at

    def place(target, values, rel):
        off, count = owner_span(counts, own_at ^ rel)
        skew = lax.rem(off, 8)
        slot = lax.broadcasted_iota(jnp.int32, (cap + 8, 1), 0)
        kept = (slot >= skew) & (slot < skew + count)
        tail = jnp.zeros((8, values.shape[1]), jnp.float32)
        moved = pltpu.roll(jnp.concatenate([values, tail], axis=0), skew, 0)
        here = pl.ds(pl.multiple_of(off - skew, 8), cap + 8)
        target[here, :] = jnp.where(kept, moved, target[here, :])

    for rel in range(n_blocks):
        place(rows, blocks[rel][...].astype(jnp.float32), rel)
    live_ref[...] = rows[: live_ref.shape[0], :].astype(live_ref.dtype)
    start = pl.multiple_of(sub_at * half, half)
    mine = rows[pl.ds(start, half), :]
    mine_sq = jnp.sum(mine * mine, axis=1, keepdims=True) * scale
    mine_x = mine.astype(jnp.bfloat16)
    sums[...] = jnp.zeros_like(sums)
    for rel in range(n_sub):
        place(sums, shifts[rel][...], rel)
    total = sums[pl.ds(start, half), :]
    step = math.gcd(slabs[0].shape[0], 512)
    for which in range(n_sub):
        for at in range(0, slabs[which].shape[0], step):
            inner = dot(mine_x, slabs[which][at : at + step, :], ROWS_ROWS)
            kern = jnp.exp2(inner * (2.0 * scale) - mine_sq - slab_sqs[which][:, at : at + step])
            high, low = split(kern)
            slab_w = slab_ws[which][at : at + step, :]
            total = total + dot(high, slab_w)
            total = total + dot(low, slab_w)
    part_ref[...] = total


def pick_kernel(n_sub, half, pick_ref, live_ref, sent_ref, sketch_ref):
    live = live_ref.shape[0]
    share = sketch_ref.shape[0] // n_sub
    sub_at = lax.axis_index("sub")
    slot = lax.broadcasted_iota(jnp.int32, (sketch_ref.shape[0], live), 1)
    hot = (as_column(pick_ref[...]) == slot).astype(jnp.float32).astype(jnp.bfloat16)
    sketch_ref[...] = dot(hot, live_ref[...]).astype(sketch_ref.dtype)
    sent_ref[:half, :] = live_ref[pl.ds(pl.multiple_of(sub_at * half, half), half), :]
    sent_ref[half:, :] = sketch_ref[pl.ds(pl.multiple_of(sub_at * share, share), share), :]


def gram_kernel(n_sub, n_col, half, counts, *refs):
    own_ref, live_ref, sketch_ref, core_ref = refs[:4]
    got, refs = refs[4 : 4 + (n_col - 1) * n_sub], refs[4 + (n_col - 1) * n_sub :]
    outs, sketch_x = refs[:-1], refs[-1]
    cap, width = own_ref.shape
    picks = sketch_ref.shape[0]
    share = picks // n_sub
    scale = LOG2E / width
    sub_at, col_at = lax.axis_index("sub"), lax.axis_index("col")
    own_at = lax.axis_index("pts") * n_sub + sub_at
    count = owner_span(counts, own_at)[1]
    sketch_x[pl.ds(pl.multiple_of(col_at * picks, picks), picks), :] = sketch_ref[...]
    for col in range(1, n_col):
        for sub in range(n_sub):
            to = (col_at ^ col) * picks + (sub_at ^ sub) * share
            block = got[(col - 1) * n_sub + sub][half:, :]
            sketch_x[pl.ds(pl.multiple_of(to, share), share), :] = block
    points = sketch_x[...]
    points_sq = row_sq(points, scale)

    def kern_of(rows):
        inner = dot(rows, points, ROWS_ROWS)
        return jnp.exp2(inner * (2.0 * scale) - col_sq(rows, scale) - points_sq)

    used = lax.broadcasted_iota(jnp.int32, (cap, 1), 0) < count
    own = jnp.where(used, kern_of(own_ref[...]), 0.0)
    mixed = split(dot_parts(split(own), split(core_ref[...])))
    for at in range(n_col * n_sub):
        if at < n_sub:
            rows = live_ref[pl.ds(pl.multiple_of((sub_at ^ at) * half, half), half), :]
        else:
            rows = got[at - n_sub][:half, :]
        high, low = split(dot_parts(mixed, split(kern_of(rows)), ROWS_ROWS))
        outs[2 * at][...] = high
        outs[2 * at + 1][...] = low


def tile_kernel(n_sub, half, counts, *refs):
    parts, grams = refs[:n_sub], refs[n_sub : 3 * n_sub]
    grad_ref, start_ref, ordered = refs[3 * n_sub :]
    cap = grad_ref.shape[0]
    sub_at = lax.axis_index("sub")
    off, count = owner_span(counts, lax.axis_index("pts") * n_sub + sub_at)
    used = lax.broadcasted_iota(jnp.int32, (cap, 1), 0) < count
    for sub in range(n_sub):
        here = pl.ds(pl.multiple_of((sub_at ^ sub) * half, half), half)
        ordered[here, :] = parts[sub][...]
    skew = lax.rem(off, 8)
    rows = ordered[pl.ds(pl.multiple_of(off - skew, 8), cap + 8), :]
    rows = pltpu.roll(rows, lax.rem(cap + 8 - skew, cap + 8), 0)[:cap]
    grad = jnp.where(used, rows, 0.0)
    grad_ref[...] = grad
    for sub in range(n_sub):
        grad = grad - dot_parts((grams[2 * sub][...], grams[2 * sub + 1][...]), split(parts[sub][...]))
    start_ref[...] = jnp.where(used, grad, 0.0)


def rest_kernel(n_sub, counts, start_ref, *refs):
    grams, others, out_ref = refs[: 2 * (len(refs) // 3)], refs[2 * (len(refs) // 3) : -1], refs[-1]
    count = owner_span(counts, lax.axis_index("pts") * n_sub + lax.axis_index("sub"))[1]
    used = lax.broadcasted_iota(jnp.int32, (out_ref.shape[0], 1), 0) < count
    total = start_ref[...]
    for at, other in enumerate(others):
        total = total - dot_parts((grams[2 * at][...], grams[2 * at + 1][...]), split(other[...]))
    out_ref[...] = jnp.where(used, total, 0.0)


def make_device(mesh):
    n_pts, n_col, n_sub = mesh.shape["pts"], mesh.shape["col"], mesh.shape["sub"]

    def hop(values, axis, step):
        return lax.ppermute(values, axis, [(j, j ^ step) for j in range(mesh.shape[axis])])

    def near_of(values):
        return [values] + [hop(values, "sub", i) for i in range(1, n_sub)]

    def call(kernel, out_shape, smem, arrays, scratch=()):
        return pl.pallas_call(
            kernel,
            out_shape=out_shape,
            in_specs=[SMEM] * len(smem) + [VMEM] * len(arrays),
            out_specs=jax.tree.map(lambda _: VMEM, out_shape),
            scratch_shapes=list(scratch),
            compiler_params=pltpu.CompilerParams(vmem_limit_bytes=VMEM_LIMIT),
        )(*smem, *arrays)

    def per_device(points, weights, tile_rows, tile_count, sketch_pick, block_targets, core_inv):
        return body(points, weights, tile_rows, tile_count, sketch_pick, block_targets, core_inv)

    def body(points, weights, tile_rows, tile_count, sketch_pick, block_targets, core_inv):
        cap = tile_rows.shape[2]
        width, outs = points.shape[1], weights.shape[1]
        owners = tile_count.shape[1]
        live = owners * cap // 2
        half = live // n_sub
        picks = sketch_pick.shape[1]

        def f32(*shape):
            return jax.ShapeDtypeStruct(shape, jnp.float32)

        def bf16(*shape):
            return jax.ShapeDtypeStruct(shape, jnp.bfloat16)

        row_ids = tile_rows[0]
        own_x = call(own_kernel, bf16(cap, width), (), (row_ids, points))
        far = [own_x] + [hop(own_x, "pts", i) for i in range(1, n_pts)]
        slabs = near_of(points)
        slab_ws = near_of(weights)
        shift, slab_sq = call(
            prep_kernel, (f32(cap, outs), f32(1, points.shape[0])), (),
            (row_ids, points, weights, block_targets[0]),
        )
        shifts = near_of(shift)
        slab_sqs = near_of(slab_sq)
        blocks = []
        for at, block in enumerate(far):
            blocks += near_of(block)
        part, live_x = call(
            lambda *refs: slab_kernel(owners, n_sub, half, *refs),
            (f32(half, outs), bf16(live, width)),
            (tile_count,),
            (*blocks, *slabs, *slab_sqs, *slab_ws, *shifts),
            (pltpu.VMEM((live + cap + 8, width), jnp.float32), pltpu.VMEM((live + cap + 8, outs), jnp.float32)),
        )

        step = 1
        while step < n_pts:
            part = part + hop(part, "pts", step)
            step *= 2

        sent, sketch = call(
            lambda *refs: pick_kernel(n_sub, half, *refs),
            (bf16(half + picks // n_sub, width), bf16(picks, width)),
            (),
            (sketch_pick, live_x),
        )
        got = []
        for i in range(1, n_col):
            got += near_of(hop(sent, "col", i))
        grams = call(
            lambda *refs: gram_kernel(n_sub, n_col, half, *refs),
            (bf16(cap, half),) * (2 * n_col * n_sub),
            (tile_count,),
            (own_x, live_x, sketch, core_inv, *got),
            (pltpu.VMEM((n_col * picks, width), jnp.bfloat16),),
        )

        parts = near_of(part)
        block_grad, total = call(
            lambda *refs: tile_kernel(n_sub, half, *refs),
            (f32(cap, outs), f32(cap, outs)),
            (tile_count,),
            (*parts, *grams[: 2 * n_sub]),
            (pltpu.VMEM((live + cap + 8, outs), jnp.float32),),
        )
        first, later, first_grams, later_grams = [], [], [], []
        for i in range(1, n_col):
            other = near_of(hop(part, "col", i))
            at = 2 * i * n_sub
            first += other[:1]
            first_grams += grams[at : at + 2]
            later += other[1:]
            later_grams += grams[at + 2 : at + 2 * n_sub]
        rest = lambda *refs: rest_kernel(n_sub, *refs)
        total = call(rest, f32(cap, outs), (tile_count,), (total, *first_grams, *first))
        direction = call(rest, f32(cap, outs), (tile_count,), (total, *later_grams, *later))
        return (block_grad[None], direction[None])

    return per_device


def solution(mesh):
    in_specs = (
        P(("grp", "pts", "sub"), None),
        P(("grp", "pts", "sub"), None),
        P(("grp", "col"), ("pts", "sub"), None),
        P(("grp", "col"), None),
        P(("grp", "col"), None),
        P(("grp", "col"), ("pts", "sub"), None),
        P("grp", None),
    )
    out_specs = (P(("grp", "col"), ("pts", "sub"), None), P(("grp", "col"), ("pts", "sub"), None))
    return jax.shard_map(
        make_device(mesh), mesh=mesh, in_specs=in_specs, out_specs=out_specs, check_vma=False
    )
```

time: 188 us -> 50.3 us (0.27)
  waiting for transfers between devices: 109 us -> 21 us
  matrix products: 26.7 us -> 0 us
  blocking collectives: 22.9 us -> 0 us
  between operations: 14.2 us -> 0.76 us
  starting transfers between devices: 0.08 us -> 12.5 us
  Pallas kernels: 0 us -> 12.1 us
  other arithmetic: 7.55 us -> 0.04 us
  local copies, waits for them, and re-layouts: 7.9 us -> 3.7 us
    psum x1 -> x0, waiting for transfers between devices: 89.1 us -> none  [per_device(): projected = lax.psum(local_proj, ('pts', 'col', 'sub'))]
    dot_general x12 -> x0, matrix products: 26.7 us -> none  [the longest x4 15.5 us: add_block(): return running + jnp.dot(kern_vals, slab_w, precision=HIGHEST_PREC)]
    all_gather x2 -> x0, blocking collectives: 22.9 us -> none  [the longest x1 16.5 us: per_device(): tile_x = lax.all_gather(own_x, ('pts', 'sub'), axis=0, tiled=True)]
    ppermute x0 -> x18, waiting for transfers between devices: none -> 21 us  [hop(): lax.ppermute(values, axis, [(j, j ^ step) for j in range(mesh.shape[axis])])]
    reduce_scatter x1 -> x0, waiting for transfers between devices: 19.5 us -> none  [per_device(): lax.psum_scatter(lax.fori_loop(0, slab_total // slab_step, add_block, sta...]
    ppermute x0 -> x18, starting transfers between devices: none -> 12.5 us  [hop(): lax.ppermute(values, axis, [(j, j ^ step) for j in range(mesh.shape[axis])])]
    pallas_call x0 -> x8, Pallas kernels: none -> 12.1 us  [call(): pl.pallas_call(kernel, out_shape=out_shape, in_specs=[SMEM] * len(smem) +...]
    gather x4 -> x0, local copies, waits for them, and re-layouts: 6.98 us -> none  [the longest x1 2.12 us: per_device(): own_x = jnp.where(used_float > 0, jnp.take(points, own_rows, axis=0), 0)]
  transfers between devices with their start and end apart: 2 -> 18, of which waited for: 2 -> 9; matrix products, arithmetic and copies ran while one was open for 3% -> 0% of each run, Pallas kernels for 0% -> 13%
where the time goes in v2:
time: 50.3 us; the launch traced here: 50 us
  waiting for transfers between devices  21 us (42%)
  starting transfers between devices  12.5 us (25%)
  Pallas kernels  12.1 us (24%)
  local copies, waits for them, and re-layouts  3.7 us (7%)
  between operations  0.76 us (2%)
    ppermute x18, waiting for transfers between devices, hop(): lax.ppermute(values, axis, [(j, j ^ step) for j in range(mesh.shape[axis])])  21 us
    ppermute x18, starting transfers between devices, hop(): lax.ppermute(values, axis, [(j, j ^ step) for j in range(mesh.shape[axis])])  12.5 us
    pallas_call x8, Pallas kernels, call(): pl.pallas_call(kernel, out_shape=out_shape, in_specs=[SMEM] * len(smem) +...  12.1 us
    unnamed x18, local copies, waits for them, and re-layouts  3.7 us
  transfers between devices with their start and end apart: 18, of which 9 were waited for; matrix products, arithmetic and copies ran while one was open for 0% of the time, Pallas kernels for 13%

profile of v2, /device:TPU:0, one launch (start us, length us, event | category | flops | bytes accessed | tf_op | source)
XLA Modules:
  0.0 50.0 jit_solution(15297456263970256559)
XLA Ops:
  0.6 0.6 %collective-permute-start.7 = (bf16[2048,256]{1,0:T(8,128)(2,1)}, bf16[2048,256]{1,0:T(8,128)(2,1)S(1)}, u32[]{:S(2)}, u32[]{:S(2)}) collective-permute-start(bf16[2048,256]{1,0:T(8,128)(2,1)} %refs_9_.1), channel_id=1, source_target_pairs={{0,1},{1,0},{2,3},{3,2},{4,5},{5,4},{6,7},{7,6},{8,9},{9,8},{10,11... | collective-permute-start | bytes 3145736 | tf_op jit(solution)/shard_map/ppermute | solution.py:214
  1.2 0.1 collective-permute-start.9
  1.3 0.7 %copy-done.7 = s32[1,1,128]{2,1,0:T(1,128)S(1)} copy-done((s32[1,1,128]{2,1,0:T(1,128)S(1)}, s32[1,1,128]{2,1,0:T(1,128)}, u32[]{:S(2)}) %copy-start.7) | copy-done | bytes 536
  1.9 1.2 %copy-done = bf16[2048,256]{1,0:T(8,128)(2,1)S(1)} copy-done((bf16[2048,256]{1,0:T(8,128)(2,1)S(1)}, bf16[2048,256]{1,0:T(8,128)(2,1)}, u32[]{:S(2)}) %copy-start) | copy-done | bytes 1048600
  3.1 1.0 %copy-done.2 = bf16[2048,128]{1,0:T(8,128)(2,1)S(1)} copy-done((bf16[2048,128]{1,0:T(8,128)(2,1)S(1)}, bf16[2048,128]{1,0:T(8,128)(2,1)}, u32[]{:S(2)}) %copy-start.2) | copy-done | bytes 524312
  4.2 0.8 %copy-done.5 = bf16[1,128,128]{2,1,0:T(8,128)(2,1)S(1)} copy-done((bf16[1,128,128]{2,1,0:T(8,128)(2,1)S(1)}, bf16[1,128,128]{2,1,0:T(8,128)(2,1)}, u32[]{:S(2)}) %copy-start.5) | copy-done | bytes 32792
  5.0 0.9 %shard_map.87 = (f32[128,128]{1,0:T(8,128)S(1)}, f32[1,2048]{1,0:T(1,128)S(1)}) custom-call(s32[1,128]{1,0:T(1,128)S(1)} %bitcast.5, bf16[2048,256]{1,0:T(8,128)(2,1)S(1)} %copy-done, bf16[2048,128]{1,0:T(8,128)(2,1)S(1)} %copy-done.2, bf16[128,128]{1,0:T(8,128)(2,1)S(1)} %bitcast.4), custom_call_target="tpu_custom_call" | custom-call | tf_op jit(solution)/shard_map/pallas_call | solution.py:220
  5.8 0.4 collective-permute-start.10
  6.3 0.4 shard_map.86.refs_1_
  6.7 0.0 copy-start.6
  6.7 4.7 %collective-permute-start.5 = (bf16[128,256]{1,0:T(8,128)(2,1)S(1)}, bf16[128,256]{1,0:T(8,128)(2,1)S(1)}, u32[]{:S(2)}, u32[]{:S(2)}) collective-permute-start(bf16[128,256]{1,0:T(8,128)(2,1)S(1)} %shard_map.86.refs_1_), channel_id=1, source_target_pairs={{0,12},{4,8},{8,4},{12,0},{1,13},{5,9},{9,5},{13,1},{2,14},{6,10},... | collective-permute-start | bytes 196616 | tf_op jit(solution)/shard_map/ppermute | solution.py:214
  11.4 0.2 collective-permute-start.8
  11.6 1.0 %collective-permute-done.8.refs_12_ = f32[1,2048]{1,0:T(1,128)S(1)} collective-permute-done((f32[1,2048]{1,0:T(1,128)S(1)}, f32[1,2048]{1,0:T(1,128)S(1)}, u32[]{:S(2)}, u32[]{:S(2)}) %collective-permute-start.8) | collective-permute-done | bytes 8224 | tf_op jit(solution)/shard_map/ppermute | solution.py:214
  12.6 0.0 collective-permute-start.3
  12.6 0.0 collective-permute-done.10.refs_16_
  12.6 0.7 %collective-permute-start.1 = (bf16[128,256]{1,0:T(8,128)(2,1)S(1)}, bf16[128,256]{1,0:T(8,128)(2,1)S(1)}, u32[]{:S(2)}, u32[]{:S(2)}) collective-permute-start(bf16[128,256]{1,0:T(8,128)(2,1)S(1)} %shard_map.86.refs_1_), channel_id=1, source_target_pairs={{0,4},{4,0},{8,12},{12,8},{1,5},{5,1},{9,13},{13,9},{2,6},{6,2},{1... | collective-permute-start | bytes 196616 | tf_op jit(solution)/shard_map/ppermute | solution.py:214
  13.4 0.9 %collective-permute-done.5.refs_7_ = bf16[128,256]{1,0:T(8,128)(2,1)S(1)} collective-permute-done((bf16[128,256]{1,0:T(8,128)(2,1)S(1)}, bf16[128,256]{1,0:T(8,128)(2,1)S(1)}, u32[]{:S(2)}, u32[]{:S(2)}) %collective-permute-start.5) | collective-permute-done | bytes 65568 | tf_op jit(solution)/shard_map/ppermute | solution.py:214
  14.2 4.0 %collective-permute-done.3.refs_5_ = bf16[128,256]{1,0:T(8,128)(2,1)S(1)} collective-permute-done((bf16[128,256]{1,0:T(8,128)(2,1)S(1)}, bf16[128,256]{1,0:T(8,128)(2,1)S(1)}, u32[]{:S(2)}, u32[]{:S(2)}) %collective-permute-start.3) | collective-permute-done | bytes 65568 | tf_op jit(solution)/shard_map/ppermute | solution.py:214
  18.3 0.0 collective-permute-start.6
  18.3 0.0 collective-permute-done.1.refs_3_
  18.3 0.5 collective-permute-start.4
  18.8 0.0 collective-permute-done.refs_2_
  18.8 0.1 collective-permute-start.2
  18.9 0.7 %collective-permute-done.6.refs_8_ = bf16[128,256]{1,0:T(8,128)(2,1)S(1)} collective-permute-done((bf16[128,256]{1,0:T(8,128)(2,1)S(1)}, bf16[128,256]{1,0:T(8,128)(2,1)S(1)}, u32[]{:S(2)}, u32[]{:S(2)}) %collective-permute-start.6) | collective-permute-done | bytes 65568 | tf_op jit(solution)/shard_map/ppermute | solution.py:214
  19.5 0.2 collective-permute-done.4.refs_6_
  19.7 0.4 collective-permute-done.2.refs_4_
  20.1 0.0 collective-permute-done.7.refs_10_
  20.1 0.0 copy-start.8
  20.1 4.0 %shard_map.88 = (f32[256,128]{1,0:T(8,128)S(1)}, bf16[512,256]{1,0:T(8,128)(2,1)S(1)}) custom-call(s32[1,8]{1,0:T(1,128)S(1)} %copy-done.6, bf16[128,256]{1,0:T(8,128)(2,1)S(1)} %shard_map.86.refs_1_, bf16[128,256]{1,0:T(8,128)(2,1)S(1)} %collective-permute-done.refs_2_, bf16[128,256]{1,0:T(8,128)(2,1)S(1)} %collective-permute-done.1.refs_3_, ...), custom_call_target="tpu_custom_call" | custom-call | tf_op jit(solution)/shard_map/pallas_call | solution.py:220
  24.1 0.0 copy-start.4
  24.1 0.2 collective-permute-start.11
  24.3 0.4 shard_map.89
  24.7 1.5 %collective-permute-start.14 = (bf16[384,256]{1,0:T(8,128)(2,1)S(1)}, bf16[384,256]{1,0:T(8,128)(2,1)S(1)}, u32[]{:S(2)}, u32[]{:S(2)}) collective-permute-start(bf16[384,256]{1,0:T(8,128)(2,1)S(1)} %get-tuple-element.23), channel_id=1, source_target_pairs={{0,2},{2,0},{1,3},{3,1},{4,6},{6,4},{5,7},{7,5},{8,10},{10,8},{9,1... | collective-permute-start | bytes 589832 | tf_op jit(solution)/shard_map/ppermute | solution.py:214
  26.2 3.5 %collective-permute-done.11 = f32[256,128]{1,0:T(8,128)S(1)} collective-permute-done((f32[256,128]{1,0:T(8,128)S(1)}, f32[256,128]{1,0:T(8,128)S(1)}, u32[]{:S(2)}, u32[]{:S(2)}) %collective-permute-start.11) | collective-permute-done | bytes 131104 | tf_op jit(solution)/shard_map/ppermute | solution.py:214
  29.7 1.5 %collective-permute-start.12 = (f32[256,128]{1,0:T(8,128)S(1)}, f32[256,128]{1,0:T(8,128)S(1)}, u32[]{:S(2)}, u32[]{:S(2)}) collective-permute-start(f32[256,128]{1,0:T(8,128)S(1)} %add.6), channel_id=1, source_target_pairs={{0,8},{4,12},{8,0},{12,4},{1,9},{5,13},{9,1},{13,5},{2,10},{6,14},... | collective-permute-start | bytes 393224 | tf_op jit(solution)/shard_map/ppermute | solution.py:214
  31.2 6.9 %collective-permute-done.12 = f32[256,128]{1,0:T(8,128)S(1)} collective-permute-done((f32[256,128]{1,0:T(8,128)S(1)}, f32[256,128]{1,0:T(8,128)S(1)}, u32[]{:S(2)}, u32[]{:S(2)}) %collective-permute-start.12) | collective-permute-done | bytes 131104 | tf_op jit(solution)/shard_map/ppermute | solution.py:214
  38.1 1.6 %collective-permute-start.16 = (f32[256,128]{1,0:T(8,128)S(1)}, f32[256,128]{1,0:T(8,128)S(1)}, u32[]{:S(2)}, u32[]{:S(2)}) collective-permute-start(f32[256,128]{1,0:T(8,128)S(1)} %add.7.refs_1_), channel_id=1, source_target_pairs={{0,2},{2,0},{1,3},{3,1},{4,6},{6,4},{5,7},{7,5},{8,10},{10,8},{9,1... | collective-permute-start | bytes 393224 | tf_op jit(solution)/shard_map/ppermute | solution.py:214
  39.7 0.0 collective-permute-done.14.refs_5_
  39.7 0.0 collective-permute-start.15
  39.7 0.5 %collective-permute-start.13 = (f32[256,128]{1,0:T(8,128)S(1)}, f32[256,128]{1,0:T(8,128)S(1)}, u32[]{:S(2)}, u32[]{:S(2)}) collective-permute-start(f32[256,128]{1,0:T(8,128)S(1)} %add.7.refs_1_), channel_id=1, source_target_pairs={{0,1},{1,0},{2,3},{3,2},{4,5},{5,4},{6,7},{7,6},{8,9},{9,8},{10,11... | collective-permute-start | bytes 393224 | tf_op jit(solution)/shard_map/ppermute | solution.py:214
  40.2 3.4 %collective-permute-done.16.refs_4_ = f32[256,128]{1,0:T(8,128)S(1)} collective-permute-done((f32[256,128]{1,0:T(8,128)S(1)}, f32[256,128]{1,0:T(8,128)S(1)}, u32[]{:S(2)}, u32[]{:S(2)}) %collective-permute-start.16) | collective-permute-done | bytes 131104 | tf_op jit(solution)/shard_map/ppermute | solution.py:214
  43.6 0.0 collective-permute-start.17
  43.6 2.9 %shard_map.90 = (bf16[128,256]{1,0:T(8,128)(2,1)S(1)}, bf16[128,256]{1,0:T(8,128)(2,1)S(1)}, bf16[128,256]{1,0:T(8,128)(2,1)S(1)}, bf16[128,256]{1,0:T(8,128)(2,...) custom-call(s32[1,8]{1,0:T(1,128)S(1)} %copy-done.6, ...), custom_call_target="tpu_custom_call" | custom-call | tf_op jit(solution)/shard_map/pallas_call | solution.py:220
  46.6 0.0 collective-permute-done.13.refs_2_
  46.6 1.3 %shard_map.91 = (f32[128,128]{1,0:T(8,128)}, f32[128,128]{1,0:T(8,128)S(1)}) custom-call(s32[1,8]{1,0:T(1,128)S(1)} %copy-done.6, f32[256,128]{1,0:T(8,128)S(1)} %add.7.refs_1_, f32[256,128]{1,0:T(8,128)S(1)} %collective-permute-done.13.refs_2_, bf16[128,256]{1,0:T(8,128)(2,1)S(1)} %get-tuple-element.24.refs_3_, ...), custom_call_target="tpu_custom_call" | custom-call | tf_op jit(solution)/shard_map/pallas_call | solution.py:220
  47.9 0.7 %shard_map.92.refs_1_ = f32[128,128]{1,0:T(8,128)S(1)} custom-call(s32[1,8]{1,0:T(1,128)S(1)} %copy-done.6, f32[128,128]{1,0:T(8,128)S(1)} %get-tuple-element.29.refs_1_, bf16[128,256]{1,0:T(8,128)(2,1)S(1)} %get-tuple-element.30.refs_2_, bf16[128,256]{1,0:T(8,128)(2,1)S(1)} %get-tuple-element.31.refs_3_, f32[256,128]{1,0:T(8,128)S(1)} %collective-permute-done.16.refs_4_), custom_call_target="tpu_custom_call" | custom-call | tf_op jit(solution)/shard_map/pallas_call | solution.py:220
  48.6 0.0 collective-permute-done.17.refs_4_
  48.7 1.4 %shard_map.93 = f32[128,128]{1,0:T(8,128)} custom-call(s32[1,8]{1,0:T(1,128)S(1)} %copy-done.6, f32[128,128]{1,0:T(8,128)S(1)} %shard_map.92.refs_1_, bf16[128,256]{1,0:T(8,128)(2,1)S(1)} %get-tuple-element.32.refs_2_, bf16[128,256]{1,0:T(8,128)(2,1)S(1)} %get-tuple-element.33.refs_3_, f32[256,128]{1,0:T(8,128)S(1)} %collective-permute-done.17.refs_4_), custom_call_target="tpu_custom_call" | custom-call | tf_op jit(solution)/shard_map/pallas_call | solution.py:220
  (16 shorter events, 0.1 us)
Async XLA Ops:
  0.6 19.4 %collective-permute-start.7 = (bf16[2048,256]{1,0:T(8,128)(2,1)}, bf16[2048,256]{1,0:T(8,128)(2,1)S(1)}, u32[]{:S(2)}, u32[]{:S(2)}) collective-permute-start(bf16[2048,256]{1,0:T(8,128)(2,1)} %refs_9_.1), channel_id=1, source_target_pairs={{0,1},{1,0},{2,3},{3,2},{4,5},{5,4},{6,7},{7,6},{8,9},{9,8},{10,11... | collective-permute-start | bytes 3145736 | tf_op jit(solution)/shard_map/ppermute | solution.py:214
  1.2 18.9 %collective-permute-start.9 = (bf16[2048,128]{1,0:T(8,128)(2,1)}, bf16[2048,128]{1,0:T(8,128)(2,1)S(1)}, u32[]{:S(2)}, u32[]{:S(2)}) collective-permute-start(bf16[2048,128]{1,0:T(8,128)(2,1)} %refs_13_.1), channel_id=1, source_target_pairs={{0,1},{1,0},{2,3},{3,2},{4,5},{5,4},{6,7},{7,6},{8,9},{9,8},{10,11... | collective-permute-start | bytes 1572872 | tf_op jit(solution)/shard_map/ppermute | solution.py:214
  1.3 0.7 %copy-start.7 = (s32[1,1,128]{2,1,0:T(1,128)S(1)}, s32[1,1,128]{2,1,0:T(1,128)}, u32[]{:S(2)}) copy-start(s32[1,1,128]{2,1,0:T(1,128)} %param.9) | copy-start | bytes 1540
  1.9 1.2 %copy-start = (bf16[2048,256]{1,0:T(8,128)(2,1)S(1)}, bf16[2048,256]{1,0:T(8,128)(2,1)}, u32[]{:S(2)}) copy-start(bf16[2048,256]{1,0:T(8,128)(2,1)} %refs_9_.1) | copy-start | bytes 3145732
  3.1 1.0 %copy-start.2 = (bf16[2048,128]{1,0:T(8,128)(2,1)S(1)}, bf16[2048,128]{1,0:T(8,128)(2,1)}, u32[]{:S(2)}) copy-start(bf16[2048,128]{1,0:T(8,128)(2,1)} %refs_13_.1) | copy-start | bytes 1572868
  4.2 0.8 %copy-start.5 = (bf16[1,128,128]{2,1,0:T(8,128)(2,1)S(1)}, bf16[1,128,128]{2,1,0:T(8,128)(2,1)}, u32[]{:S(2)}) copy-start(bf16[1,128,128]{2,1,0:T(8,128)(2,1)} %param.12) | copy-start | bytes 98308
  4.9 15.1 %copy-start.1 = (bf16[2048,256]{1,0:T(8,128)(2,1)S(1)}, bf16[2048,256]{1,0:T(8,128)(2,1)}, u32[]{:S(2)}) copy-start(bf16[2048,256]{1,0:T(8,128)(2,1)} %refs_9_.1) | copy-start | bytes 3145732
  5.8 14.2 %copy-start.3 = (bf16[2048,128]{1,0:T(8,128)(2,1)S(1)}, bf16[2048,128]{1,0:T(8,128)(2,1)}, u32[]{:S(2)}) copy-start(bf16[2048,128]{1,0:T(8,128)(2,1)} %refs_13_.1) | copy-start | bytes 1572868
  5.8 6.8 %collective-permute-start.10 = (f32[128,128]{1,0:T(8,128)S(1)}, f32[128,128]{1,0:T(8,128)S(1)}, u32[]{:S(2)}, u32[]{:S(2)}) collective-permute-start(f32[128,128]{1,0:T(8,128)S(1)} %get-tuple-element.19.refs_15_), channel_id=1, source_target_pairs={{0,1},{1,0},{2,3},{3,2},{4,5},{5,4},{6,7},{7,6},{8,9},{9,8},{10,11... | collective-permute-start | bytes 196616 | tf_op jit(solution)/shard_map/ppermute | solution.py:214
  6.7 13.4 %copy-start.6 = (s32[1,8]{1,0:T(1,128)S(1)}, s32[1,8]{1,0:T(1,128)}, u32[]{:S(2)}) copy-start(s32[1,8]{1,0:T(1,128)} %refs_0_.11) | copy-start | bytes 100
  6.7 7.5 %collective-permute-start.5 = (bf16[128,256]{1,0:T(8,128)(2,1)S(1)}, bf16[128,256]{1,0:T(8,128)(2,1)S(1)}, u32[]{:S(2)}, u32[]{:S(2)}) collective-permute-start(bf16[128,256]{1,0:T(8,128)(2,1)S(1)} %shard_map.86.refs_1_), channel_id=1, source_target_pairs={{0,12},{4,8},{8,4},{12,0},{1,13},{5,9},{9,5},{13,1},{2,14},{6,10},... | collective-permute-start | bytes 196616 | tf_op jit(solution)/shard_map/ppermute | solution.py:214
  11.4 1.2 %collective-permute-start.8 = (f32[1,2048]{1,0:T(1,128)S(1)}, f32[1,2048]{1,0:T(1,128)S(1)}, u32[]{:S(2)}, u32[]{:S(2)}) collective-permute-start(f32[1,2048]{1,0:T(1,128)S(1)} %get-tuple-element.18.refs_11_), channel_id=1, source_target_pairs={{0,1},{1,0},{2,3},{3,2},{4,5},{5,4},{6,7},{7,6},{8,9},{9,8},{10,11... | collective-permute-start | bytes 24584 | tf_op jit(solution)/shard_map/ppermute | solution.py:214
  12.6 5.7 %collective-permute-start.3 = (bf16[128,256]{1,0:T(8,128)(2,1)S(1)}, bf16[128,256]{1,0:T(8,128)(2,1)S(1)}, u32[]{:S(2)}, u32[]{:S(2)}) collective-permute-start(bf16[128,256]{1,0:T(8,128)(2,1)S(1)} %shard_map.86.refs_1_), channel_id=1, source_target_pairs={{0,8},{4,12},{8,0},{12,4},{1,9},{5,13},{9,1},{13,5},{2,10},{6,14},... | collective-permute-start | bytes 196616 | tf_op jit(solution)/shard_map/ppermute | solution.py:214
  12.6 5.7 %collective-permute-start.1 = (bf16[128,256]{1,0:T(8,128)(2,1)S(1)}, bf16[128,256]{1,0:T(8,128)(2,1)S(1)}, u32[]{:S(2)}, u32[]{:S(2)}) collective-permute-start(bf16[128,256]{1,0:T(8,128)(2,1)S(1)} %shard_map.86.refs_1_), channel_id=1, source_target_pairs={{0,4},{4,0},{8,12},{12,8},{1,5},{5,1},{9,13},{13,9},{2,6},{6,2},{1... | collective-permute-start | bytes 196616 | tf_op jit(solution)/shard_map/ppermute | solution.py:214
  14.2 4.6 %collective-permute-start = (bf16[128,256]{1,0:T(8,128)(2,1)S(1)}, bf16[128,256]{1,0:T(8,128)(2,1)S(1)}, u32[]{:S(2)}, u32[]{:S(2)}) collective-permute-start(bf16[128,256]{1,0:T(8,128)(2,1)S(1)} %shard_map.86.refs_1_), channel_id=1, source_target_pairs={{0,1},{1,0},{2,3},{3,2},{4,5},{5,4},{6,7},{7,6},{8,9},{9,8},{10,11... | collective-permute-start | bytes 196616 | tf_op jit(solution)/shard_map/ppermute | solution.py:214
  18.3 1.3 %collective-permute-start.6 = (bf16[128,256]{1,0:T(8,128)(2,1)S(1)}, bf16[128,256]{1,0:T(8,128)(2,1)S(1)}, u32[]{:S(2)}, u32[]{:S(2)}) collective-permute-start(bf16[128,256]{1,0:T(8,128)(2,1)S(1)} %collective-permute-done.5.refs_7_), channel_id=1, source_target_pairs={{0,1},{1,0},{2,3},{3,2},{4,5},{5,4},{6,7},{7,6},{8,9},{9,8},{10,11... | collective-permute-start | bytes 196616 | tf_op jit(solution)/shard_map/ppermute | solution.py:214
  18.3 1.4 %collective-permute-start.4 = (bf16[128,256]{1,0:T(8,128)(2,1)S(1)}, bf16[128,256]{1,0:T(8,128)(2,1)S(1)}, u32[]{:S(2)}, u32[]{:S(2)}) collective-permute-start(bf16[128,256]{1,0:T(8,128)(2,1)S(1)} %collective-permute-done.3.refs_5_), channel_id=1, source_target_pairs={{0,1},{1,0},{2,3},{3,2},{4,5},{5,4},{6,7},{7,6},{8,9},{9,8},{10,11... | collective-permute-start | bytes 196616 | tf_op jit(solution)/shard_map/ppermute | solution.py:214
  18.8 1.3 %collective-permute-start.2 = (bf16[128,256]{1,0:T(8,128)(2,1)S(1)}, bf16[128,256]{1,0:T(8,128)(2,1)S(1)}, u32[]{:S(2)}, u32[]{:S(2)}) collective-permute-start(bf16[128,256]{1,0:T(8,128)(2,1)S(1)} %collective-permute-done.1.refs_3_), channel_id=1, source_target_pairs={{0,1},{1,0},{2,3},{3,2},{4,5},{5,4},{6,7},{7,6},{8,9},{9,8},{10,11... | collective-permute-start | bytes 196616 | tf_op jit(solution)/shard_map/ppermute | solution.py:214
  20.1 4.2 %copy-start.8 = (s32[1,256]{1,0:T(1,128)S(1)}, s32[1,256]{1,0:T(1,128)}, u32[]{:S(2)}) copy-start(s32[1,256]{1,0:T(1,128)} %refs_0_.7) | copy-start | bytes 3076
  24.1 19.5 %copy-start.4 = (f32[512,512]{1,0:T(8,128)S(1)}, f32[512,512]{1,0:T(8,128)}, u32[]{:S(2)}) copy-start(f32[512,512]{1,0:T(8,128)} %refs_4_.1) | copy-start | bytes 3145732
  24.1 5.6 %collective-permute-start.11 = (f32[256,128]{1,0:T(8,128)S(1)}, f32[256,128]{1,0:T(8,128)S(1)}, u32[]{:S(2)}, u32[]{:S(2)}) collective-permute-start(f32[256,128]{1,0:T(8,128)S(1)} %get-tuple-element.20), channel_id=1, source_target_pairs={{0,4},{4,0},{8,12},{12,8},{1,5},{5,1},{9,13},{13,9},{2,6},{6,2},{1... | collective-permute-start | bytes 393224 | tf_op jit(solution)/shard_map/ppermute | solution.py:214
  24.7 15.0 %collective-permute-start.14 = (bf16[384,256]{1,0:T(8,128)(2,1)S(1)}, bf16[384,256]{1,0:T(8,128)(2,1)S(1)}, u32[]{:S(2)}, u32[]{:S(2)}) collective-permute-start(bf16[384,256]{1,0:T(8,128)(2,1)S(1)} %get-tuple-element.23), channel_id=1, source_target_pairs={{0,2},{2,0},{1,3},{3,1},{4,6},{6,4},{5,7},{7,5},{8,10},{10,8},{9,1... | collective-permute-start | bytes 589832 | tf_op jit(solution)/shard_map/ppermute | solution.py:214
  29.7 8.4 %collective-permute-start.12 = (f32[256,128]{1,0:T(8,128)S(1)}, f32[256,128]{1,0:T(8,128)S(1)}, u32[]{:S(2)}, u32[]{:S(2)}) collective-permute-start(f32[256,128]{1,0:T(8,128)S(1)} %add.6), channel_id=1, source_target_pairs={{0,8},{4,12},{8,0},{12,4},{1,9},{5,13},{9,1},{13,5},{2,10},{6,14},... | collective-permute-start | bytes 393224 | tf_op jit(solution)/shard_map/ppermute | solution.py:214
  38.1 5.5 %collective-permute-start.16 = (f32[256,128]{1,0:T(8,128)S(1)}, f32[256,128]{1,0:T(8,128)S(1)}, u32[]{:S(2)}, u32[]{:S(2)}) collective-permute-start(f32[256,128]{1,0:T(8,128)S(1)} %add.7.refs_1_), channel_id=1, source_target_pairs={{0,2},{2,0},{1,3},{3,1},{4,6},{6,4},{5,7},{7,5},{8,10},{10,8},{9,1... | collective-permute-start | bytes 393224 | tf_op jit(solution)/shard_map/ppermute | solution.py:214
  39.7 3.9 %collective-permute-start.15 = (bf16[384,256]{1,0:T(8,128)(2,1)S(1)}, bf16[384,256]{1,0:T(8,128)(2,1)S(1)}, u32[]{:S(2)}, u32[]{:S(2)}) collective-permute-start(bf16[384,256]{1,0:T(8,128)(2,1)S(1)} %collective-permute-done.14.refs_5_), channel_id=1, source_target_pairs={{0,1},{1,0},{2,3},{3,2},{4,5},{5,4},{6,7},{7,6},{8,9},{9,8},{10,11... | collective-permute-start | bytes 589832 | tf_op jit(solution)/shard_map/ppermute | solution.py:214
  39.7 6.9 %collective-permute-start.13 = (f32[256,128]{1,0:T(8,128)S(1)}, f32[256,128]{1,0:T(8,128)S(1)}, u32[]{:S(2)}, u32[]{:S(2)}) collective-permute-start(f32[256,128]{1,0:T(8,128)S(1)} %add.7.refs_1_), channel_id=1, source_target_pairs={{0,1},{1,0},{2,3},{3,2},{4,5},{5,4},{6,7},{7,6},{8,9},{9,8},{10,11... | collective-permute-start | bytes 393224 | tf_op jit(solution)/shard_map/ppermute | solution.py:214
  43.6 5.0 %collective-permute-start.17 = (f32[256,128]{1,0:T(8,128)S(1)}, f32[256,128]{1,0:T(8,128)S(1)}, u32[]{:S(2)}, u32[]{:S(2)}) collective-permute-start(f32[256,128]{1,0:T(8,128)S(1)} %collective-permute-done.16.refs_4_), channel_id=1, source_target_pairs={{0,1},{1,0},{2,3},{3,2},{4,5},{5,4},{6,7},{7,6},{8,9},{9,8},{10,11... | collective-permute-start | bytes 393224 | tf_op jit(solution)/shard_map/ppermute | solution.py:214

commit v3 on v2

v3 whole, which is shorter than its diff:
```python
import math

import jax
import jax.numpy as jnp
from jax import lax
from jax.experimental import pallas as pl
from jax.experimental.pallas import tpu as pltpu
from jax.sharding import PartitionSpec as P

RIDGE_COEF = 50.0
LOG2E = 1.4426950408889634
VMEM_LIMIT = 24 << 20
ROWS_ROWS = (((1,), (1,)), ((), ()))
VMEM = pl.BlockSpec(memory_space=pltpu.VMEM)
SMEM = pl.BlockSpec(memory_space=pltpu.SMEM)


def split(values):
    high = values.astype(jnp.bfloat16)
    return high, (values - high.astype(jnp.float32)).astype(jnp.bfloat16)


def dot(left, right, dims=(((1,), (0,)), ((), ()))):
    return lax.dot_general(left, right, dims, preferred_element_type=jnp.float32)


def dot_parts(left, right, dims=(((1,), (0,)), ((), ()))):
    return dot(left[0], right[0], dims) + (dot(left[0], right[1], dims) + dot(left[1], right[0], dims))


def row_sq(points, scale):
    wide = points.astype(jnp.float32)
    high, low = split(wide * wide)
    ones = jnp.ones((8, points.shape[1]), jnp.bfloat16)
    return (dot(ones, high, ROWS_ROWS) + dot(ones, low, ROWS_ROWS))[:1] * scale


def col_sq(points, scale):
    wide = points.astype(jnp.float32)
    return jnp.sum(wide * wide, axis=1, keepdims=True) * scale


def as_column(row):
    lanes = 128
    square = [
        jnp.transpose(jnp.broadcast_to(row[:, at : at + lanes], (lanes, lanes)))[:, :1]
        for at in range(0, row.shape[1], lanes)
    ]
    return jnp.concatenate(square, axis=0)


def owner_span(counts, owner):
    off = jnp.int32(0)
    count = jnp.int32(0)
    for at in range(counts.shape[1]):
        here = counts[0, at]
        off = off + jnp.where(at < owner, here, 0)
        count = count + jnp.where(at == owner, here, 0)
    return off, count


def one_hot(row_ids, at, step):
    slot = lax.broadcasted_iota(jnp.int32, (row_ids.shape[0], step), 1) + at
    return (row_ids == slot).astype(jnp.float32).astype(jnp.bfloat16)


def own_kernel(rows_hbm, points_hbm, own_ref, rows_ref, points_ref, rows_sem, points_sem):
    total, width = points_ref.shape
    cap = own_ref.shape[0]
    step = math.gcd(total, 256)
    rows_copy = pltpu.make_async_copy(rows_hbm, rows_ref, rows_sem)
    points_copy = pltpu.make_async_copy(points_hbm, points_ref, points_sem)
    rows_copy.start()
    points_copy.start()
    rows_copy.wait()
    row_ids = as_column(rows_ref[...])
    points_copy.wait()
    own = jnp.zeros((cap, width), jnp.float32)
    for at in range(0, total, step):
        own = own + dot(one_hot(row_ids, at, step), points_ref[at : at + step, :])
    own_ref[...] = own.astype(own_ref.dtype)


def prep_kernel(rows_ref, weights_ref, targets_ref, shift_ref, turned_ref):
    total = weights_ref.shape[0]
    step = math.gcd(total, 256)
    row_ids = as_column(rows_ref[...])
    alpha = jnp.zeros(shift_ref.shape, jnp.float32)
    for at in range(0, total, step):
        part = weights_ref[at : at + step, :]
        alpha = alpha + dot(one_hot(row_ids, at, step), part)
        turned_ref[:, at : at + step] = jnp.transpose(part.astype(jnp.float32)).astype(jnp.bfloat16)
    shift_ref[...] = RIDGE_COEF * alpha - targets_ref[...].astype(jnp.float32)


def norm_kernel(points_ref, sq_ref):
    sq_ref[...] = col_sq(points_ref[...], LOG2E / points_ref.shape[1])


def slab_kernel(n_blocks, n_sub, quarter, counts, *refs):
    blocks, refs = refs[:n_blocks], refs[n_blocks:]
    slabs, slab_sqs = refs[:n_sub], refs[n_sub : 2 * n_sub]
    slab_ws, shifts = refs[2 * n_sub : 3 * n_sub], refs[3 * n_sub : 4 * n_sub]
    keep_ref, send_ref, live_ref, rows, sums = refs[4 * n_sub :]
    cap, width = blocks[0].shape
    scale = LOG2E / width
    pts_at, sub_at = lax.axis_index("pts"), lax.axis_index("sub")
    own_at = pts_at * n_sub + sub_at

    def place(target, values, rel):
        off, count = owner_span(counts, own_at ^ rel)
        skew = lax.rem(off, 8)
        slot = lax.broadcasted_iota(jnp.int32, (cap + 8, 1), 0)
        kept = (slot >= skew) & (slot < skew + count)
        source = lax.broadcasted_iota(jnp.int32, (cap + 8, cap), 1) + skew
        move = (lax.broadcasted_iota(jnp.int32, (cap + 8, cap), 0) == source)
        move = move.astype(jnp.float32).astype(jnp.bfloat16)
        moved = sum(dot(move, part) for part in values)
        here = pl.ds(pl.multiple_of(off - skew, 8), cap + 8)
        target[here, :] = jnp.where(kept, moved, target[here, :])

    for rel in range(n_blocks):
        place(rows, [blocks[rel][...]], rel)
    live_ref[...] = rows[: live_ref.shape[0], :].astype(live_ref.dtype)
    sums[...] = jnp.zeros_like(sums)
    for rel in range(n_sub):
        high, low = split(shifts[rel][...])
        rest = shifts[rel][...] - high.astype(jnp.float32) - low.astype(jnp.float32)
        place(sums, [high, low, rest.astype(jnp.bfloat16)], rel)
    base = (sub_at * 2 + pts_at % 2) * quarter
    keep = pl.ds(pl.multiple_of(base, quarter), quarter)
    send = pl.ds(pl.multiple_of((sub_at * 2 + 1 - pts_at % 2) * quarter, quarter), quarter)
    mine_x = jnp.concatenate([rows[keep, :], rows[send, :]], axis=0).astype(jnp.bfloat16)
    mine_sq = row_sq(mine_x, scale)
    total = jnp.zeros((keep_ref.shape[1], 2 * quarter), jnp.float32)
    step = math.gcd(slabs[0].shape[0], 256)
    for which in range(n_sub):
        for at in range(0, slabs[which].shape[0], step):
            inner = dot(slabs[which][at : at + step, :], mine_x, ROWS_ROWS)
            kern = jnp.exp2(inner * (2.0 * scale) - mine_sq - slab_sqs[which][at : at + step, :])
            high, low = split(kern)
            turned = slab_ws[which][:, at : at + step]
            total = total + dot(turned, high) + dot(turned, low)
    total = jnp.transpose(total)
    keep_ref[...] = total[:quarter] + sums[keep, :]
    send_ref[...] = total[quarter:] + sums[send, :]


def pick_kernel(half, pick_ref, live_ref, rows_ref, share_ref, sketch_ref):
    live = live_ref.shape[0]
    share = share_ref.shape[0]
    sub_at = lax.axis_index("sub")
    hot = one_hot(as_column(pick_ref[...]), 0, live)
    sketch_ref[...] = dot(hot, live_ref[...]).astype(sketch_ref.dtype)
    rows_ref[...] = live_ref[pl.ds(pl.multiple_of(sub_at * half, half), half), :]
    share_ref[...] = sketch_ref[pl.ds(pl.multiple_of(sub_at * share, share), share), :]


def sketch_rows(rows, points, points_sq):
    inner = dot(rows, points, ROWS_ROWS)
    scale = LOG2E / rows.shape[1]
    return jnp.exp2(inner * (2.0 * scale) - col_sq(rows, scale) - points_sq)


def gram_group(mixed, points, points_sq, blocks, high_ref, low_ref):
    parts = split(sketch_rows(jnp.concatenate(blocks, axis=0), points, points_sq))
    high_ref[...], low_ref[...] = split(dot_parts(mixed, parts, ROWS_ROWS))


def near_gram_kernel(n_sub, n_col, quarter, groups, counts, *refs):
    own_ref, live_ref, sketch_ref, core_ref = refs[:4]
    got, refs = refs[4 : 4 + (n_col - 1) * n_sub], refs[4 + (n_col - 1) * n_sub :]
    sketch_x, mixed_high, mixed_low, outs = refs[0], refs[1], refs[2], refs[3:]
    cap, width = own_ref.shape
    picks = sketch_ref.shape[0]
    share = picks // n_sub
    pts_at, sub_at, col_at = lax.axis_index("pts"), lax.axis_index("sub"), lax.axis_index("col")
    count = owner_span(counts, pts_at * n_sub + sub_at)[1]
    sketch_x[pl.ds(pl.multiple_of(col_at * picks, picks), picks), :] = sketch_ref[...]
    for col in range(1, n_col):
        for sub in range(n_sub):
            to = (col_at ^ col) * picks + (sub_at ^ sub) * share
            sketch_x[pl.ds(pl.multiple_of(to, share), share), :] = got[(col - 1) * n_sub + sub][...]
    points = sketch_x[...]
    points_sq = row_sq(points, LOG2E / width)
    used = lax.broadcasted_iota(jnp.int32, (cap, 1), 0) < count
    own = jnp.where(used, sketch_rows(own_ref[...], points, points_sq), 0.0)
    mixed = split(dot_parts(split(own), split(core_ref[...])))
    mixed_high[...], mixed_low[...] = mixed
    for at, group in enumerate(groups):
        blocks = []
        for _, pts, sub in group:
            base = ((sub_at ^ sub) * 2 + (pts_at % 2 ^ pts)) * quarter
            blocks.append(live_ref[pl.ds(pl.multiple_of(base, quarter), quarter), :])
        gram_group(mixed, points, points_sq, blocks, *outs[2 * at : 2 * at + 2])


def far_gram_kernel(n_sub, quarter, groups, *refs):
    sketch_x, mixed_high, mixed_low = refs[:3]
    got, outs = refs[3 : -2 * len(groups)], refs[-2 * len(groups) :]
    pts_at = lax.axis_index("pts")
    points = sketch_x[...]
    points_sq = row_sq(points, LOG2E / points.shape[1])
    for at, group in enumerate(groups):
        blocks = []
        for col, pts, sub in group:
            base = (pts_at % 2 ^ pts) * quarter
            blocks.append(got[(col - 1) * n_sub + sub][pl.ds(pl.multiple_of(base, quarter), quarter), :])
        mixed = (mixed_high[...], mixed_low[...])
        gram_group(mixed, points, points_sq, blocks, *outs[2 * at : 2 * at + 2])


def apply_grams(grams, parts):
    total, at = None, 0
    for high, low in grams:
        many = high.shape[1] // parts[0].shape[0]
        right = split(jnp.concatenate([ref[...] for ref in parts[at : at + many]], axis=0))
        term = dot_parts((high[...], low[...]), right)
        total = term if total is None else total + term
        at += many
    return total


def part_kernel(n_grams, *refs):
    grams = [refs[2 * at : 2 * at + 2] for at in range(n_grams)]
    refs[-1][...] = apply_grams(grams, refs[2 * n_grams : -1])


def last_kernel(n_sub, n_early, n_grams, counts, *refs):
    early, refs = refs[:n_early], refs[n_early:]
    grams, refs = [refs[2 * at : 2 * at + 2] for at in range(n_grams)], refs[2 * n_grams :]
    tile, later, refs = refs[: 2 * n_sub], refs[2 * n_sub : -3], refs[-3:]
    grad_ref, out_ref, ordered = refs
    cap = grad_ref.shape[0]
    quarter = tile[0].shape[0]
    pts_at, sub_at = lax.axis_index("pts"), lax.axis_index("sub")
    off, count = owner_span(counts, pts_at * n_sub + sub_at)
    used = lax.broadcasted_iota(jnp.int32, (cap, 1), 0) < count
    for at in range(2 * n_sub):
        to = ((sub_at ^ (at % n_sub)) * 2 + (pts_at % 2 ^ (at // n_sub))) * quarter
        ordered[pl.ds(pl.multiple_of(to, quarter), quarter), :] = tile[at][...]
    skew = lax.rem(off, 8)
    rows = ordered[pl.ds(pl.multiple_of(off - skew, 8), cap + 8), :]
    rows = pltpu.roll(rows, lax.rem(cap + 8 - skew, cap + 8), 0)[:cap]
    grad = jnp.where(used, rows, 0.0)
    grad_ref[...] = grad
    for ref in early:
        grad = grad - ref[...]
    out_ref[...] = jnp.where(used, grad - apply_grams(grams, later), 0.0)


def make_device(mesh):
    n_pts, n_col, n_sub = mesh.shape["pts"], mesh.shape["col"], mesh.shape["sub"]

    def hop(values, axis, step):
        axes = axis if isinstance(axis, tuple) else (axis,)
        size = math.prod(mesh.shape[name] for name in axes)
        return lax.ppermute(values, axis, [(j, j ^ step) for j in range(size)])

    def near_of(values):
        return [values] + [hop(values, "sub", i) for i in range(1, n_sub)]

    def call(kernel, out_shape, smem, arrays, scratch=(), space=VMEM):
        return pl.pallas_call(
            kernel,
            out_shape=out_shape,
            in_specs=[SMEM] * len(smem) + [space] * len(arrays),
            out_specs=jax.tree.map(lambda _: VMEM, out_shape),
            scratch_shapes=list(scratch),
            compiler_params=pltpu.CompilerParams(vmem_limit_bytes=VMEM_LIMIT),
        )(*smem, *arrays)

    def per_device(points, weights, tile_rows, tile_count, sketch_pick, block_targets, core_inv):
        return body(points, weights, tile_rows, tile_count, sketch_pick, block_targets, core_inv)

    def body(points, weights, tile_rows, tile_count, sketch_pick, block_targets, core_inv):
        cap = tile_rows.shape[2]
        width, outs = points.shape[1], weights.shape[1]
        owners = tile_count.shape[1]
        live = owners * cap // 2
        quarter = live // n_sub // 2
        picks = sketch_pick.shape[1]

        def f32(*shape):
            return jax.ShapeDtypeStruct(shape, jnp.float32)

        def bf16(*shape):
            return jax.ShapeDtypeStruct(shape, jnp.bfloat16)

        own_x, row_ids, points = call(
            own_kernel,
            (bf16(cap, width), jax.ShapeDtypeStruct((1, cap), jnp.int32), bf16(*points.shape)),
            (),
            tuple(
                pltpu.with_memory_space_constraint(value, pltpu.MemorySpace.HBM)
                for value in (tile_rows[0], points)
            ),
            (pltpu.SemaphoreType.DMA(()), pltpu.SemaphoreType.DMA(())),
            pl.BlockSpec(memory_space=pltpu.MemorySpace.HBM),
        )
        far = [own_x] + [hop(own_x, "pts", i) for i in range(1, n_pts)]
        slabs = near_of(points)
        shift, turned = call(
            prep_kernel, (f32(cap, outs), bf16(outs, points.shape[0])), (),
            (row_ids, weights, block_targets[0]),
        )
        slab_ws = near_of(turned)
        shifts = near_of(shift)
        slab_sqs = [call(norm_kernel, f32(points.shape[0], 1), (), (slab,)) for slab in slabs]
        blocks = []
        for block in far:
            blocks += near_of(block)
        part, send, live_x = call(
            lambda *refs: slab_kernel(owners, n_sub, quarter, *refs),
            (f32(quarter, outs), f32(quarter, outs), bf16(live, width)),
            (tile_count,),
            (*blocks, *slabs, *slab_sqs, *slab_ws, *shifts),
            (pltpu.VMEM((live + cap + 8, width), jnp.float32), pltpu.VMEM((live + cap + 8, outs), jnp.float32)),
        )

        part = part + hop(send, "pts", 1)
        step = 2
        while step < n_pts:
            part = part + hop(part, "pts", step)
            step *= 2

        rows, share, sketch = call(
            lambda *refs: pick_kernel(2 * quarter, *refs),
            (bf16(2 * quarter, width), bf16(picks // n_sub, width), bf16(picks, width)),
            (),
            (sketch_pick, live_x),
        )
        got_sketch, got_rows = [], []
        for i in range(1, n_col):
            got_sketch += near_of(hop(share, "col", i))
        for i in range(1, n_col):
            got_rows += near_of(hop(rows, "col", i))

        def gram_shapes(groups):
            return tuple(bf16(cap, quarter * len(group)) for group in groups for _ in range(2))

        away = [(col, pts) for col in range(1, n_col) for pts in range(2)]
        near_groups = [
            [(0, 0, sub) for sub in range(n_sub)],
            [(0, 1, 0)],
            [(0, 1, sub) for sub in range(1, n_sub)],
        ]
        far_groups = [
            [(col, pts, 0) for col, pts in away],
            [(col, pts, sub) for col, pts in away for sub in range(1, n_sub)],
        ]
        near_grams = call(
            lambda *refs: near_gram_kernel(n_sub, n_col, quarter, near_groups, *refs),
            (bf16(n_col * picks, width), *(bf16(cap, n_col * picks),) * 2, *gram_shapes(near_groups)),
            (tile_count,),
            (own_x, live_x, sketch, core_inv, *got_sketch),
        )
        far_grams = call(
            lambda *refs: far_gram_kernel(n_sub, quarter, far_groups, *refs),
            gram_shapes(far_groups),
            (),
            (*near_grams[:3], *got_rows),
        )
        near_grams = near_grams[3:]
        grads = {}
        for sub, value in enumerate(near_of(part)):
            grads[0, 0, sub] = value
        for col, pts in [*reversed(away), (0, 1)]:
            other = hop(part, ("pts", "col"), pts * n_col + col)
            for sub, value in enumerate(near_of(other)):
                grads[col, pts, sub] = value

        def data(*groups):
            return [grads[key] for group in groups for key in group]

        early = [
            call(lambda *refs: part_kernel(1, *refs), f32(cap, outs), (),
                 (*near_grams[:2], *data(near_groups[0]))),
            call(lambda *refs: part_kernel(2, *refs), f32(cap, outs), (),
                 (*near_grams[2:4], *far_grams[:2], *data(near_groups[1], far_groups[0]))),
        ]
        block_grad, direction = call(
            lambda *refs: last_kernel(n_sub, len(early), 2, *refs),
            (f32(cap, outs), f32(cap, outs)),
            (tile_count,),
            (
                *early, *near_grams[4:], *far_grams[2:],
                *[grads[0, pts, sub] for pts in range(2) for sub in range(n_sub)],
                *data(near_groups[2], far_groups[1]),
            ),
            (pltpu.VMEM((live + cap + 8, outs), jnp.float32),),
        )
        return (block_grad[None], direction[None])

    return per_device


def solution(mesh):
    in_specs = (
        P(("grp", "pts", "sub"), None),
        P(("grp", "pts", "sub"), None),
        P(("grp", "col"), ("pts", "sub"), None),
        P(("grp", "col"), None),
        P(("grp", "col"), None),
        P(("grp", "col"), ("pts", "sub"), None),
        P("grp", None),
    )
    out_specs = (P(("grp", "col"), ("pts", "sub"), None), P(("grp", "col"), ("pts", "sub"), None))
    return jax.shard_map(
        make_device(mesh), mesh=mesh, in_specs=in_specs, out_specs=out_specs, check_vma=False
    )
```

time: 50.3 us -> 43.7 us (0.87)
  waiting for transfers between devices: 21 us -> 14.4 us
  starting transfers between devices: 12.5 us -> 16.2 us
  local copies, waits for them, and re-layouts: 3.7 us -> 0.79 us
  Pallas kernels: 12.1 us -> 11.3 us
    ppermute x18 -> x23, waiting for transfers between devices: 21 us -> 14.4 us  [hop(): return lax.ppermute(values, axis, [(j, j ^ step) for j in range(size)])]
    ppermute x18 -> x23, starting transfers between devices: 12.5 us -> 16.2 us  [hop(): return lax.ppermute(values, axis, [(j, j ^ step) for j in range(size)])]
    unnamed x18 -> x10, local copies, waits for them, and re-layouts: 3.7 us -> 0.79 us
    pallas_call x8 -> x11, Pallas kernels: 12.1 us -> 11.3 us  [call(): pl.pallas_call(kernel, out_shape=out_shape, in_specs=[SMEM] * len(smem) +...]
  transfers between devices with their start and end apart: 18 -> 23, of which waited for: 9 -> 7; matrix products, arithmetic and copies ran while one was open for 0% -> 0% of each run, Pallas kernels for 13% -> 12%
where the time goes in v3:
time: 43.7 us; the launch traced here: 43.5 us
  starting transfers between devices  16.2 us (37%)
  waiting for transfers between devices  14.4 us (33%)
  Pallas kernels  11.3 us (26%)
  between operations  0.81 us (2%)
  local copies, waits for them, and re-layouts  0.79 us (2%)
    ppermute x23, starting transfers between devices, hop(): return lax.ppermute(values, axis, [(j, j ^ step) for j in range(size)])  16.2 us
    ppermute x23, waiting for transfers between devices, hop(): return lax.ppermute(values, axis, [(j, j ^ step) for j in range(size)])  14.4 us
    pallas_call x11, Pallas kernels, call(): pl.pallas_call(kernel, out_shape=out_shape, in_specs=[SMEM] * len(smem) +...  11.3 us
  transfers between devices with their start and end apart: 23, of which 7 were waited for; matrix products, arithmetic and copies ran while one was open for 0% of the time, Pallas kernels for 12%

profile of v3, /device:TPU:0, one launch (start us, length us, event | category | flops | bytes accessed | tf_op | source)
XLA Modules:
  0.0 43.5 jit_solution(12427307266310092047)
XLA Ops:
  0.7 1.7 %shard_map.86 = (bf16[128,256]{1,0:T(8,128)(2,1)S(1)}, s32[1,128]{1,0:T(1,128)S(1)}, bf16[2048,256]{1,0:T(8,128)(2,1)S(1)}) custom-call(s32[1,128]{1,0:T(1,128)} %bitcast.5, bf16[2048,256]{1,0:T(8,128)(2,1)} %points_hbm.1), custom_call_target="tpu_custom_call" | custom-call | tf_op jit(solution)/shard_map/pallas_call | solution.py:264
  2.3 0.6 %collective-permute-start.7 = (bf16[2048,256]{1,0:T(8,128)(2,1)S(1)}, bf16[2048,256]{1,0:T(8,128)(2,1)S(1)}, u32[]{:S(2)}, u32[]{:S(2)}) collective-permute-start(bf16[2048,256]{1,0:T(8,128)(2,1)S(1)} %get-tuple-element.29.points_ref.refs_9_), channel_id=1, source_target_pairs={{0,1},{1,0},{2,3},{3,2},{4,5},{5,4},{6,7},{7,6},{8,9},{9,8},{10,11... | collective-permute-start | bytes 3145736 | tf_op jit(solution)/shard_map/ppermute | solution.py:258
  2.9 0.4 shard_map.89
  3.3 0.1 collective-permute-start.8
  3.4 5.1 %collective-permute-start.5 = (bf16[128,256]{1,0:T(8,128)(2,1)S(1)}, bf16[128,256]{1,0:T(8,128)(2,1)S(1)}, u32[]{:S(2)}, u32[]{:S(2)}) collective-permute-start(bf16[128,256]{1,0:T(8,128)(2,1)S(1)} %get-tuple-element.28.refs_1_), channel_id=1, source_target_pairs={{0,12},{4,8},{8,4},{12,0},{1,13},{5,9},{9,5},{13,1},{2,14},{6,10},... | collective-permute-start | bytes 196616 | tf_op jit(solution)/shard_map/ppermute | solution.py:258
  8.5 0.0 collective-permute-start.3
  8.5 0.6 %collective-permute-start.1 = (bf16[128,256]{1,0:T(8,128)(2,1)S(1)}, bf16[128,256]{1,0:T(8,128)(2,1)S(1)}, u32[]{:S(2)}, u32[]{:S(2)}) collective-permute-start(bf16[128,256]{1,0:T(8,128)(2,1)S(1)} %get-tuple-element.28.refs_1_), channel_id=1, source_target_pairs={{0,4},{4,0},{8,12},{12,8},{1,5},{5,1},{9,13},{13,9},{2,6},{6,2},{1... | collective-permute-start | bytes 196616 | tf_op jit(solution)/shard_map/ppermute | solution.py:258
  9.1 2.0 %collective-permute-done.5.refs_7_ = bf16[128,256]{1,0:T(8,128)(2,1)S(1)} collective-permute-done((bf16[128,256]{1,0:T(8,128)(2,1)S(1)}, bf16[128,256]{1,0:T(8,128)(2,1)S(1)}, u32[]{:S(2)}, u32[]{:S(2)}) %collective-permute-start.5) | collective-permute-done | bytes 65568 | tf_op jit(solution)/shard_map/ppermute | solution.py:258
  11.0 0.0 collective-permute-start
  11.0 3.3 %collective-permute-done.3.refs_5_ = bf16[128,256]{1,0:T(8,128)(2,1)S(1)} collective-permute-done((bf16[128,256]{1,0:T(8,128)(2,1)S(1)}, bf16[128,256]{1,0:T(8,128)(2,1)S(1)}, u32[]{:S(2)}, u32[]{:S(2)}) %collective-permute-start.3) | collective-permute-done | bytes 65568 | tf_op jit(solution)/shard_map/ppermute | solution.py:258
  14.3 0.0 collective-permute-start.9
  14.3 0.0 collective-permute-done.1.refs_3_
  14.3 0.5 %collective-permute-start.6 = (bf16[128,256]{1,0:T(8,128)(2,1)S(1)}, bf16[128,256]{1,0:T(8,128)(2,1)S(1)}, u32[]{:S(2)}, u32[]{:S(2)}) collective-permute-start(bf16[128,256]{1,0:T(8,128)(2,1)S(1)} %collective-permute-done.5.refs_7_), channel_id=1, source_target_pairs={{0,1},{1,0},{2,3},{3,2},{4,5},{5,4},{6,7},{7,6},{8,9},{9,8},{10,11... | collective-permute-start | bytes 196616 | tf_op jit(solution)/shard_map/ppermute | solution.py:258
  14.9 0.0 collective-permute-done.refs_2_
  14.9 0.1 collective-permute-start.4
  14.9 0.0 collective-permute-done.7.points_ref.refs_10_
  14.9 0.4 %collective-permute-start.2 = (bf16[128,256]{1,0:T(8,128)(2,1)S(1)}, bf16[128,256]{1,0:T(8,128)(2,1)S(1)}, u32[]{:S(2)}, u32[]{:S(2)}) collective-permute-start(bf16[128,256]{1,0:T(8,128)(2,1)S(1)} %collective-permute-done.1.refs_3_), channel_id=1, source_target_pairs={{0,1},{1,0},{2,3},{3,2},{4,5},{5,4},{6,7},{7,6},{8,9},{9,8},{10,11... | collective-permute-start | bytes 196616 | tf_op jit(solution)/shard_map/ppermute | solution.py:258
  15.4 0.3 shard_map.87.refs_11_
  15.7 0.0 copy-start.3
  15.7 0.3 shard_map.88.refs_12_
  16.1 0.0 collective-permute-done.9.refs_16_
  16.1 0.0 collective-permute-done.4.refs_6_
  16.1 0.2 collective-permute-done.2.refs_4_
  16.3 0.1 copy-done.3
  16.4 2.7 %shard_map.90 = (f32[128,128]{1,0:T(8,128)S(1)}, f32[128,128]{1,0:T(8,128)S(1)}, bf16[512,256]{1,0:T(8,128)(2,1)S(1)}) custom-call(s32[1,8]{1,0:T(1,128)S(1)} %copy-done.3, bf16[128,256]{1,0:T(8,128)(2,1)S(1)} %get-tuple-element.28.refs_1_, bf16[128,256]{1,0:T(8,128)(2,1)S(1)} %collective-permute-done.refs_2_, ...), custom_call_target="tpu_custom_call" | custom-call | tf_op jit(solution)/shard_map/pallas_call | solution.py:264
  19.1 0.0 copy-start.4
  19.1 0.7 %copy-done.4 = s32[1,256]{1,0:T(1,128)S(1)} copy-done((s32[1,256]{1,0:T(1,128)S(1)}, s32[1,256]{1,0:T(1,128)}, u32[]{:S(2)}) %copy-start.4) | copy-done | bytes 1048
  19.8 0.4 shard_map.91
  20.2 1.6 %collective-permute-start.15 = (bf16[256,256]{1,0:T(8,128)(2,1)S(1)}, bf16[256,256]{1,0:T(8,128)(2,1)S(1)}, u32[]{:S(2)}, u32[]{:S(2)}) collective-permute-start(bf16[256,256]{1,0:T(8,128)(2,1)S(1)} %get-tuple-element.45), channel_id=1, source_target_pairs={{0,2},{2,0},{1,3},{3,1},{4,6},{6,4},{5,7},{7,5},{8,10},{10,8},{9,1... | collective-permute-start | bytes 393224 | tf_op jit(solution)/shard_map/ppermute | solution.py:258
  21.8 0.8 %collective-permute-start.12 = (f32[128,128]{1,0:T(8,128)S(1)}, f32[128,128]{1,0:T(8,128)S(1)}, u32[]{:S(2)}, u32[]{:S(2)}) collective-permute-start(f32[128,128]{1,0:T(8,128)S(1)} %get-tuple-element.39), channel_id=1, source_target_pairs={{0,4},{4,0},{8,12},{12,8},{1,5},{5,1},{9,13},{13,9},{2,6},{6,2},{1... | collective-permute-start | bytes 196616 | tf_op jit(solution)/shard_map/ppermute | solution.py:258
  22.6 0.5 %collective-permute-start.10 = (bf16[128,256]{1,0:T(8,128)(2,1)S(1)}, bf16[128,256]{1,0:T(8,128)(2,1)S(1)}, u32[]{:S(2)}, u32[]{:S(2)}) collective-permute-start(bf16[128,256]{1,0:T(8,128)(2,1)S(1)} %get-tuple-element.35), channel_id=1, source_target_pairs={{0,2},{2,0},{1,3},{3,1},{4,6},{6,4},{5,7},{7,5},{8,10},{10,8},{9,1... | collective-permute-start | bytes 196616 | tf_op jit(solution)/shard_map/ppermute | solution.py:258
  23.2 2.9 %collective-permute-done.12 = f32[128,128]{1,0:T(8,128)S(1)} collective-permute-done((f32[128,128]{1,0:T(8,128)S(1)}, f32[128,128]{1,0:T(8,128)S(1)}, u32[]{:S(2)}, u32[]{:S(2)}) %collective-permute-start.12) | collective-permute-done | bytes 65568 | tf_op jit(solution)/shard_map/ppermute | solution.py:258
  26.1 1.3 %collective-permute-start.13 = (f32[128,128]{1,0:T(8,128)S(1)}, f32[128,128]{1,0:T(8,128)S(1)}, u32[]{:S(2)}, u32[]{:S(2)}) collective-permute-start(f32[128,128]{1,0:T(8,128)S(1)} %add.6), channel_id=1, source_target_pairs={{0,8},{4,12},{8,0},{12,4},{1,9},{5,13},{9,1},{13,5},{2,10},{6,14},... | collective-permute-start | bytes 196616 | tf_op jit(solution)/shard_map/ppermute | solution.py:258
  27.4 0.0 collective-permute-done.10.refs_5_
  27.4 0.0 collective-permute-start.11
  27.4 0.5 %collective-permute-start.16 = (bf16[256,256]{1,0:T(8,128)(2,1)S(1)}, bf16[256,256]{1,0:T(8,128)(2,1)S(1)}, u32[]{:S(2)}, u32[]{:S(2)}) collective-permute-start(bf16[256,256]{1,0:T(8,128)(2,1)S(1)} %collective-permute-done.15.refs_3_), channel_id=1, source_target_pairs={{0,1},{1,0},{2,3},{3,2},{4,5},{5,4},{6,7},{7,6},{8,9},{9,8},{10,11... | collective-permute-start | bytes 393224 | tf_op jit(solution)/shard_map/ppermute | solution.py:258
  27.9 4.1 %collective-permute-done.13 = f32[128,128]{1,0:T(8,128)S(1)} collective-permute-done((f32[128,128]{1,0:T(8,128)S(1)}, f32[128,128]{1,0:T(8,128)S(1)}, u32[]{:S(2)}, u32[]{:S(2)}) %collective-permute-start.13) | collective-permute-done | bytes 65568 | tf_op jit(solution)/shard_map/ppermute | solution.py:258
  32.0 0.3 collective-permute-start.19
  32.3 1.5 %collective-permute-start.18 = (f32[128,128]{1,0:T(8,128)S(1)}, f32[128,128]{1,0:T(8,128)S(1)}, u32[]{:S(2)}, u32[]{:S(2)}) collective-permute-start(f32[128,128]{1,0:T(8,128)S(1)} %add.7.refs_2_.refs_7_), channel_id=1, source_target_pairs={{0,2},{2,0},{4,6},{6,4},{8,10},{10,8},{12,14},{14,12},{1,3},{3,1},... | collective-permute-start | bytes 196616 | tf_op jit(solution)/shard_map/ppermute | solution.py:258
  33.8 1.8 %collective-permute-start.17 = (f32[128,128]{1,0:T(8,128)S(1)}, f32[128,128]{1,0:T(8,128)S(1)}, u32[]{:S(2)}, u32[]{:S(2)}) collective-permute-start(f32[128,128]{1,0:T(8,128)S(1)} %add.7.refs_2_.refs_7_), channel_id=1, source_target_pairs={{0,4},{2,6},{4,0},{6,2},{8,12},{10,14},{12,8},{14,10},{1,5},{3,7},... | collective-permute-start | bytes 196616 | tf_op jit(solution)/shard_map/ppermute | solution.py:258
  35.6 1.7 %collective-permute-done.19.refs_6_ = f32[128,128]{1,0:T(8,128)S(1)} collective-permute-done((f32[128,128]{1,0:T(8,128)S(1)}, f32[128,128]{1,0:T(8,128)S(1)}, u32[]{:S(2)}, u32[]{:S(2)}) %collective-permute-start.19) | collective-permute-done | bytes 65568 | tf_op jit(solution)/shard_map/ppermute | solution.py:258
  37.3 0.5 %collective-permute-start.21 = (f32[128,128]{1,0:T(8,128)S(1)}, f32[128,128]{1,0:T(8,128)S(1)}, u32[]{:S(2)}, u32[]{:S(2)}) collective-permute-start(f32[128,128]{1,0:T(8,128)S(1)} %collective-permute-done.18.refs_5_), channel_id=1, source_target_pairs={{0,1},{1,0},{2,3},{3,2},{4,5},{5,4},{6,7},{7,6},{8,9},{9,8},{10,11... | collective-permute-start | bytes 196616 | tf_op jit(solution)/shard_map/ppermute | solution.py:258
  37.8 0.3 collective-permute-done.17.refs_4_.refs_9_
  38.0 2.4 %shard_map.92 = (bf16[512,256]{1,0:T(8,128)(2,1)S(1)}, bf16[128,512]{1,0:T(8,128)(2,1)S(1)}, bf16[128,512]{1,0:T(8,128)(2,1)S(1)}, bf16[128,256]{1,0:T(8,128)(2,...) custom-call(s32[1,8]{1,0:T(1,128)S(1)} %copy-done.3, ...), custom_call_target="tpu_custom_call" | custom-call | tf_op jit(solution)/shard_map/pallas_call | solution.py:264
  40.5 0.2 shard_map.93.refs_1_
  40.7 1.1 %shard_map.94 = (bf16[128,256]{1,0:T(8,128)(2,1)S(1)}, bf16[128,256]{1,0:T(8,128)(2,1)S(1)}, bf16[128,256]{1,0:T(8,128)(2,1)S(1)}, bf16[128,256]{1,0:T(8,128)(2,1)S(1)}) custom-call(bf16[512,256]{1,0:T(8,128)(2,1)S(1)} %get-tuple-element.42.refs_0_, bf16[128,512]{1,0:T(8,128)(2,1)S(1)} %get-tuple-element.43.refs_1_, ...), custom_call_target="tpu_custom_call" | custom-call | tf_op jit(solution)/shard_map/pallas_call | solution.py:264
  41.8 0.2 shard_map.95.refs_2_
  42.1 1.4 %shard_map.96 = (f32[128,128]{1,0:T(8,128)}, f32[128,128]{1,0:T(8,128)}) custom-call(s32[1,8]{1,0:T(1,128)S(1)} %copy-done.3, f32[128,128]{1,0:T(8,128)S(1)} %shard_map.93.refs_1_, f32[128,128]{1,0:T(8,128)S(1)} %shard_map.95.refs_2_, bf16[128,128]{1,0:T(8,128)(2,1)S(1)} %get-tuple-element.48.refs_3_, bf16[128,128]{1,0:T(8,128)(2,1)S(1)} %get-tuple-element.49.refs_4_, ...), custom_call_target="tpu_custom_call" | custom-call | tf_op jit(solution)/shard_map/pallas_call | solution.py:264
  (21 shorter events, 0.1 us)
Async XLA Ops:
  0.6 2.3 %copy-start.1 = (bf16[2048,128]{1,0:T(8,128)(2,1)S(1)}, bf16[2048,128]{1,0:T(8,128)(2,1)}, u32[]{:S(2)}) copy-start(bf16[2048,128]{1,0:T(8,128)(2,1)} %weights_ref.1) | copy-start | bytes 1572868
  0.6 2.3 %copy-start.2 = (bf16[1,128,128]{2,1,0:T(8,128)(2,1)S(1)}, bf16[1,128,128]{2,1,0:T(8,128)(2,1)}, u32[]{:S(2)}) copy-start(bf16[1,128,128]{2,1,0:T(8,128)(2,1)} %param.12) | copy-start | bytes 98308
  2.3 12.6 %collective-permute-start.7 = (bf16[2048,256]{1,0:T(8,128)(2,1)S(1)}, bf16[2048,256]{1,0:T(8,128)(2,1)S(1)}, u32[]{:S(2)}, u32[]{:S(2)}) collective-permute-start(bf16[2048,256]{1,0:T(8,128)(2,1)S(1)} %get-tuple-element.29.points_ref.refs_9_), channel_id=1, source_target_pairs={{0,1},{1,0},{2,3},{3,2},{4,5},{5,4},{6,7},{7,6},{8,9},{9,8},{10,11... | collective-permute-start | bytes 3145736 | tf_op jit(solution)/shard_map/ppermute | solution.py:258
  3.3 12.9 %collective-permute-start.8 = (bf16[128,2048]{1,0:T(8,128)(2,1)S(1)}, bf16[128,2048]{1,0:T(8,128)(2,1)S(1)}, u32[]{:S(2)}, u32[]{:S(2)}) collective-permute-start(bf16[128,2048]{1,0:T(8,128)(2,1)S(1)} %get-tuple-element.31.refs_13_), channel_id=1, source_target_pairs={{0,1},{1,0},{2,3},{3,2},{4,5},{5,4},{6,7},{7,6},{8,9},{9,8},{10,11... | collective-permute-start | bytes 1572872 | tf_op jit(solution)/shard_map/ppermute | solution.py:258
  3.4 7.6 %collective-permute-start.5 = (bf16[128,256]{1,0:T(8,128)(2,1)S(1)}, bf16[128,256]{1,0:T(8,128)(2,1)S(1)}, u32[]{:S(2)}, u32[]{:S(2)}) collective-permute-start(bf16[128,256]{1,0:T(8,128)(2,1)S(1)} %get-tuple-element.28.refs_1_), channel_id=1, source_target_pairs={{0,12},{4,8},{8,4},{12,0},{1,13},{5,9},{9,5},{13,1},{2,14},{6,10},... | collective-permute-start | bytes 196616 | tf_op jit(solution)/shard_map/ppermute | solution.py:258
  8.5 5.8 %collective-permute-start.3 = (bf16[128,256]{1,0:T(8,128)(2,1)S(1)}, bf16[128,256]{1,0:T(8,128)(2,1)S(1)}, u32[]{:S(2)}, u32[]{:S(2)}) collective-permute-start(bf16[128,256]{1,0:T(8,128)(2,1)S(1)} %get-tuple-element.28.refs_1_), channel_id=1, source_target_pairs={{0,8},{4,12},{8,0},{12,4},{1,9},{5,13},{9,1},{13,5},{2,10},{6,14},... | collective-permute-start | bytes 196616 | tf_op jit(solution)/shard_map/ppermute | solution.py:258
  8.5 5.8 %collective-permute-start.1 = (bf16[128,256]{1,0:T(8,128)(2,1)S(1)}, bf16[128,256]{1,0:T(8,128)(2,1)S(1)}, u32[]{:S(2)}, u32[]{:S(2)}) collective-permute-start(bf16[128,256]{1,0:T(8,128)(2,1)S(1)} %get-tuple-element.28.refs_1_), channel_id=1, source_target_pairs={{0,4},{4,0},{8,12},{12,8},{1,5},{5,1},{9,13},{13,9},{2,6},{6,2},{1... | collective-permute-start | bytes 196616 | tf_op jit(solution)/shard_map/ppermute | solution.py:258
  11.0 3.8 %collective-permute-start = (bf16[128,256]{1,0:T(8,128)(2,1)S(1)}, bf16[128,256]{1,0:T(8,128)(2,1)S(1)}, u32[]{:S(2)}, u32[]{:S(2)}) collective-permute-start(bf16[128,256]{1,0:T(8,128)(2,1)S(1)} %get-tuple-element.28.refs_1_), channel_id=1, source_target_pairs={{0,1},{1,0},{2,3},{3,2},{4,5},{5,4},{6,7},{7,6},{8,9},{9,8},{10,11... | collective-permute-start | bytes 196616 | tf_op jit(solution)/shard_map/ppermute | solution.py:258
  14.3 1.7 %collective-permute-start.9 = (f32[128,128]{1,0:T(8,128)S(1)}, f32[128,128]{1,0:T(8,128)S(1)}, u32[]{:S(2)}, u32[]{:S(2)}) collective-permute-start(f32[128,128]{1,0:T(8,128)S(1)} %get-tuple-element.32.refs_15_), channel_id=1, source_target_pairs={{0,1},{1,0},{2,3},{3,2},{4,5},{5,4},{6,7},{7,6},{8,9},{9,8},{10,11... | collective-permute-start | bytes 196616 | tf_op jit(solution)/shard_map/ppermute | solution.py:258
  14.3 1.8 %collective-permute-start.6 = (bf16[128,256]{1,0:T(8,128)(2,1)S(1)}, bf16[128,256]{1,0:T(8,128)(2,1)S(1)}, u32[]{:S(2)}, u32[]{:S(2)}) collective-permute-start(bf16[128,256]{1,0:T(8,128)(2,1)S(1)} %collective-permute-done.5.refs_7_), channel_id=1, source_target_pairs={{0,1},{1,0},{2,3},{3,2},{4,5},{5,4},{6,7},{7,6},{8,9},{9,8},{10,11... | collective-permute-start | bytes 196616 | tf_op jit(solution)/shard_map/ppermute | solution.py:258
  14.9 1.3 %collective-permute-start.4 = (bf16[128,256]{1,0:T(8,128)(2,1)S(1)}, bf16[128,256]{1,0:T(8,128)(2,1)S(1)}, u32[]{:S(2)}, u32[]{:S(2)}) collective-permute-start(bf16[128,256]{1,0:T(8,128)(2,1)S(1)} %collective-permute-done.3.refs_5_), channel_id=1, source_target_pairs={{0,1},{1,0},{2,3},{3,2},{4,5},{5,4},{6,7},{7,6},{8,9},{9,8},{10,11... | collective-permute-start | bytes 196616 | tf_op jit(solution)/shard_map/ppermute | solution.py:258
  14.9 1.3 %collective-permute-start.2 = (bf16[128,256]{1,0:T(8,128)(2,1)S(1)}, bf16[128,256]{1,0:T(8,128)(2,1)S(1)}, u32[]{:S(2)}, u32[]{:S(2)}) collective-permute-start(bf16[128,256]{1,0:T(8,128)(2,1)S(1)} %collective-permute-done.1.refs_3_), channel_id=1, source_target_pairs={{0,1},{1,0},{2,3},{3,2},{4,5},{5,4},{6,7},{7,6},{8,9},{9,8},{10,11... | collective-permute-start | bytes 196616 | tf_op jit(solution)/shard_map/ppermute | solution.py:258
  15.7 0.7 %copy-start.3 = (s32[1,8]{1,0:T(1,128)S(1)}, s32[1,8]{1,0:T(1,128)}, u32[]{:S(2)}) copy-start(s32[1,8]{1,0:T(1,128)} %refs_0_.7) | copy-start | bytes 100
  16.4 21.7 %copy-start = (f32[512,512]{1,0:T(8,128)S(1)}, f32[512,512]{1,0:T(8,128)}, u32[]{:S(2)}) copy-start(f32[512,512]{1,0:T(8,128)} %refs_4_.1) | copy-start | bytes 3145732
  19.1 0.7 %copy-start.4 = (s32[1,256]{1,0:T(1,128)S(1)}, s32[1,256]{1,0:T(1,128)}, u32[]{:S(2)}) copy-start(s32[1,256]{1,0:T(1,128)} %refs_0_.5) | copy-start | bytes 3076
  20.2 7.2 %collective-permute-start.15 = (bf16[256,256]{1,0:T(8,128)(2,1)S(1)}, bf16[256,256]{1,0:T(8,128)(2,1)S(1)}, u32[]{:S(2)}, u32[]{:S(2)}) collective-permute-start(bf16[256,256]{1,0:T(8,128)(2,1)S(1)} %get-tuple-element.45), channel_id=1, source_target_pairs={{0,2},{2,0},{1,3},{3,1},{4,6},{6,4},{5,7},{7,5},{8,10},{10,8},{9,1... | collective-permute-start | bytes 393224 | tf_op jit(solution)/shard_map/ppermute | solution.py:258
  21.8 4.3 %collective-permute-start.12 = (f32[128,128]{1,0:T(8,128)S(1)}, f32[128,128]{1,0:T(8,128)S(1)}, u32[]{:S(2)}, u32[]{:S(2)}) collective-permute-start(f32[128,128]{1,0:T(8,128)S(1)} %get-tuple-element.39), channel_id=1, source_target_pairs={{0,4},{4,0},{8,12},{12,8},{1,5},{5,1},{9,13},{13,9},{2,6},{6,2},{1... | collective-permute-start | bytes 196616 | tf_op jit(solution)/shard_map/ppermute | solution.py:258
  22.6 4.8 %collective-permute-start.10 = (bf16[128,256]{1,0:T(8,128)(2,1)S(1)}, bf16[128,256]{1,0:T(8,128)(2,1)S(1)}, u32[]{:S(2)}, u32[]{:S(2)}) collective-permute-start(bf16[128,256]{1,0:T(8,128)(2,1)S(1)} %get-tuple-element.35), channel_id=1, source_target_pairs={{0,2},{2,0},{1,3},{3,1},{4,6},{6,4},{5,7},{7,5},{8,10},{10,8},{9,1... | collective-permute-start | bytes 196616 | tf_op jit(solution)/shard_map/ppermute | solution.py:258
  26.1 5.9 %collective-permute-start.13 = (f32[128,128]{1,0:T(8,128)S(1)}, f32[128,128]{1,0:T(8,128)S(1)}, u32[]{:S(2)}, u32[]{:S(2)}) collective-permute-start(f32[128,128]{1,0:T(8,128)S(1)} %add.6), channel_id=1, source_target_pairs={{0,8},{4,12},{8,0},{12,4},{1,9},{5,13},{9,1},{13,5},{2,10},{6,14},... | collective-permute-start | bytes 196616 | tf_op jit(solution)/shard_map/ppermute | solution.py:258
  27.4 8.2 %collective-permute-start.11 = (bf16[128,256]{1,0:T(8,128)(2,1)S(1)}, bf16[128,256]{1,0:T(8,128)(2,1)S(1)}, u32[]{:S(2)}, u32[]{:S(2)}) collective-permute-start(bf16[128,256]{1,0:T(8,128)(2,1)S(1)} %collective-permute-done.10.refs_5_), channel_id=1, source_target_pairs={{0,1},{1,0},{2,3},{3,2},{4,5},{5,4},{6,7},{7,6},{8,9},{9,8},{10,11... | collective-permute-start | bytes 196616 | tf_op jit(solution)/shard_map/ppermute | solution.py:258
  27.4 13.3 %collective-permute-start.16 = (bf16[256,256]{1,0:T(8,128)(2,1)S(1)}, bf16[256,256]{1,0:T(8,128)(2,1)S(1)}, u32[]{:S(2)}, u32[]{:S(2)}) collective-permute-start(bf16[256,256]{1,0:T(8,128)(2,1)S(1)} %collective-permute-done.15.refs_3_), channel_id=1, source_target_pairs={{0,1},{1,0},{2,3},{3,2},{4,5},{5,4},{6,7},{7,6},{8,9},{9,8},{10,11... | collective-permute-start | bytes 393224 | tf_op jit(solution)/shard_map/ppermute | solution.py:258
  32.0 5.2 %collective-permute-start.19 = (f32[128,128]{1,0:T(8,128)S(1)}, f32[128,128]{1,0:T(8,128)S(1)}, u32[]{:S(2)}, u32[]{:S(2)}) collective-permute-start(f32[128,128]{1,0:T(8,128)S(1)} %add.7.refs_2_.refs_7_), channel_id=1, source_target_pairs={{0,6},{2,4},{4,2},{6,0},{8,14},{10,12},{12,10},{14,8},{1,7},{3,5},... | collective-permute-start | bytes 196616 | tf_op jit(solution)/shard_map/ppermute | solution.py:258
  32.3 5.0 %collective-permute-start.18 = (f32[128,128]{1,0:T(8,128)S(1)}, f32[128,128]{1,0:T(8,128)S(1)}, u32[]{:S(2)}, u32[]{:S(2)}) collective-permute-start(f32[128,128]{1,0:T(8,128)S(1)} %add.7.refs_2_.refs_7_), channel_id=1, source_target_pairs={{0,2},{2,0},{4,6},{6,4},{8,10},{10,8},{12,14},{14,12},{1,3},{3,1},... | collective-permute-start | bytes 196616 | tf_op jit(solution)/shard_map/ppermute | solution.py:258
  33.8 4.3 %collective-permute-start.17 = (f32[128,128]{1,0:T(8,128)S(1)}, f32[128,128]{1,0:T(8,128)S(1)}, u32[]{:S(2)}, u32[]{:S(2)}) collective-permute-start(f32[128,128]{1,0:T(8,128)S(1)} %add.7.refs_2_.refs_7_), channel_id=1, source_target_pairs={{0,4},{2,6},{4,0},{6,2},{8,12},{10,14},{12,8},{14,10},{1,5},{3,7},... | collective-permute-start | bytes 196616 | tf_op jit(solution)/shard_map/ppermute | solution.py:258
  35.6 4.9 %collective-permute-start.14 = (f32[128,128]{1,0:T(8,128)S(1)}, f32[128,128]{1,0:T(8,128)S(1)}, u32[]{:S(2)}, u32[]{:S(2)}) collective-permute-start(f32[128,128]{1,0:T(8,128)S(1)} %add.7.refs_2_.refs_7_), channel_id=1, source_target_pairs={{0,1},{1,0},{2,3},{3,2},{4,5},{5,4},{6,7},{7,6},{8,9},{9,8},{10,11... | collective-permute-start | bytes 196616 | tf_op jit(solution)/shard_map/ppermute | solution.py:258
  37.2 4.8 %collective-permute-start.22 = (f32[128,128]{1,0:T(8,128)S(1)}, f32[128,128]{1,0:T(8,128)S(1)}, u32[]{:S(2)}, u32[]{:S(2)}) collective-permute-start(f32[128,128]{1,0:T(8,128)S(1)} %collective-permute-done.19.refs_6_), channel_id=1, source_target_pairs={{0,1},{1,0},{2,3},{3,2},{4,5},{5,4},{6,7},{7,6},{8,9},{9,8},{10,11... | collective-permute-start | bytes 196616 | tf_op jit(solution)/shard_map/ppermute | solution.py:258
  37.3 4.8 %collective-permute-start.21 = (f32[128,128]{1,0:T(8,128)S(1)}, f32[128,128]{1,0:T(8,128)S(1)}, u32[]{:S(2)}, u32[]{:S(2)}) collective-permute-start(f32[128,128]{1,0:T(8,128)S(1)} %collective-permute-done.18.refs_5_), channel_id=1, source_target_pairs={{0,1},{1,0},{2,3},{3,2},{4,5},{5,4},{6,7},{7,6},{8,9},{9,8},{10,11... | collective-permute-start | bytes 196616 | tf_op jit(solution)/shard_map/ppermute | solution.py:258
  38.0 4.0 %collective-permute-start.20 = (f32[128,128]{1,0:T(8,128)S(1)}, f32[128,128]{1,0:T(8,128)S(1)}, u32[]{:S(2)}, u32[]{:S(2)}) collective-permute-start(f32[128,128]{1,0:T(8,128)S(1)} %collective-permute-done.17.refs_4_.refs_9_), channel_id=1, source_target_pairs={{0,1},{1,0},{2,3},{3,2},{4,5},{5,4},{6,7},{7,6},{8,9},{9,8},{10,11... | collective-permute-start | bytes 196616 | tf_op jit(solution)/shard_map/ppermute | solution.py:258

commit v4 on v3

v4 whole, which is shorter than its diff:
```python
import math

import jax
import jax.numpy as jnp
from jax import lax
from jax.experimental import pallas as pl
from jax.experimental.pallas import tpu as pltpu
from jax.sharding import PartitionSpec as P

RIDGE_COEF = 50.0
LOG2E = 1.4426950408889634
VMEM_LIMIT = 24 << 20
SLAB_STEP = 512
ROWS_ROWS = (((1,), (1,)), ((), ()))
VMEM = pl.BlockSpec(memory_space=pltpu.VMEM)
SMEM = pl.BlockSpec(memory_space=pltpu.SMEM)


def split(values):
    high = values.astype(jnp.bfloat16)
    return high, (values - high.astype(jnp.float32)).astype(jnp.bfloat16)


def dot(left, right, dims=(((1,), (0,)), ((), ()))):
    return lax.dot_general(left, right, dims, preferred_element_type=jnp.float32)


def dot_parts(left, right, dims=(((1,), (0,)), ((), ()))):
    return dot(left[0], right[0], dims) + (dot(left[0], right[1], dims) + dot(left[1], right[0], dims))


def row_sq(points, scale):
    wide = points.astype(jnp.float32)
    high, low = split(wide * wide)
    ones = jnp.ones((8, points.shape[1]), jnp.bfloat16)
    return (dot(ones, high, ROWS_ROWS) + dot(ones, low, ROWS_ROWS))[:1] * scale


def col_sq(points, scale):
    wide = points.astype(jnp.float32)
    return jnp.sum(wide * wide, axis=1, keepdims=True) * scale


def as_column(row):
    lanes = 128
    square = [
        jnp.transpose(jnp.broadcast_to(row[:, at : at + lanes], (lanes, lanes)))[:, :1]
        for at in range(0, row.shape[1], lanes)
    ]
    return jnp.concatenate(square, axis=0)


def owner_span(counts, owner):
    off = jnp.int32(0)
    count = jnp.int32(0)
    for at in range(counts.shape[1]):
        here = counts[0, at]
        off = off + jnp.where(at < owner, here, 0)
        count = count + jnp.where(at == owner, here, 0)
    return off, count


def one_hot(row_ids, at, step):
    slot = lax.broadcasted_iota(jnp.int32, (row_ids.shape[0], step), 1) + at
    return (row_ids == slot).astype(jnp.float32).astype(jnp.bfloat16)


def own_kernel(
    n_sub, quarter, rows_hbm, points_hbm, counts_hbm,
    own_ref, rows_ref, points_ref, to_ref, counts, rows_sem, points_sem, counts_sem,
):
    total, width = points_ref.shape
    cap = own_ref.shape[0]
    step = math.gcd(total, 256)
    rows_copy = pltpu.make_async_copy(rows_hbm, rows_ref, rows_sem)
    points_copy = pltpu.make_async_copy(points_hbm, points_ref, points_sem)
    counts_copy = pltpu.make_async_copy(counts_hbm, counts, counts_sem)
    rows_copy.start()
    counts_copy.start()
    points_copy.start()
    rows_copy.wait()
    row_ids = as_column(rows_ref[...])
    hots = [one_hot(row_ids, at, step) for at in range(0, total, step)]
    counts_copy.wait()
    pts_at, sub_at = lax.axis_index("pts"), lax.axis_index("sub")
    turn = (sub_at * 2 + pts_at % 2) * quarter
    slot = lax.broadcasted_iota(jnp.int32, (1, cap), 1)
    for rel in range(to_ref.shape[0]):
        off, count = owner_span(counts, (pts_at * n_sub + sub_at) ^ rel)
        to_ref[rel : rel + 1, :] = jnp.where(slot < count, (slot + off) ^ turn, -1)
    points_copy.wait()
    own = jnp.zeros((cap, width), jnp.float32)
    for at, hot in enumerate(hots):
        own = own + dot(hot, points_ref[at * step : (at + 1) * step, :])
    own_ref[...] = own.astype(own_ref.dtype)


def hots_of(to_ref, rels, base, size):
    place = lax.broadcasted_iota(jnp.int32, (size, to_ref.shape[1]), 0) + base
    hots = [(place == to_ref[rel : rel + 1, :]).astype(jnp.float32).astype(jnp.bfloat16) for rel in rels]
    return jnp.concatenate(hots, axis=1)


def prep_kernel(rows_ref, weights_ref, targets_ref, to_ref, shift_ref, turned_ref, place_ref, hots_ref):
    place_ref[...] = one_hot(as_column(to_ref[:1, :]), 0, place_ref.shape[1])
    hots_ref[...] = hots_of(to_ref, range(to_ref.shape[0]), 0, hots_ref.shape[0])
    total = weights_ref.shape[0]
    step = math.gcd(total, 256)
    row_ids = as_column(rows_ref[...])
    alpha = jnp.zeros(shift_ref.shape, jnp.float32)
    for at in range(0, total, step):
        part = weights_ref[at : at + step, :]
        alpha = alpha + dot(one_hot(row_ids, at, step), part)
        turned_ref[:, at : at + step] = jnp.transpose(part.astype(jnp.float32)).astype(jnp.bfloat16)
    shift_ref[...] = RIDGE_COEF * alpha - targets_ref[...].astype(jnp.float32)


def norm_kernel(points_ref, sq_ref):
    sq_ref[...] = jnp.broadcast_to(col_sq(points_ref[...], LOG2E / points_ref.shape[1]), sq_ref.shape)


def three_parts(values):
    high, low = split(values)
    rest = values - high.astype(jnp.float32) - low.astype(jnp.float32)
    return high, low, rest.astype(jnp.bfloat16)


def shift_kernel(to_ref, *refs):
    parts = [three_parts(ref[...]) for ref in refs[:-1]]
    hots = hots_of(to_ref, range(len(parts)), 0, refs[-1].shape[0])
    refs[-1][...] = sum(dot(hots, jnp.concatenate(part, axis=0)) for part in zip(*parts))


def slab_kernel(n_blocks, n_sub, quarter, *refs):
    blocks, refs = refs[:n_blocks], refs[n_blocks:]
    slabs, slab_sqs, slab_ws = refs[:n_sub], refs[n_sub : 2 * n_sub], refs[2 * n_sub : 3 * n_sub]
    hots_ref, sums_ref, keep_ref, send_ref, mine_ref = refs[3 * n_sub :]
    scale = LOG2E / mine_ref.shape[1]
    points = jnp.concatenate([block[...] for block in blocks], axis=0)
    mine_x = dot(hots_ref[...], points).astype(jnp.bfloat16)
    mine_ref[...] = mine_x
    mine_sq = row_sq(mine_x, scale)
    total = jnp.zeros((keep_ref.shape[1], 2 * quarter), jnp.float32)
    step = math.gcd(slabs[0].shape[0], SLAB_STEP)
    for which in range(n_sub):
        for at in range(0, slabs[which].shape[0], step):
            inner = dot(slabs[which][at : at + step, :], mine_x, ROWS_ROWS)
            slab_sq = slab_sqs[which][at : at + step, :]
            slab_sq = jnp.concatenate([slab_sq] * (2 * quarter // slab_sq.shape[1]), axis=1)
            kern = jnp.exp2(inner * (2.0 * scale) - mine_sq - slab_sq)
            high, low = split(kern)
            turned = slab_ws[which][:, at : at + step]
            total = total + dot(turned, high) + dot(turned, low)
    total = jnp.transpose(total) + sums_ref[...]
    keep_ref[...] = total[:quarter]
    send_ref[...] = total[quarter:]


def pick_kernel(n_blocks, quarter, *refs):
    blocks, (to_ref, pick_ref, mine_ref, live_ref, sketch_ref) = refs[:n_blocks], refs[n_blocks:]
    live, half = live_ref.shape[0], mine_ref.shape[0]
    points = jnp.concatenate([block[...] for block in blocks], axis=0)
    live_ref[:half, :] = mine_ref[...]
    for base in range(half, live, half):
        hots = hots_of(to_ref, range(n_blocks), base, half)
        live_ref[base : base + half, :] = dot(hots, points).astype(jnp.bfloat16)
    turn = (lax.axis_index("sub") * 2 + lax.axis_index("pts") % 2) * quarter
    hot = one_hot(as_column(pick_ref[...] ^ turn), 0, live)
    sketch_ref[...] = dot(hot, live_ref[...]).astype(sketch_ref.dtype)


def sketch_rows(rows, points):
    scale = LOG2E / rows.shape[1]
    inner = dot(rows, points, ROWS_ROWS)
    return jnp.exp2(inner * (2.0 * scale) - col_sq(rows, scale) - row_sq(points, scale))


def write_groups(total, quarter, order, groups, outs):
    high, low = split(total)
    for at, group in enumerate(groups):
        for where, key in enumerate(group):
            base = order.index(key) * quarter
            outs[2 * at][:, where * quarter : (where + 1) * quarter] = high[:, base : base + quarter]
            outs[2 * at + 1][:, where * quarter : (where + 1) * quarter] = low[:, base : base + quarter]


def near_gram_kernel(n_sub, n_col, quarter, groups, *refs):
    own_ref, live_ref, to_ref, core_ref = refs[:4]
    sketches, refs = refs[4 : 4 + n_col], refs[4 + n_col :]
    mixed_high, mixed_low, outs = refs[0], refs[1], refs[2:]
    picks = sketches[0].shape[0]
    points = jnp.concatenate([ref[...] for ref in sketches], axis=0)
    used = as_column(to_ref[:1, :]) >= 0
    own = split(jnp.where(used, sketch_rows(own_ref[...], points), 0.0))
    col_at = lax.axis_index("col")
    tiles = [pl.ds(pl.multiple_of((col_at ^ col) * picks, picks), picks) for col in range(n_col)]
    core = [jnp.concatenate([core_ref[row, col] for col in tiles], axis=1) for row in tiles]
    mixed = split(dot_parts(own, split(jnp.concatenate(core, axis=0))))
    mixed_high[...], mixed_low[...] = mixed
    total = dot_parts(mixed, split(sketch_rows(live_ref[...], points)), ROWS_ROWS)
    order = [(0, pts, sub) for sub in range(n_sub) for pts in range(2)]
    write_groups(total, quarter, order, groups, outs)


def far_gram_kernel(n_sub, n_col, quarter, groups, *refs):
    mixed = refs[0][...], refs[1][...]
    sketches, refs = refs[2 : 2 + n_col], refs[2 + n_col :]
    got, outs = refs[: -2 * len(groups)], refs[-2 * len(groups) :]
    points = jnp.concatenate([ref[...] for ref in sketches], axis=0)
    rows = jnp.concatenate([ref[...] for ref in got], axis=0)
    total = dot_parts(mixed, split(sketch_rows(rows, points)), ROWS_ROWS)
    order = [(col, pts, sub) for col in range(1, n_col) for sub in range(n_sub) for pts in range(2)]
    write_groups(total, quarter, order, groups, outs)


def apply_grams(grams, parts):
    total, at = None, 0
    for high, low in grams:
        many = high.shape[1] // parts[0].shape[0]
        right = split(jnp.concatenate([ref[...] for ref in parts[at : at + many]], axis=0))
        term = dot_parts((high[...], low[...]), right)
        total = term if total is None else total + term
        at += many
    return total


def part_kernel(n_grams, *refs):
    grams = [refs[2 * at : 2 * at + 2] for at in range(n_grams)]
    refs[-1][...] = apply_grams(grams, refs[2 * n_grams : -1])


def tile_kernel(place_ref, *refs):
    rows = jnp.concatenate([ref[...] for ref in refs[:-1]], axis=0)
    refs[-1][...] = sum(dot(place_ref[...], part) for part in three_parts(rows))


def last_kernel(n_early, n_grams, *refs):
    early, refs = refs[: n_early + 1], refs[n_early + 1 :]
    grams, refs = [refs[2 * at : 2 * at + 2] for at in range(n_grams)], refs[2 * n_grams :]
    later, grad_ref, out_ref = refs[:-2], refs[-2], refs[-1]
    grad = early[0][...]
    grad_ref[...] = grad
    for ref in early[1:]:
        grad = grad - ref[...]
    out_ref[...] = grad - apply_grams(grams, later)


def make_device(mesh):
    n_pts, n_col, n_sub = mesh.shape["pts"], mesh.shape["col"], mesh.shape["sub"]

    def hop(values, axis, step):
        axes = axis if isinstance(axis, tuple) else (axis,)
        size = math.prod(mesh.shape[name] for name in axes)
        return lax.ppermute(values, axis, [(j, j ^ step) for j in range(size)])

    def near_of(values):
        return [values] + [hop(values, "sub", i) for i in range(1, n_sub)]

    def call(kernel, out_shape, smem, arrays, scratch=(), space=VMEM):
        return pl.pallas_call(
            kernel,
            out_shape=out_shape,
            in_specs=[SMEM] * len(smem) + [space] * len(arrays),
            out_specs=jax.tree.map(lambda _: VMEM, out_shape),
            scratch_shapes=list(scratch),
            compiler_params=pltpu.CompilerParams(vmem_limit_bytes=VMEM_LIMIT),
        )(*smem, *arrays)

    def per_device(points, weights, tile_rows, tile_count, sketch_pick, block_targets, core_inv):
        return body(points, weights, tile_rows, tile_count, sketch_pick, block_targets, core_inv)

    def body(points, weights, tile_rows, tile_count, sketch_pick, block_targets, core_inv):
        cap = tile_rows.shape[2]
        width, outs = points.shape[1], weights.shape[1]
        owners = tile_count.shape[1]
        live = owners * cap // 2
        quarter = live // n_sub // 2
        picks = sketch_pick.shape[1]

        def f32(*shape):
            return jax.ShapeDtypeStruct(shape, jnp.float32)

        def bf16(*shape):
            return jax.ShapeDtypeStruct(shape, jnp.bfloat16)

        own_x, row_ids, points, places = call(
            lambda *refs: own_kernel(n_sub, quarter, *refs),
            (
                bf16(cap, width),
                jax.ShapeDtypeStruct((1, cap), jnp.int32),
                bf16(*points.shape),
                jax.ShapeDtypeStruct((owners, cap), jnp.int32),
            ),
            (),
            tuple(
                pltpu.with_memory_space_constraint(value, pltpu.MemorySpace.HBM)
                for value in (tile_rows[0], points, tile_count)
            ),
            (pltpu.SMEM(tile_count.shape, jnp.int32), *(pltpu.SemaphoreType.DMA(()),) * 3),
            pl.BlockSpec(memory_space=pltpu.MemorySpace.HBM),
        )
        far = [own_x] + [hop(own_x, "pts", i) for i in range(1, n_pts)]
        slabs = near_of(points)
        shift, turned, own_place, hots = call(
            prep_kernel,
            (
                f32(cap, outs), bf16(outs, points.shape[0]),
                bf16(cap, live), bf16(2 * quarter, owners * cap),
            ),
            (),
            (row_ids, weights, block_targets[0], places),
        )
        slab_ws = near_of(turned)
        sums = call(shift_kernel, f32(2 * quarter, outs), (), (places, *near_of(shift)))
        slab_sqs = [call(norm_kernel, f32(points.shape[0], 128), (), (slab,)) for slab in slabs]
        blocks = []
        for block in far:
            blocks += near_of(block)
        part, send, mine_x = call(
            lambda *refs: slab_kernel(owners, n_sub, quarter, *refs),
            (f32(quarter, outs), f32(quarter, outs), bf16(2 * quarter, width)),
            (),
            (*blocks, *slabs, *slab_sqs, *slab_ws, hots, sums),
        )

        part = part + hop(send, "pts", 1)
        step = 2
        while step < n_pts:
            part = part + hop(part, "pts", step)
            step *= 2

        live_x, sketch = call(
            lambda *refs: pick_kernel(owners, quarter, *refs),
            (bf16(live, width), bf16(picks, width)),
            (),
            (*blocks, places, sketch_pick, mine_x),
        )
        got_sketch = [hop(sketch, "col", i) for i in range(1, n_col)]
        got_rows = []
        for i in range(1, n_col):
            got_rows += near_of(hop(mine_x, "col", i))

        def gram_shapes(groups):
            return tuple(bf16(cap, quarter * len(group)) for group in groups for _ in range(2))

        away = [(col, pts) for col in range(1, n_col) for pts in range(2)]
        near_groups = [
            [(0, 0, sub) for sub in range(n_sub)],
            [(0, 1, 0)],
            [(0, 1, sub) for sub in range(1, n_sub)],
        ]
        far_groups = [
            [(col, pts, 0) for col, pts in away],
            [(col, pts, sub) for col, pts in away for sub in range(1, n_sub)],
        ]
        near_grams = call(
            lambda *refs: near_gram_kernel(n_sub, n_col, quarter, near_groups, *refs),
            (*(bf16(cap, n_col * picks),) * 2, *gram_shapes(near_groups)),
            (),
            (own_x, live_x, places, core_inv, sketch, *got_sketch),
        )
        mixed, near_grams = near_grams[:2], near_grams[2:]
        far_grams = call(
            lambda *refs: far_gram_kernel(n_sub, n_col, quarter, far_groups, *refs),
            gram_shapes(far_groups),
            (),
            (*mixed, sketch, *got_sketch, *got_rows),
        )
        grads = {}
        for sub, value in enumerate(near_of(part)):
            grads[0, 0, sub] = value
        for col, pts in [*reversed(away), (0, 1)]:
            other = hop(part, ("pts", "col"), pts * n_col + col)
            for sub, value in enumerate(near_of(other)):
                grads[col, pts, sub] = value

        def data(*groups):
            return [grads[key] for group in groups for key in group]

        early = [
            call(lambda *refs: part_kernel(1, *refs), f32(cap, outs), (),
                 (*near_grams[:2], *data(near_groups[0]))),
            call(lambda *refs: part_kernel(2, *refs), f32(cap, outs), (),
                 (*near_grams[2:4], *far_grams[:2], *data(near_groups[1], far_groups[0]))),
        ]
        grad = call(
            tile_kernel, f32(cap, outs), (),
            (own_place, *[grads[0, pts, sub] for sub in range(n_sub) for pts in range(2)]),
        )
        block_grad, direction = call(
            lambda *refs: last_kernel(len(early), 2, *refs),
            (f32(cap, outs), f32(cap, outs)),
            (),
            (grad, *early, *near_grams[4:], *far_grams[2:], *data(near_groups[2], far_groups[1])),
        )
        return (block_grad[None], direction[None])

    return per_device


def solution(mesh):
    in_specs = (
        P(("grp", "pts", "sub"), None),
        P(("grp", "pts", "sub"), None),
        P(("grp", "col"), ("pts", "sub"), None),
        P(("grp", "col"), None),
        P(("grp", "col"), None),
        P(("grp", "col"), ("pts", "sub"), None),
        P("grp", None),
    )
    out_specs = (P(("grp", "col"), ("pts", "sub"), None), P(("grp", "col"), ("pts", "sub"), None))
    return jax.shard_map(
        make_device(mesh), mesh=mesh, in_specs=in_specs, out_specs=out_specs, check_vma=False
    )
```

time: 43.7 us -> 41.2 us (0.943)
  Pallas kernels: 11.3 us -> 10 us
  starting transfers between devices: 16.2 us -> 15.2 us
  local copies, waits for them, and re-layouts: 0.79 us -> 0.02 us
  waiting for transfers between devices: 14.4 us -> 15 us
    pallas_call x11 -> x13, Pallas kernels: 11.3 us -> 10 us  [call(): pl.pallas_call(kernel, out_shape=out_shape, in_specs=[SMEM] * len(smem) +...]
    ppermute x23 -> x22, starting transfers between devices: 16.2 us -> 15.2 us  [hop(): return lax.ppermute(values, axis, [(j, j ^ step) for j in range(size)])]
    unnamed x10 -> x8, local copies, waits for them, and re-layouts: 0.79 us -> 0.02 us
    ppermute x23 -> x22, waiting for transfers between devices: 14.4 us -> 15 us  [hop(): return lax.ppermute(values, axis, [(j, j ^ step) for j in range(size)])]
  transfers between devices with their start and end apart: 23 -> 22, of which waited for: 7 -> 7; matrix products, arithmetic and copies ran while one was open for 0% -> 0% of each run, Pallas kernels for 12% -> 13%
where the time goes in v4:
time: 41.2 us; the launch traced here: 41 us
  starting transfers between devices  15.2 us (37%)
  waiting for transfers between devices  15 us (36%)
  Pallas kernels  10 us (24%)
  between operations  0.85 us (2%)
    ppermute x22, starting transfers between devices, hop(): return lax.ppermute(values, axis, [(j, j ^ step) for j in range(size)])  15.2 us
    ppermute x22, waiting for transfers between devices, hop(): return lax.ppermute(values, axis, [(j, j ^ step) for j in range(size)])  15 us
    pallas_call x13, Pallas kernels, call(): pl.pallas_call(kernel, out_shape=out_shape, in_specs=[SMEM] * len(smem) +...  10 us
  transfers between devices with their start and end apart: 22, of which 7 were waited for; matrix products, arithmetic and copies ran while one was open for 0% of the time, Pallas kernels for 13%

profile of v4, /device:TPU:0, one launch (start us, length us, event | category | flops | bytes accessed | tf_op | source)
XLA Modules:
  0.0 41.0 jit_solution(14360339833124921809)
XLA Ops:
  0.7 1.6 %shard_map.86 = (bf16[128,256]{1,0:T(8,128)(2,1)S(1)}, s32[1,128]{1,0:T(1,128)S(1)}, bf16[2048,256]{1,0:T(8,128)(2,1)S(1)}, s32[8,128]{1,0:T(8,128)S(1)}) custom-call(s32[1,128]{1,0:T(1,128)} %bitcast.5, bf16[2048,256]{1,0:T(8,128)(2,1)} %refs_1_.1, s32[1,8]{1,0:T(1,128)} %refs_2_.1), custom_call_target="tpu_custom_call" | custom-call | tf_op jit(solution)/shard_map/pallas_call | solution.py:260
  2.3 0.6 %collective-permute-start.7 = (bf16[2048,256]{1,0:T(8,128)(2,1)S(1)}, bf16[2048,256]{1,0:T(8,128)(2,1)S(1)}, u32[]{:S(2)}, u32[]{:S(2)}) collective-permute-start(bf16[2048,256]{1,0:T(8,128)(2,1)S(1)} %get-tuple-element.33.points_ref.refs_8_), channel_id=1, source_target_pairs={{0,1},{1,0},{2,3},{3,2},{4,5},{5,4},{6,7},{7,6},{8,9},{9,8},{10,11... | collective-permute-start | bytes 3145736 | tf_op jit(solution)/shard_map/ppermute | solution.py:254
  2.9 0.6 %shard_map.87 = (f32[128,128]{1,0:T(8,128)S(1)}, bf16[128,2048]{1,0:T(8,128)(2,1)S(1)}, bf16[128,512]{1,0:T(8,128)(2,1)S(1)}, bf16[256,1024]{1,0:T(8,128)(2,1)S(1)}) custom-call(s32[1,128]{1,0:T(1,128)S(1)} %get-tuple-element.29.rows_ref, bf16[2048,128]{1,0:T(8,128)(2,1)S(1)} %copy-done.1, bf16[128,128]{1,0:T(8,128)(2,1)S(1)} %bitcast.4, ...), custom_call_target="tpu_custom_call" | custom-call | tf_op jit(solution)/shard_map/pallas_call | solution.py:260
  3.4 0.1 collective-permute-start.8
  3.5 5.1 %collective-permute-start.5 = (bf16[128,256]{1,0:T(8,128)(2,1)S(1)}, bf16[128,256]{1,0:T(8,128)(2,1)S(1)}, u32[]{:S(2)}, u32[]{:S(2)}) collective-permute-start(bf16[128,256]{1,0:T(8,128)(2,1)S(1)} %get-tuple-element.32.refs_0_), channel_id=1, source_target_pairs={{0,12},{4,8},{8,4},{12,0},{1,13},{5,9},{9,5},{13,1},{2,14},{6,10},... | collective-permute-start | bytes 196616 | tf_op jit(solution)/shard_map/ppermute | solution.py:254
  8.6 0.6 %collective-permute-start.1 = (bf16[128,256]{1,0:T(8,128)(2,1)S(1)}, bf16[128,256]{1,0:T(8,128)(2,1)S(1)}, u32[]{:S(2)}, u32[]{:S(2)}) collective-permute-start(bf16[128,256]{1,0:T(8,128)(2,1)S(1)} %get-tuple-element.32.refs_0_), channel_id=1, source_target_pairs={{0,4},{4,0},{8,12},{12,8},{1,5},{5,1},{9,13},{13,9},{2,6},{6,2},{1... | collective-permute-start | bytes 196616 | tf_op jit(solution)/shard_map/ppermute | solution.py:254
  9.2 2.0 %collective-permute-done.5.refs_6_ = bf16[128,256]{1,0:T(8,128)(2,1)S(1)} collective-permute-done((bf16[128,256]{1,0:T(8,128)(2,1)S(1)}, bf16[128,256]{1,0:T(8,128)(2,1)S(1)}, u32[]{:S(2)}, u32[]{:S(2)}) %collective-permute-start.5) | collective-permute-done | bytes 65568 | tf_op jit(solution)/shard_map/ppermute | solution.py:254
  11.1 3.3 %collective-permute-done.3.refs_4_ = bf16[128,256]{1,0:T(8,128)(2,1)S(1)} collective-permute-done((bf16[128,256]{1,0:T(8,128)(2,1)S(1)}, bf16[128,256]{1,0:T(8,128)(2,1)S(1)}, u32[]{:S(2)}, u32[]{:S(2)}) %collective-permute-start.3) | collective-permute-done | bytes 65568 | tf_op jit(solution)/shard_map/ppermute | solution.py:254
  14.4 0.0 collective-permute-start
  14.4 0.0 collective-permute-done.1.refs_2_
  14.4 0.5 %collective-permute-start.6 = (bf16[128,256]{1,0:T(8,128)(2,1)S(1)}, bf16[128,256]{1,0:T(8,128)(2,1)S(1)}, u32[]{:S(2)}, u32[]{:S(2)}) collective-permute-start(bf16[128,256]{1,0:T(8,128)(2,1)S(1)} %collective-permute-done.5.refs_6_), channel_id=1, source_target_pairs={{0,1},{1,0},{2,3},{3,2},{4,5},{5,4},{6,7},{7,6},{8,9},{9,8},{10,11... | collective-permute-start | bytes 196616 | tf_op jit(solution)/shard_map/ppermute | solution.py:254
  15.0 0.1 collective-permute-start.4
  15.0 0.0 collective-permute-done.7.points_ref.refs_9_
  15.0 0.4 %collective-permute-start.2 = (bf16[128,256]{1,0:T(8,128)(2,1)S(1)}, bf16[128,256]{1,0:T(8,128)(2,1)S(1)}, u32[]{:S(2)}, u32[]{:S(2)}) collective-permute-start(bf16[128,256]{1,0:T(8,128)(2,1)S(1)} %collective-permute-done.1.refs_2_), channel_id=1, source_target_pairs={{0,1},{1,0},{2,3},{3,2},{4,5},{5,4},{6,7},{7,6},{8,9},{9,8},{10,11... | collective-permute-start | bytes 196616 | tf_op jit(solution)/shard_map/ppermute | solution.py:254
  15.5 0.3 shard_map.88.refs_10_
  15.8 0.3 shard_map.90.refs_15_
  16.1 0.3 shard_map.89.refs_11_
  16.4 0.0 collective-permute-done.refs_1_
  16.4 0.0 collective-permute-done.6.refs_7_
  16.5 0.0 collective-permute-done.2.refs_3_
  16.5 0.0 collective-permute-done.8.refs_13_
  16.5 0.0 copy-start.3
  16.5 2.1 %shard_map.91 = (f32[128,128]{1,0:T(8,128)S(1)}, f32[128,128]{1,0:T(8,128)S(1)}, bf16[256,256]{1,0:T(8,128)(2,1)S(1)}) custom-call(bf16[128,256]{1,0:T(8,128)(2,1)S(1)} %get-tuple-element.32.refs_0_, bf16[128,256]{1,0:T(8,128)(2,1)S(1)} %collective-permute-done.refs_1_, bf16[128,256]{1,0:T(8,128)(2,1)S(1)} %collective-permute-done.1.refs_2_, ...), custom_call_target="tpu_custom_call" | custom-call | tf_op jit(solution)/shard_map/pallas_call | solution.py:260
  18.6 0.0 copy-start
  18.6 1.6 %collective-permute-start.16 = (bf16[256,256]{1,0:T(8,128)(2,1)S(1)}, bf16[256,256]{1,0:T(8,128)(2,1)S(1)}, u32[]{:S(2)}, u32[]{:S(2)}) collective-permute-start(bf16[256,256]{1,0:T(8,128)(2,1)S(1)} %get-tuple-element.39.refs_10_), channel_id=1, source_target_pairs={{0,2},{2,0},{1,3},{3,1},{4,6},{6,4},{5,7},{7,5},{8,10},{10,8},{9,1... | collective-permute-start | bytes 393224 | tf_op jit(solution)/shard_map/ppermute | solution.py:254
  20.1 0.8 %collective-permute-start.10 = (f32[128,128]{1,0:T(8,128)S(1)}, f32[128,128]{1,0:T(8,128)S(1)}, u32[]{:S(2)}, u32[]{:S(2)}) collective-permute-start(f32[128,128]{1,0:T(8,128)S(1)} %get-tuple-element.38), channel_id=1, source_target_pairs={{0,4},{4,0},{8,12},{12,8},{1,5},{5,1},{9,13},{13,9},{2,6},{6,2},{1... | collective-permute-start | bytes 196616 | tf_op jit(solution)/shard_map/ppermute | solution.py:254
  20.9 0.5 %shard_map.93 = (bf16[512,256]{1,0:T(8,128)(2,1)S(1)}, bf16[256,256]{1,0:T(8,128)(2,1)S(1)}) custom-call(bf16[128,256]{1,0:T(8,128)(2,1)S(1)} %get-tuple-element.32.refs_0_, bf16[128,256]{1,0:T(8,128)(2,1)S(1)} %collective-permute-done.refs_1_, bf16[128,256]{1,0:T(8,128)(2,1)S(1)} %collective-permute-done.1.refs_2_, ...), custom_call_target="tpu_custom_call" | custom-call | tf_op jit(solution)/shard_map/pallas_call | solution.py:260
  21.5 0.6 %collective-permute-start.15 = (bf16[256,256]{1,0:T(8,128)(2,1)S(1)}, bf16[256,256]{1,0:T(8,128)(2,1)S(1)}, u32[]{:S(2)}, u32[]{:S(2)}) collective-permute-start(bf16[256,256]{1,0:T(8,128)(2,1)S(1)} %get-tuple-element.41.refs_4_.refs_2_), channel_id=1, source_target_pairs={{0,2},{2,0},{1,3},{3,1},{4,6},{6,4},{5,7},{7,5},{8,10},{10,8},{9,1... | collective-permute-start | bytes 393224 | tf_op jit(solution)/shard_map/ppermute | solution.py:254
  22.1 2.3 %collective-permute-done.10 = f32[128,128]{1,0:T(8,128)S(1)} collective-permute-done((f32[128,128]{1,0:T(8,128)S(1)}, f32[128,128]{1,0:T(8,128)S(1)}, u32[]{:S(2)}, u32[]{:S(2)}) %collective-permute-start.10) | collective-permute-done | bytes 65568 | tf_op jit(solution)/shard_map/ppermute | solution.py:254
  24.4 1.3 %collective-permute-start.11 = (f32[128,128]{1,0:T(8,128)S(1)}, f32[128,128]{1,0:T(8,128)S(1)}, u32[]{:S(2)}, u32[]{:S(2)}) collective-permute-start(f32[128,128]{1,0:T(8,128)S(1)} %add.6), channel_id=1, source_target_pairs={{0,8},{4,12},{8,0},{12,4},{1,9},{5,13},{9,1},{13,5},{2,10},{6,14},... | collective-permute-start | bytes 196616 | tf_op jit(solution)/shard_map/ppermute | solution.py:254
  25.8 0.0 collective-permute-done.16.refs_4_
  25.8 0.0 collective-permute-start.17
  25.8 4.6 %collective-permute-done.11 = f32[128,128]{1,0:T(8,128)S(1)} collective-permute-done((f32[128,128]{1,0:T(8,128)S(1)}, f32[128,128]{1,0:T(8,128)S(1)}, u32[]{:S(2)}, u32[]{:S(2)}) %collective-permute-start.11) | collective-permute-done | bytes 65568 | tf_op jit(solution)/shard_map/ppermute | solution.py:254
  30.4 0.3 collective-permute-start.12
  30.6 1.8 %collective-permute-start.19 = (f32[128,128]{1,0:T(8,128)S(1)}, f32[128,128]{1,0:T(8,128)S(1)}, u32[]{:S(2)}, u32[]{:S(2)}) collective-permute-start(f32[128,128]{1,0:T(8,128)S(1)} %add.7.refs_0_.refs_2_), channel_id=1, source_target_pairs={{0,6},{2,4},{4,2},{6,0},{8,14},{10,12},{12,10},{14,8},{1,7},{3,5},... | collective-permute-start | bytes 196616 | tf_op jit(solution)/shard_map/ppermute | solution.py:254
  32.4 1.5 %collective-permute-start.18 = (f32[128,128]{1,0:T(8,128)S(1)}, f32[128,128]{1,0:T(8,128)S(1)}, u32[]{:S(2)}, u32[]{:S(2)}) collective-permute-start(f32[128,128]{1,0:T(8,128)S(1)} %add.7.refs_0_.refs_2_), channel_id=1, source_target_pairs={{0,2},{2,0},{4,6},{6,4},{8,10},{10,8},{12,14},{14,12},{1,3},{3,1},... | collective-permute-start | bytes 196616 | tf_op jit(solution)/shard_map/ppermute | solution.py:254
  33.9 0.0 collective-permute-done.15.refs_5_.refs_3_
  33.9 0.0 collective-permute-start.13
  33.9 0.8 %collective-permute-done.12.refs_1_.refs_4_ = f32[128,128]{1,0:T(8,128)S(1)} collective-permute-done((f32[128,128]{1,0:T(8,128)S(1)}, f32[128,128]{1,0:T(8,128)S(1)}, u32[]{:S(2)}, u32[]{:S(2)}) %collective-permute-start.12) | collective-permute-done | bytes 65568 | tf_op jit(solution)/shard_map/ppermute | solution.py:254
  34.7 1.1 %collective-permute-done.19.refs_6_ = f32[128,128]{1,0:T(8,128)S(1)} collective-permute-done((f32[128,128]{1,0:T(8,128)S(1)}, f32[128,128]{1,0:T(8,128)S(1)}, u32[]{:S(2)}, u32[]{:S(2)}) %collective-permute-start.19) | collective-permute-done | bytes 65568 | tf_op jit(solution)/shard_map/ppermute | solution.py:254
  35.8 0.0 collective-permute-start.21
  35.8 0.9 %collective-permute-done.18.refs_5_ = f32[128,128]{1,0:T(8,128)S(1)} collective-permute-done((f32[128,128]{1,0:T(8,128)S(1)}, f32[128,128]{1,0:T(8,128)S(1)}, u32[]{:S(2)}, u32[]{:S(2)}) %collective-permute-start.18) | collective-permute-done | bytes 65568 | tf_op jit(solution)/shard_map/ppermute | solution.py:254
  36.7 1.6 %shard_map.94 = (bf16[128,512]{1,0:T(8,128)(2,1)S(1)}, bf16[128,512]{1,0:T(8,128)(2,1)S(1)}, bf16[128,256]{1,0:T(8,128)(2,1)S(1)}, bf16[128,256]{1,0:T(8,128)(2,...) custom-call(bf16[128,256]{1,0:T(8,128)(2,1)S(1)} %get-tuple-element., ...), custom_call_target="tpu_custom_call" | custom-call | tf_op jit(solution)/shard_map/pallas_call | solution.py:260
  38.3 0.2 shard_map.95.refs_1_
  38.5 1.1 %shard_map.96 = (bf16[128,256]{1,0:T(8,128)(2,1)S(1)}, bf16[128,256]{1,0:T(8,128)(2,1)S(1)}, bf16[128,256]{1,0:T(8,128)(2,1)S(1)}, bf16[128,256]{1,0:T(8,128)(2,1)S(1)}) custom-call(bf16[128,512]{1,0:T(8,128)(2,1)S(1)} %get-tuple-element.46.refs_0_, bf16[128,512]{1,0:T(8,128)(2,1)S(1)} %get-tuple-element.47.refs_1_, ...), custom_call_target="tpu_custom_call" | custom-call | tf_op jit(solution)/shard_map/pallas_call | solution.py:260
  39.6 0.2 shard_map.97.refs_2_
  39.9 0.3 shard_map.92.refs_0_
  40.2 0.9 %shard_map.98 = (f32[128,128]{1,0:T(8,128)}, f32[128,128]{1,0:T(8,128)}) custom-call(f32[128,128]{1,0:T(8,128)S(1)} %shard_map.92.refs_0_, f32[128,128]{1,0:T(8,128)S(1)} %shard_map.95.refs_1_, f32[128,128]{1,0:T(8,128)S(1)} %shard_map.97.refs_2_, bf16[128,128]{1,0:T(8,128)(2,1)S(1)} %get-tuple-element.50.refs_3_, ...), custom_call_target="tpu_custom_call" | custom-call | tf_op jit(solution)/shard_map/pallas_call | solution.py:260
  (19 shorter events, 0.1 us)
Async XLA Ops:
  0.6 2.2 %copy-start.1 = (bf16[2048,128]{1,0:T(8,128)(2,1)S(1)}, bf16[2048,128]{1,0:T(8,128)(2,1)}, u32[]{:S(2)}) copy-start(bf16[2048,128]{1,0:T(8,128)(2,1)} %weights_ref.1) | copy-start | bytes 1572868
  0.6 2.2 %copy-start.2 = (bf16[1,128,128]{2,1,0:T(8,128)(2,1)S(1)}, bf16[1,128,128]{2,1,0:T(8,128)(2,1)}, u32[]{:S(2)}) copy-start(bf16[1,128,128]{2,1,0:T(8,128)(2,1)} %param.12) | copy-start | bytes 98308
  2.3 12.7 %collective-permute-start.7 = (bf16[2048,256]{1,0:T(8,128)(2,1)S(1)}, bf16[2048,256]{1,0:T(8,128)(2,1)S(1)}, u32[]{:S(2)}, u32[]{:S(2)}) collective-permute-start(bf16[2048,256]{1,0:T(8,128)(2,1)S(1)} %get-tuple-element.33.points_ref.refs_8_), channel_id=1, source_target_pairs={{0,1},{1,0},{2,3},{3,2},{4,5},{5,4},{6,7},{7,6},{8,9},{9,8},{10,11... | collective-permute-start | bytes 3145736 | tf_op jit(solution)/shard_map/ppermute | solution.py:254
  3.4 13.0 %collective-permute-start.8 = (bf16[128,2048]{1,0:T(8,128)(2,1)S(1)}, bf16[128,2048]{1,0:T(8,128)(2,1)S(1)}, u32[]{:S(2)}, u32[]{:S(2)}) collective-permute-start(bf16[128,2048]{1,0:T(8,128)(2,1)S(1)} %get-tuple-element.34.refs_12_), channel_id=1, source_target_pairs={{0,1},{1,0},{2,3},{3,2},{4,5},{5,4},{6,7},{7,6},{8,9},{9,8},{10,11... | collective-permute-start | bytes 1572872 | tf_op jit(solution)/shard_map/ppermute | solution.py:254
  3.5 7.6 %collective-permute-start.5 = (bf16[128,256]{1,0:T(8,128)(2,1)S(1)}, bf16[128,256]{1,0:T(8,128)(2,1)S(1)}, u32[]{:S(2)}, u32[]{:S(2)}) collective-permute-start(bf16[128,256]{1,0:T(8,128)(2,1)S(1)} %get-tuple-element.32.refs_0_), channel_id=1, source_target_pairs={{0,12},{4,8},{8,4},{12,0},{1,13},{5,9},{9,5},{13,1},{2,14},{6,10},... | collective-permute-start | bytes 196616 | tf_op jit(solution)/shard_map/ppermute | solution.py:254
  8.6 5.8 %collective-permute-start.3 = (bf16[128,256]{1,0:T(8,128)(2,1)S(1)}, bf16[128,256]{1,0:T(8,128)(2,1)S(1)}, u32[]{:S(2)}, u32[]{:S(2)}) collective-permute-start(bf16[128,256]{1,0:T(8,128)(2,1)S(1)} %get-tuple-element.32.refs_0_), channel_id=1, source_target_pairs={{0,8},{4,12},{8,0},{12,4},{1,9},{5,13},{9,1},{13,5},{2,10},{6,14},... | collective-permute-start | bytes 196616 | tf_op jit(solution)/shard_map/ppermute | solution.py:254
  8.6 5.8 %collective-permute-start.1 = (bf16[128,256]{1,0:T(8,128)(2,1)S(1)}, bf16[128,256]{1,0:T(8,128)(2,1)S(1)}, u32[]{:S(2)}, u32[]{:S(2)}) collective-permute-start(bf16[128,256]{1,0:T(8,128)(2,1)S(1)} %get-tuple-element.32.refs_0_), channel_id=1, source_target_pairs={{0,4},{4,0},{8,12},{12,8},{1,5},{5,1},{9,13},{13,9},{2,6},{6,2},{1... | collective-permute-start | bytes 196616 | tf_op jit(solution)/shard_map/ppermute | solution.py:254
  11.1 3.8 %collective-permute-start.9 = (f32[128,128]{1,0:T(8,128)S(1)}, f32[128,128]{1,0:T(8,128)S(1)}, u32[]{:S(2)}, u32[]{:S(2)}) collective-permute-start(f32[128,128]{1,0:T(8,128)S(1)} %get-tuple-element.36.refs_0_), channel_id=1, source_target_pairs={{0,1},{1,0},{2,3},{3,2},{4,5},{5,4},{6,7},{7,6},{8,9},{9,8},{10,11... | collective-permute-start | bytes 196616 | tf_op jit(solution)/shard_map/ppermute | solution.py:254
  14.4 2.0 %collective-permute-start = (bf16[128,256]{1,0:T(8,128)(2,1)S(1)}, bf16[128,256]{1,0:T(8,128)(2,1)S(1)}, u32[]{:S(2)}, u32[]{:S(2)}) collective-permute-start(bf16[128,256]{1,0:T(8,128)(2,1)S(1)} %get-tuple-element.32.refs_0_), channel_id=1, source_target_pairs={{0,1},{1,0},{2,3},{3,2},{4,5},{5,4},{6,7},{7,6},{8,9},{9,8},{10,11... | collective-permute-start | bytes 196616 | tf_op jit(solution)/shard_map/ppermute | solution.py:254
  14.4 2.0 %collective-permute-start.6 = (bf16[128,256]{1,0:T(8,128)(2,1)S(1)}, bf16[128,256]{1,0:T(8,128)(2,1)S(1)}, u32[]{:S(2)}, u32[]{:S(2)}) collective-permute-start(bf16[128,256]{1,0:T(8,128)(2,1)S(1)} %collective-permute-done.5.refs_6_), channel_id=1, source_target_pairs={{0,1},{1,0},{2,3},{3,2},{4,5},{5,4},{6,7},{7,6},{8,9},{9,8},{10,11... | collective-permute-start | bytes 196616 | tf_op jit(solution)/shard_map/ppermute | solution.py:254
  15.0 1.5 %collective-permute-start.4 = (bf16[128,256]{1,0:T(8,128)(2,1)S(1)}, bf16[128,256]{1,0:T(8,128)(2,1)S(1)}, u32[]{:S(2)}, u32[]{:S(2)}) collective-permute-start(bf16[128,256]{1,0:T(8,128)(2,1)S(1)} %collective-permute-done.3.refs_4_), channel_id=1, source_target_pairs={{0,1},{1,0},{2,3},{3,2},{4,5},{5,4},{6,7},{7,6},{8,9},{9,8},{10,11... | collective-permute-start | bytes 196616 | tf_op jit(solution)/shard_map/ppermute | solution.py:254
  15.0 1.4 %collective-permute-start.2 = (bf16[128,256]{1,0:T(8,128)(2,1)S(1)}, bf16[128,256]{1,0:T(8,128)(2,1)S(1)}, u32[]{:S(2)}, u32[]{:S(2)}) collective-permute-start(bf16[128,256]{1,0:T(8,128)(2,1)S(1)} %collective-permute-done.1.refs_2_), channel_id=1, source_target_pairs={{0,1},{1,0},{2,3},{3,2},{4,5},{5,4},{6,7},{7,6},{8,9},{9,8},{10,11... | collective-permute-start | bytes 196616 | tf_op jit(solution)/shard_map/ppermute | solution.py:254
  16.5 4.5 %copy-start.3 = (s32[1,256]{1,0:T(1,128)S(1)}, s32[1,256]{1,0:T(1,128)}, u32[]{:S(2)}) copy-start(s32[1,256]{1,0:T(1,128)} %refs_9_.1) | copy-start | bytes 3076
  18.6 18.1 %copy-start = (f32[512,512]{1,0:T(8,128)S(1)}, f32[512,512]{1,0:T(8,128)}, u32[]{:S(2)}) copy-start(f32[512,512]{1,0:T(8,128)} %refs_3_.1) | copy-start | bytes 3145732
  18.6 7.2 %collective-permute-start.16 = (bf16[256,256]{1,0:T(8,128)(2,1)S(1)}, bf16[256,256]{1,0:T(8,128)(2,1)S(1)}, u32[]{:S(2)}, u32[]{:S(2)}) collective-permute-start(bf16[256,256]{1,0:T(8,128)(2,1)S(1)} %get-tuple-element.39.refs_10_), channel_id=1, source_target_pairs={{0,2},{2,0},{1,3},{3,1},{4,6},{6,4},{5,7},{7,5},{8,10},{10,8},{9,1... | collective-permute-start | bytes 393224 | tf_op jit(solution)/shard_map/ppermute | solution.py:254
  20.1 4.3 %collective-permute-start.10 = (f32[128,128]{1,0:T(8,128)S(1)}, f32[128,128]{1,0:T(8,128)S(1)}, u32[]{:S(2)}, u32[]{:S(2)}) collective-permute-start(f32[128,128]{1,0:T(8,128)S(1)} %get-tuple-element.38), channel_id=1, source_target_pairs={{0,4},{4,0},{8,12},{12,8},{1,5},{5,1},{9,13},{13,9},{2,6},{6,2},{1... | collective-permute-start | bytes 196616 | tf_op jit(solution)/shard_map/ppermute | solution.py:254
  21.5 12.4 %collective-permute-start.15 = (bf16[256,256]{1,0:T(8,128)(2,1)S(1)}, bf16[256,256]{1,0:T(8,128)(2,1)S(1)}, u32[]{:S(2)}, u32[]{:S(2)}) collective-permute-start(bf16[256,256]{1,0:T(8,128)(2,1)S(1)} %get-tuple-element.41.refs_4_.refs_2_), channel_id=1, source_target_pairs={{0,2},{2,0},{1,3},{3,1},{4,6},{6,4},{5,7},{7,5},{8,10},{10,8},{9,1... | collective-permute-start | bytes 393224 | tf_op jit(solution)/shard_map/ppermute | solution.py:254
  24.4 5.9 %collective-permute-start.11 = (f32[128,128]{1,0:T(8,128)S(1)}, f32[128,128]{1,0:T(8,128)S(1)}, u32[]{:S(2)}, u32[]{:S(2)}) collective-permute-start(f32[128,128]{1,0:T(8,128)S(1)} %add.6), channel_id=1, source_target_pairs={{0,8},{4,12},{8,0},{12,4},{1,9},{5,13},{9,1},{13,5},{2,10},{6,14},... | collective-permute-start | bytes 196616 | tf_op jit(solution)/shard_map/ppermute | solution.py:254
  25.8 12.8 %collective-permute-start.17 = (bf16[256,256]{1,0:T(8,128)(2,1)S(1)}, bf16[256,256]{1,0:T(8,128)(2,1)S(1)}, u32[]{:S(2)}, u32[]{:S(2)}) collective-permute-start(bf16[256,256]{1,0:T(8,128)(2,1)S(1)} %collective-permute-done.16.refs_4_), channel_id=1, source_target_pairs={{0,1},{1,0},{2,3},{3,2},{4,5},{5,4},{6,7},{7,6},{8,9},{9,8},{10,11... | collective-permute-start | bytes 393224 | tf_op jit(solution)/shard_map/ppermute | solution.py:254
  30.4 4.3 %collective-permute-start.12 = (f32[128,128]{1,0:T(8,128)S(1)}, f32[128,128]{1,0:T(8,128)S(1)}, u32[]{:S(2)}, u32[]{:S(2)}) collective-permute-start(f32[128,128]{1,0:T(8,128)S(1)} %add.7.refs_0_.refs_2_), channel_id=1, source_target_pairs={{0,4},{2,6},{4,0},{6,2},{8,12},{10,14},{12,8},{14,10},{1,5},{3,7},... | collective-permute-start | bytes 196616 | tf_op jit(solution)/shard_map/ppermute | solution.py:254
  30.6 5.2 %collective-permute-start.19 = (f32[128,128]{1,0:T(8,128)S(1)}, f32[128,128]{1,0:T(8,128)S(1)}, u32[]{:S(2)}, u32[]{:S(2)}) collective-permute-start(f32[128,128]{1,0:T(8,128)S(1)} %add.7.refs_0_.refs_2_), channel_id=1, source_target_pairs={{0,6},{2,4},{4,2},{6,0},{8,14},{10,12},{12,10},{14,8},{1,7},{3,5},... | collective-permute-start | bytes 196616 | tf_op jit(solution)/shard_map/ppermute | solution.py:254
  32.4 4.3 %collective-permute-start.18 = (f32[128,128]{1,0:T(8,128)S(1)}, f32[128,128]{1,0:T(8,128)S(1)}, u32[]{:S(2)}, u32[]{:S(2)}) collective-permute-start(f32[128,128]{1,0:T(8,128)S(1)} %add.7.refs_0_.refs_2_), channel_id=1, source_target_pairs={{0,2},{2,0},{4,6},{6,4},{8,10},{10,8},{12,14},{14,12},{1,3},{3,1},... | collective-permute-start | bytes 196616 | tf_op jit(solution)/shard_map/ppermute | solution.py:254
  33.9 4.4 %collective-permute-start.13 = (f32[128,128]{1,0:T(8,128)S(1)}, f32[128,128]{1,0:T(8,128)S(1)}, u32[]{:S(2)}, u32[]{:S(2)}) collective-permute-start(f32[128,128]{1,0:T(8,128)S(1)} %add.7.refs_0_.refs_2_), channel_id=1, source_target_pairs={{0,1},{1,0},{2,3},{3,2},{4,5},{5,4},{6,7},{7,6},{8,9},{9,8},{10,11... | collective-permute-start | bytes 196616 | tf_op jit(solution)/shard_map/ppermute | solution.py:254
  34.7 5.2 %collective-permute-start.14 = (f32[128,128]{1,0:T(8,128)S(1)}, f32[128,128]{1,0:T(8,128)S(1)}, u32[]{:S(2)}, u32[]{:S(2)}) collective-permute-start(f32[128,128]{1,0:T(8,128)S(1)} %collective-permute-done.12.refs_1_.refs_4_), channel_id=1, source_target_pairs={{0,1},{1,0},{2,3},{3,2},{4,5},{5,4},{6,7},{7,6},{8,9},{9,8},{10,11... | collective-permute-start | bytes 196616 | tf_op jit(solution)/shard_map/ppermute | solution.py:254
  35.8 4.4 %collective-permute-start.21 = (f32[128,128]{1,0:T(8,128)S(1)}, f32[128,128]{1,0:T(8,128)S(1)}, u32[]{:S(2)}, u32[]{:S(2)}) collective-permute-start(f32[128,128]{1,0:T(8,128)S(1)} %collective-permute-done.19.refs_6_), channel_id=1, source_target_pairs={{0,1},{1,0},{2,3},{3,2},{4,5},{5,4},{6,7},{7,6},{8,9},{9,8},{10,11... | collective-permute-start | bytes 196616 | tf_op jit(solution)/shard_map/ppermute | solution.py:254
  36.7 3.5 %collective-permute-start.20 = (f32[128,128]{1,0:T(8,128)S(1)}, f32[128,128]{1,0:T(8,128)S(1)}, u32[]{:S(2)}, u32[]{:S(2)}) collective-permute-start(f32[128,128]{1,0:T(8,128)S(1)} %collective-permute-done.18.refs_5_), channel_id=1, source_target_pairs={{0,1},{1,0},{2,3},{3,2},{4,5},{5,4},{6,7},{7,6},{8,9},{9,8},{10,11... | collective-permute-start | bytes 196616 | tf_op jit(solution)/shard_map/ppermute | solution.py:254

commit v5 on v4

--- a/solution.py
+++ b/solution.py
@@ -11,6 +11,7 @@
 LOG2E = 1.4426950408889634
 VMEM_LIMIT = 24 << 20
 SLAB_STEP = 512
+OWN_CHUNKS = 1
 ROWS_ROWS = (((1,), (1,)), ((), ()))
 VMEM = pl.BlockSpec(memory_space=pltpu.VMEM)
 SMEM = pl.BlockSpec(memory_space=pltpu.SMEM)
@@ -66,18 +67,29 @@
 
 
 def own_kernel(
-    n_sub, quarter, rows_hbm, points_hbm, counts_hbm,
-    own_ref, rows_ref, points_ref, to_ref, counts, rows_sem, points_sem, counts_sem,
+    n_sub, quarter, rows_hbm, points_hbm, counts_hbm, pick_hbm,
+    own_ref, rows_ref, points_ref, to_ref, pick_ref, counts, rows_sem, counts_sem, pick_sem, points_sems,
 ):
     total, width = points_ref.shape
     cap = own_ref.shape[0]
-    step = math.gcd(total, 256)
+    chunk = total // OWN_CHUNKS
+    step = math.gcd(chunk, 256)
     rows_copy = pltpu.make_async_copy(rows_hbm, rows_ref, rows_sem)
-    points_copy = pltpu.make_async_copy(points_hbm, points_ref, points_sem)
     counts_copy = pltpu.make_async_copy(counts_hbm, counts, counts_sem)
+    pick_copy = pltpu.make_async_copy(pick_hbm, pick_ref, pick_sem)
+    points_copies = [
+        pltpu.make_async_copy(
+            points_hbm.at[pl.ds(at * chunk, chunk), :],
+            points_ref.at[pl.ds(at * chunk, chunk), :],
+            points_sems.at[at],
+        )
+        for at in range(OWN_CHUNKS)
+    ]
     rows_copy.start()
     counts_copy.start()
-    points_copy.start()
+    for copy in points_copies:
+        copy.start()
+    pick_copy.start()
     rows_copy.wait()
     row_ids = as_column(rows_ref[...])
     hots = [one_hot(row_ids, at, step) for at in range(0, total, step)]
@@ -88,11 +100,13 @@
     for rel in range(to_ref.shape[0]):
         off, count = owner_span(counts, (pts_at * n_sub + sub_at) ^ rel)
         to_ref[rel : rel + 1, :] = jnp.where(slot < count, (slot + off) ^ turn, -1)
-    points_copy.wait()
     own = jnp.zeros((cap, width), jnp.float32)
     for at, hot in enumerate(hots):
+        if at * step % chunk == 0:
+            points_copies[at * step // chunk].wait()
         own = own + dot(hot, points_ref[at * step : (at + 1) * step, :])
     own_ref[...] = own.astype(own_ref.dtype)
+    pick_copy.wait()
 
 
 def hots_of(to_ref, rels, base, size):
@@ -101,9 +115,14 @@
     return jnp.concatenate(hots, axis=1)
 
 
-def prep_kernel(rows_ref, weights_ref, targets_ref, to_ref, shift_ref, turned_ref, place_ref, hots_ref):
+def prep_kernel(
+    quarter, rows_ref, weights_ref, targets_ref, to_ref, pick_ref,
+    shift_ref, turned_ref, place_ref, hots_ref, picks_ref,
+):
     place_ref[...] = one_hot(as_column(to_ref[:1, :]), 0, place_ref.shape[1])
     hots_ref[...] = hots_of(to_ref, range(to_ref.shape[0]), 0, hots_ref.shape[0])
+    turn = (lax.axis_index("sub") * 2 + lax.axis_index("pts") % 2) * quarter
+    picks_ref[...] = one_hot(as_column(pick_ref[...] ^ turn), 0, picks_ref.shape[1])
     total = weights_ref.shape[0]
     step = math.gcd(total, 256)
     row_ids = as_column(rows_ref[...])
@@ -131,13 +150,20 @@
     refs[-1][...] = sum(dot(hots, jnp.concatenate(part, axis=0)) for part in zip(*parts))
 
 
-def slab_kernel(n_blocks, n_sub, quarter, *refs):
-    blocks, refs = refs[:n_blocks], refs[n_blocks:]
+def most_kernel(late, hots_ref, *refs):
+    blocks, out_ref = refs[:-1], refs[-1]
+    cap = blocks[0].shape[0]
+    hots = jnp.concatenate([hots_ref[:, : late * cap], hots_ref[:, (late + 1) * cap :]], axis=1)
+    out_ref[...] = dot(hots, jnp.concatenate([block[...] for block in blocks], axis=0))
+
+
+def slab_kernel(late, n_sub, quarter, block_ref, most_ref, *refs):
     slabs, slab_sqs, slab_ws = refs[:n_sub], refs[n_sub : 2 * n_sub], refs[2 * n_sub : 3 * n_sub]
     hots_ref, sums_ref, keep_ref, send_ref, mine_ref = refs[3 * n_sub :]
     scale = LOG2E / mine_ref.shape[1]
-    points = jnp.concatenate([block[...] for block in blocks], axis=0)
-    mine_x = dot(hots_ref[...], points).astype(jnp.bfloat16)
+    cap = block_ref.shape[0]
+    hots = hots_ref[:, late * cap : (late + 1) * cap]
+    mine_x = (most_ref[...] + dot(hots, block_ref[...])).astype(jnp.bfloat16)
     mine_ref[...] = mine_x
     mine_sq = row_sq(mine_x, scale)
     total = jnp.zeros((keep_ref.shape[1], 2 * quarter), jnp.float32)
@@ -156,17 +182,15 @@
     send_ref[...] = total[quarter:]
 
 
-def pick_kernel(n_blocks, quarter, *refs):
-    blocks, (to_ref, pick_ref, mine_ref, live_ref, sketch_ref) = refs[:n_blocks], refs[n_blocks:]
+def pick_kernel(n_blocks, *refs):
+    blocks, (to_ref, picks_ref, mine_ref, live_ref, sketch_ref) = refs[:n_blocks], refs[n_blocks:]
     live, half = live_ref.shape[0], mine_ref.shape[0]
     points = jnp.concatenate([block[...] for block in blocks], axis=0)
     live_ref[:half, :] = mine_ref[...]
     for base in range(half, live, half):
         hots = hots_of(to_ref, range(n_blocks), base, half)
         live_ref[base : base + half, :] = dot(hots, points).astype(jnp.bfloat16)
-    turn = (lax.axis_index("sub") * 2 + lax.axis_index("pts") % 2) * quarter
-    hot = one_hot(as_column(pick_ref[...] ^ turn), 0, live)
-    sketch_ref[...] = dot(hot, live_ref[...]).astype(sketch_ref.dtype)
+    sketch_ref[...] = dot(picks_ref[...], live_ref[...]).astype(sketch_ref.dtype)
 
 
 def sketch_rows(rows, points):
@@ -283,32 +307,37 @@
         def bf16(*shape):
             return jax.ShapeDtypeStruct(shape, jnp.bfloat16)
 
-        own_x, row_ids, points, places = call(
+        own_x, row_ids, points, places, pick_ids = call(
             lambda *refs: own_kernel(n_sub, quarter, *refs),
             (
                 bf16(cap, width),
                 jax.ShapeDtypeStruct((1, cap), jnp.int32),
                 bf16(*points.shape),
                 jax.ShapeDtypeStruct((owners, cap), jnp.int32),
+                jax.ShapeDtypeStruct(sketch_pick.shape, jnp.int32),
             ),
             (),
             tuple(
                 pltpu.with_memory_space_constraint(value, pltpu.MemorySpace.HBM)
-                for value in (tile_rows[0], points, tile_count)
+                for value in (tile_rows[0], points, tile_count, sketch_pick)
             ),
-            (pltpu.SMEM(tile_count.shape, jnp.int32), *(pltpu.SemaphoreType.DMA(()),) * 3),
+            (
+                pltpu.SMEM(tile_count.shape, jnp.int32),
+                *(pltpu.SemaphoreType.DMA(()),) * 3,
+                pltpu.SemaphoreType.DMA((OWN_CHUNKS,)),
+            ),
             pl.BlockSpec(memory_space=pltpu.MemorySpace.HBM),
         )
         far = [own_x] + [hop(own_x, "pts", i) for i in range(1, n_pts)]
         slabs = near_of(points)
-        shift, turned, own_place, hots = call(
-            prep_kernel,
+        shift, turned, own_place, hots, pick_hots = call(
+            lambda *refs: prep_kernel(quarter, *refs),
             (
                 f32(cap, outs), bf16(outs, points.shape[0]),
-                bf16(cap, live), bf16(2 * quarter, owners * cap),
+                bf16(cap, live), bf16(2 * quarter, owners * cap), bf16(picks, live),
             ),
             (),
-            (row_ids, weights, block_targets[0], places),
+            (row_ids, weights, block_targets[0], places, pick_ids),
         )
         slab_ws = near_of(turned)
         sums = call(shift_kernel, f32(2 * quarter, outs), (), (places, *near_of(shift)))
@@ -316,11 +345,18 @@
         blocks = []
         for block in far:
             blocks += near_of(block)
+        late = min(3 * n_sub, owners) - 1
+        most = call(
+            lambda *refs: most_kernel(late, *refs),
+            f32(2 * quarter, width),
+            (),
+            (hots, *blocks[:late], *blocks[late + 1 :]),
+        )
         part, send, mine_x = call(
-            lambda *refs: slab_kernel(owners, n_sub, quarter, *refs),
+            lambda *refs: slab_kernel(late, n_sub, quarter, *refs),
             (f32(quarter, outs), f32(quarter, outs), bf16(2 * quarter, width)),
             (),
-            (*blocks, *slabs, *slab_sqs, *slab_ws, hots, sums),
+            (blocks[late], most, *slabs, *slab_sqs, *slab_ws, hots, sums),
         )
 
         part = part + hop(send, "pts", 1)
@@ -330,10 +366,10 @@
             step *= 2
 
         live_x, sketch = call(
-            lambda *refs: pick_kernel(owners, quarter, *refs),
+            lambda *refs: pick_kernel(owners, *refs),
             (bf16(live, width), bf16(picks, width)),
             (),
-            (*blocks, places, sketch_pick, mine_x),
+            (*blocks, places, pick_hots, mine_x),
         )
         got_sketch = [hop(sketch, "col", i) for i in range(1, n_col)]
         got_rows = []

time: 41.2 us -> 43.8 us (1.063)
  waiting for transfers between devices: 15 us -> 17.1 us
    ppermute x22, waiting for transfers between devices: 15 us -> 17.1 us  [hop(): return lax.ppermute(values, axis, [(j, j ^ step) for j in range(size)])]
    pallas_call x13 -> x14, Pallas kernels: 10 us -> 10.3 us  [call(): pl.pallas_call(kernel, out_shape=out_shape, in_specs=[SMEM] * len(smem) +...]
  transfers between devices with their start and end apart: 22 -> 22, of which waited for: 7 -> 9; matrix products, arithmetic and copies ran while one was open for 0% -> 0% of each run, Pallas kernels for 13% -> 14%
where the time goes in v5:
time: 43.8 us; the launch traced here: 43.6 us
  waiting for transfers between devices  17.1 us (39%)
  starting transfers between devices  15.4 us (35%)
  Pallas kernels  10.3 us (24%)
  between operations  0.85 us (2%)
    ppermute x22, waiting for transfers between devices, hop(): return lax.ppermute(values, axis, [(j, j ^ step) for j in range(size)])  17.1 us
    ppermute x22, starting transfers between devices, hop(): return lax.ppermute(values, axis, [(j, j ^ step) for j in range(size)])  15.4 us
    pallas_call x14, Pallas kernels, call(): pl.pallas_call(kernel, out_shape=out_shape, in_specs=[SMEM] * len(smem) +...  10.3 us
  transfers between devices with their start and end apart: 22, of which 9 were waited for; matrix products, arithmetic and copies ran while one was open for 0% of the time, Pallas kernels for 14%

profile of v5, /device:TPU:0, one launch (start us, length us, event | category | flops | bytes accessed | tf_op | source)
XLA Modules:
  0.0 43.6 jit_solution(7147359762833358717)
XLA Ops:
  0.7 1.6 %shard_map.86 = (bf16[128,256]{1,0:T(8,128)(2,1)S(1)}, s32[1,128]{1,0:T(1,128)S(1)}, bf16[2048,256]{1,0:T(8,128)(2,1)S(1)}, s32[8,128]{1,0:T(8,128)S(1)}, s32[1,256]{1,0:T(1,128)S(1)}) custom-call(s32[1,128]{1,0:T(1,128)} %bitcast.5, bf16[2048,256]{1,0:T(8,128)(2,1)} %refs_1_.2, s32[1,8]{1,0:T(1,128)} %refs_2_.1, s32[1,256]{1,0:T(1,128)} %refs_3_.2), custom_call_target="tpu_custom_call" | custom-call | tf_op jit(solution)/shard_map/pallas_call | solution.py:284
  2.3 0.6 %collective-permute-start.7 = (bf16[2048,256]{1,0:T(8,128)(2,1)S(1)}, bf16[2048,256]{1,0:T(8,128)(2,1)S(1)}, u32[]{:S(2)}, u32[]{:S(2)}) collective-permute-start(bf16[2048,256]{1,0:T(8,128)(2,1)S(1)} %get-tuple-element.37.points_ref.refs_2_), channel_id=1, source_target_pairs={{0,1},{1,0},{2,3},{3,2},{4,5},{5,4},{6,7},{7,6},{8,9},{9,8},{10,11... | collective-permute-start | bytes 3145736 | tf_op jit(solution)/shard_map/ppermute | solution.py:278
  2.9 0.7 %shard_map.87 = (f32[128,128]{1,0:T(8,128)S(1)}, bf16[128,2048]{1,0:T(8,128)(2,1)S(1)}, bf16[128,512]{1,0:T(8,128)(2,1)S(1)}, bf16[256,1024]{1,0:T(8,128)(2,1)S(1)}, bf16[256,512]{1,0:T(8,128)(2,1)S(1)}) custom-call(s32[1,128]{1,0:T(1,128)S(1)} %get-tuple-element.31.refs_0_, bf16[2048,128]{1,0:T(8,128)(2,1)S(1)} %copy-done.1, bf16[128,128]{1,0:T(8,128)(2,1)S(1)} %bitcast.4, ...), custom_call_target="tpu_custom_call" | custom-call | tf_op jit(solution)/shard_map/pallas_call | solution.py:284
  3.6 0.1 collective-permute-start.8
  3.7 5.1 %collective-permute-start.5 = (bf16[128,256]{1,0:T(8,128)(2,1)S(1)}, bf16[128,256]{1,0:T(8,128)(2,1)S(1)}, u32[]{:S(2)}, u32[]{:S(2)}) collective-permute-start(bf16[128,256]{1,0:T(8,128)(2,1)S(1)} %get-tuple-element.35.refs_1_.refs_0_), channel_id=1, source_target_pairs={{0,12},{4,8},{8,4},{12,0},{1,13},{5,9},{9,5},{13,1},{2,14},{6,10},... | collective-permute-start | bytes 196616 | tf_op jit(solution)/shard_map/ppermute | solution.py:278
  8.8 0.0 collective-permute-start.3
  8.8 0.0 collective-permute-start.2
  8.8 2.9 %collective-permute-done.5.refs_6_ = bf16[128,256]{1,0:T(8,128)(2,1)S(1)} collective-permute-done((bf16[128,256]{1,0:T(8,128)(2,1)S(1)}, bf16[128,256]{1,0:T(8,128)(2,1)S(1)}, u32[]{:S(2)}, u32[]{:S(2)}) %collective-permute-start.5) | collective-permute-done | bytes 65568 | tf_op jit(solution)/shard_map/ppermute | solution.py:278
  11.7 0.3 collective-permute-start
  12.0 1.0 %collective-permute-done.3.refs_3_.refs_2_ = bf16[128,256]{1,0:T(8,128)(2,1)S(1)} collective-permute-done((bf16[128,256]{1,0:T(8,128)(2,1)S(1)}, bf16[128,256]{1,0:T(8,128)(2,1)S(1)}, u32[]{:S(2)}, u32[]{:S(2)}) %collective-permute-start.3) | collective-permute-done | bytes 65568 | tf_op jit(solution)/shard_map/ppermute | solution.py:278
  13.0 0.0 collective-permute-start.9
  13.0 0.0 collective-permute-done.2.refs_2_.refs_1_
  13.0 0.5 %collective-permute-start.6 = (bf16[128,256]{1,0:T(8,128)(2,1)S(1)}, bf16[128,256]{1,0:T(8,128)(2,1)S(1)}, u32[]{:S(2)}, u32[]{:S(2)}) collective-permute-start(bf16[128,256]{1,0:T(8,128)(2,1)S(1)} %collective-permute-done.5.refs_6_), channel_id=1, source_target_pairs={{0,1},{1,0},{2,3},{3,2},{4,5},{5,4},{6,7},{7,6},{8,9},{9,8},{10,11... | collective-permute-start | bytes 196616 | tf_op jit(solution)/shard_map/ppermute | solution.py:278
  13.6 3.3 %collective-permute-done.refs_5_.refs_4_ = bf16[128,256]{1,0:T(8,128)(2,1)S(1)} collective-permute-done((bf16[128,256]{1,0:T(8,128)(2,1)S(1)}, bf16[128,256]{1,0:T(8,128)(2,1)S(1)}, u32[]{:S(2)}, u32[]{:S(2)}) %collective-permute-start) | collective-permute-done | bytes 65568 | tf_op jit(solution)/shard_map/ppermute | solution.py:278
  16.9 0.0 collective-permute-start.4
  16.9 0.5 %collective-permute-start.1 = (bf16[128,256]{1,0:T(8,128)(2,1)S(1)}, bf16[128,256]{1,0:T(8,128)(2,1)S(1)}, u32[]{:S(2)}, u32[]{:S(2)}) collective-permute-start(bf16[128,256]{1,0:T(8,128)(2,1)S(1)} %collective-permute-done.refs_5_.refs_4_), channel_id=1, source_target_pairs={{0,1},{1,0},{2,3},{3,2},{4,5},{5,4},{6,7},{7,6},{8,9},{9,8},{10,11... | collective-permute-start | bytes 196616 | tf_op jit(solution)/shard_map/ppermute | solution.py:278
  17.4 0.3 shard_map.89.refs_4_
  17.7 0.3 shard_map.91.refs_9_
  18.0 0.0 collective-permute-done.6.refs_7_
  18.0 0.1 collective-permute-done.4.refs_4_.refs_3_
  18.1 0.3 shard_map.88.refs_1_
  18.5 0.3 shard_map.90.refs_5_
  18.8 0.0 collective-permute-done.8.refs_7_
  18.8 1.8 %shard_map.92 = (f32[128,128]{1,0:T(8,128)S(1)}, f32[128,128]{1,0:T(8,128)S(1)}, bf16[256,256]{1,0:T(8,128)(2,1)S(1)}) custom-call(bf16[128,256]{1,0:T(8,128)(2,1)S(1)} %collective-permute-done.1.refs_0_.refs_5_, f32[256,256]{1,0:T(8,128)S(1)} %shard_map.88.refs_1_, bf16[2048,256]{1,0:T(8,128)(2,1)S(1)} %get-tuple-element.37.points_ref.refs_2_, ...), custom_call_target="tpu_custom_call" | custom-call | tf_op jit(solution)/shard_map/pallas_call | solution.py:284
  20.7 0.0 copy-start
  20.7 2.5 %collective-permute-start.16 = (bf16[256,256]{1,0:T(8,128)(2,1)S(1)}, bf16[256,256]{1,0:T(8,128)(2,1)S(1)}, u32[]{:S(2)}, u32[]{:S(2)}) collective-permute-start(bf16[256,256]{1,0:T(8,128)(2,1)S(1)} %get-tuple-element.43.refs_10_), channel_id=1, source_target_pairs={{0,2},{2,0},{1,3},{3,1},{4,6},{6,4},{5,7},{7,5},{8,10},{10,8},{9,1... | collective-permute-start | bytes 393224 | tf_op jit(solution)/shard_map/ppermute | solution.py:278
  23.1 0.5 %collective-permute-start.10 = (f32[128,128]{1,0:T(8,128)S(1)}, f32[128,128]{1,0:T(8,128)S(1)}, u32[]{:S(2)}, u32[]{:S(2)}) collective-permute-start(f32[128,128]{1,0:T(8,128)S(1)} %get-tuple-element.41), channel_id=1, source_target_pairs={{0,4},{4,0},{8,12},{12,8},{1,5},{5,1},{9,13},{13,9},{2,6},{6,2},{1... | collective-permute-start | bytes 196616 | tf_op jit(solution)/shard_map/ppermute | solution.py:278
  23.6 0.5 %shard_map.94 = (bf16[512,256]{1,0:T(8,128)(2,1)S(1)}, bf16[256,256]{1,0:T(8,128)(2,1)S(1)}) custom-call(bf16[128,256]{1,0:T(8,128)(2,1)S(1)} %get-tuple-element.35.refs_1_.refs_0_, bf16[128,256]{1,0:T(8,128)(2,1)S(1)} %collective-permute-done.2.refs_2_.refs_1_, bf16[128,256]{1,0:T(8,128)(2,1)S(1)} %collective-permute-done.3.refs_3_.refs_2_, ...), custom_call_target="tpu_custom_call" | custom-call | tf_op jit(solution)/shard_map/pallas_call | solution.py:284
  24.2 0.5 %collective-permute-start.15 = (bf16[256,256]{1,0:T(8,128)(2,1)S(1)}, bf16[256,256]{1,0:T(8,128)(2,1)S(1)}, u32[]{:S(2)}, u32[]{:S(2)}) collective-permute-start(bf16[256,256]{1,0:T(8,128)(2,1)S(1)} %get-tuple-element.45.refs_4_.refs_2_), channel_id=1, source_target_pairs={{0,2},{2,0},{1,3},{3,1},{4,6},{6,4},{5,7},{7,5},{8,10},{10,8},{9,1... | collective-permute-start | bytes 393224 | tf_op jit(solution)/shard_map/ppermute | solution.py:278
  24.7 2.7 %collective-permute-done.10 = f32[128,128]{1,0:T(8,128)S(1)} collective-permute-done((f32[128,128]{1,0:T(8,128)S(1)}, f32[128,128]{1,0:T(8,128)S(1)}, u32[]{:S(2)}, u32[]{:S(2)}) %collective-permute-start.10) | collective-permute-done | bytes 65568 | tf_op jit(solution)/shard_map/ppermute | solution.py:278
  27.4 1.3 %collective-permute-start.11 = (f32[128,128]{1,0:T(8,128)S(1)}, f32[128,128]{1,0:T(8,128)S(1)}, u32[]{:S(2)}, u32[]{:S(2)}) collective-permute-start(f32[128,128]{1,0:T(8,128)S(1)} %add.6), channel_id=1, source_target_pairs={{0,8},{4,12},{8,0},{12,4},{1,9},{5,13},{9,1},{13,5},{2,10},{6,14},... | collective-permute-start | bytes 196616 | tf_op jit(solution)/shard_map/ppermute | solution.py:278
  28.8 4.5 %collective-permute-done.11 = f32[128,128]{1,0:T(8,128)S(1)} collective-permute-done((f32[128,128]{1,0:T(8,128)S(1)}, f32[128,128]{1,0:T(8,128)S(1)}, u32[]{:S(2)}, u32[]{:S(2)}) %collective-permute-start.11) | collective-permute-done | bytes 65568 | tf_op jit(solution)/shard_map/ppermute | solution.py:278
  33.3 0.1 collective-permute-start.12
  33.4 1.6 %collective-permute-start.19 = (f32[128,128]{1,0:T(8,128)S(1)}, f32[128,128]{1,0:T(8,128)S(1)}, u32[]{:S(2)}, u32[]{:S(2)}) collective-permute-start(f32[128,128]{1,0:T(8,128)S(1)} %add.7.refs_0_.refs_2_), channel_id=1, source_target_pairs={{0,6},{2,4},{4,2},{6,0},{8,14},{10,12},{12,10},{14,8},{1,7},{3,5},... | collective-permute-start | bytes 196616 | tf_op jit(solution)/shard_map/ppermute | solution.py:278
  35.0 1.9 %collective-permute-start.18 = (f32[128,128]{1,0:T(8,128)S(1)}, f32[128,128]{1,0:T(8,128)S(1)}, u32[]{:S(2)}, u32[]{:S(2)}) collective-permute-start(f32[128,128]{1,0:T(8,128)S(1)} %add.7.refs_0_.refs_2_), channel_id=1, source_target_pairs={{0,2},{2,0},{4,6},{6,4},{8,10},{10,8},{12,14},{14,12},{1,3},{3,1},... | collective-permute-start | bytes 196616 | tf_op jit(solution)/shard_map/ppermute | solution.py:278
  36.8 0.8 %collective-permute-done.12.refs_1_.refs_4_ = f32[128,128]{1,0:T(8,128)S(1)} collective-permute-done((f32[128,128]{1,0:T(8,128)S(1)}, f32[128,128]{1,0:T(8,128)S(1)}, u32[]{:S(2)}, u32[]{:S(2)}) %collective-permute-start.12) | collective-permute-done | bytes 65568 | tf_op jit(solution)/shard_map/ppermute | solution.py:278
  37.6 1.0 %collective-permute-done.19.refs_6_ = f32[128,128]{1,0:T(8,128)S(1)} collective-permute-done((f32[128,128]{1,0:T(8,128)S(1)}, f32[128,128]{1,0:T(8,128)S(1)}, u32[]{:S(2)}, u32[]{:S(2)}) %collective-permute-start.19) | collective-permute-done | bytes 65568 | tf_op jit(solution)/shard_map/ppermute | solution.py:278
  38.6 0.0 collective-permute-start.21
  38.6 0.7 %collective-permute-done.18.refs_5_ = f32[128,128]{1,0:T(8,128)S(1)} collective-permute-done((f32[128,128]{1,0:T(8,128)S(1)}, f32[128,128]{1,0:T(8,128)S(1)}, u32[]{:S(2)}, u32[]{:S(2)}) %collective-permute-start.18) | collective-permute-done | bytes 65568 | tf_op jit(solution)/shard_map/ppermute | solution.py:278
  39.3 1.6 %shard_map.95 = (bf16[128,512]{1,0:T(8,128)(2,1)S(1)}, bf16[128,512]{1,0:T(8,128)(2,1)S(1)}, bf16[128,256]{1,0:T(8,128)(2,1)S(1)}, bf16[128,256]{1,0:T(8,128)(2,...) custom-call(bf16[128,256]{1,0:T(8,128)(2,1)S(1)} %get-tuple-element., ...), custom_call_target="tpu_custom_call" | custom-call | tf_op jit(solution)/shard_map/pallas_call | solution.py:284
  40.9 0.0 collective-permute-done.13.refs_2_.refs_3_
  40.9 0.2 shard_map.96.refs_1_
  41.1 0.0 collective-permute-done.17.refs_5_
  41.2 1.1 %shard_map.97 = (bf16[128,256]{1,0:T(8,128)(2,1)S(1)}, bf16[128,256]{1,0:T(8,128)(2,1)S(1)}, bf16[128,256]{1,0:T(8,128)(2,1)S(1)}, bf16[128,256]{1,0:T(8,128)(2,1)S(1)}) custom-call(bf16[128,512]{1,0:T(8,128)(2,1)S(1)} %get-tuple-element.50.refs_0_, bf16[128,512]{1,0:T(8,128)(2,1)S(1)} %get-tuple-element.51.refs_1_, ...), custom_call_target="tpu_custom_call" | custom-call | tf_op jit(solution)/shard_map/pallas_call | solution.py:284
  42.2 0.2 shard_map.98.refs_2_
  42.5 0.0 collective-permute-done.14.refs_3_.refs_7_
  42.5 0.3 shard_map.93.refs_0_
  42.8 0.9 %shard_map.99 = (f32[128,128]{1,0:T(8,128)}, f32[128,128]{1,0:T(8,128)}) custom-call(f32[128,128]{1,0:T(8,128)S(1)} %shard_map.93.refs_0_, f32[128,128]{1,0:T(8,128)S(1)} %shard_map.96.refs_1_, f32[128,128]{1,0:T(8,128)S(1)} %shard_map.98.refs_2_, bf16[128,128]{1,0:T(8,128)(2,1)S(1)} %get-tuple-element.54.refs_3_, ...), custom_call_target="tpu_custom_call" | custom-call | tf_op jit(solution)/shard_map/pallas_call | solution.py:284
  (18 shorter events, 0.1 us)
Async XLA Ops:
  0.6 2.2 %copy-start.1 = (bf16[2048,128]{1,0:T(8,128)(2,1)S(1)}, bf16[2048,128]{1,0:T(8,128)(2,1)}, u32[]{:S(2)}) copy-start(bf16[2048,128]{1,0:T(8,128)(2,1)} %refs_1_.3) | copy-start | bytes 1572868
  0.6 2.2 %copy-start.2 = (bf16[1,128,128]{2,1,0:T(8,128)(2,1)S(1)}, bf16[1,128,128]{2,1,0:T(8,128)(2,1)}, u32[]{:S(2)}) copy-start(bf16[1,128,128]{2,1,0:T(8,128)(2,1)} %param.12) | copy-start | bytes 98308
  2.3 16.1 %collective-permute-start.7 = (bf16[2048,256]{1,0:T(8,128)(2,1)S(1)}, bf16[2048,256]{1,0:T(8,128)(2,1)S(1)}, u32[]{:S(2)}, u32[]{:S(2)}) collective-permute-start(bf16[2048,256]{1,0:T(8,128)(2,1)S(1)} %get-tuple-element.37.points_ref.refs_2_), channel_id=1, source_target_pairs={{0,1},{1,0},{2,3},{3,2},{4,5},{5,4},{6,7},{7,6},{8,9},{9,8},{10,11... | collective-permute-start | bytes 3145736 | tf_op jit(solution)/shard_map/ppermute | solution.py:278
  3.6 15.2 %collective-permute-start.8 = (bf16[128,2048]{1,0:T(8,128)(2,1)S(1)}, bf16[128,2048]{1,0:T(8,128)(2,1)S(1)}, u32[]{:S(2)}, u32[]{:S(2)}) collective-permute-start(bf16[128,2048]{1,0:T(8,128)(2,1)S(1)} %get-tuple-element.38.refs_6_), channel_id=1, source_target_pairs={{0,1},{1,0},{2,3},{3,2},{4,5},{5,4},{6,7},{7,6},{8,9},{9,8},{10,11... | collective-permute-start | bytes 1572872 | tf_op jit(solution)/shard_map/ppermute | solution.py:278
  3.7 8.0 %collective-permute-start.5 = (bf16[128,256]{1,0:T(8,128)(2,1)S(1)}, bf16[128,256]{1,0:T(8,128)(2,1)S(1)}, u32[]{:S(2)}, u32[]{:S(2)}) collective-permute-start(bf16[128,256]{1,0:T(8,128)(2,1)S(1)} %get-tuple-element.35.refs_1_.refs_0_), channel_id=1, source_target_pairs={{0,12},{4,8},{8,4},{12,0},{1,13},{5,9},{9,5},{13,1},{2,14},{6,10},... | collective-permute-start | bytes 196616 | tf_op jit(solution)/shard_map/ppermute | solution.py:278
  8.8 4.3 %collective-permute-start.3 = (bf16[128,256]{1,0:T(8,128)(2,1)S(1)}, bf16[128,256]{1,0:T(8,128)(2,1)S(1)}, u32[]{:S(2)}, u32[]{:S(2)}) collective-permute-start(bf16[128,256]{1,0:T(8,128)(2,1)S(1)} %get-tuple-element.35.refs_1_.refs_0_), channel_id=1, source_target_pairs={{0,4},{4,0},{8,12},{12,8},{1,5},{5,1},{9,13},{13,9},{2,6},{6,2},{1... | collective-permute-start | bytes 196616 | tf_op jit(solution)/shard_map/ppermute | solution.py:278
  8.8 4.3 %collective-permute-start.2 = (bf16[128,256]{1,0:T(8,128)(2,1)S(1)}, bf16[128,256]{1,0:T(8,128)(2,1)S(1)}, u32[]{:S(2)}, u32[]{:S(2)}) collective-permute-start(bf16[128,256]{1,0:T(8,128)(2,1)S(1)} %get-tuple-element.35.refs_1_.refs_0_), channel_id=1, source_target_pairs={{0,1},{1,0},{2,3},{3,2},{4,5},{5,4},{6,7},{7,6},{8,9},{9,8},{10,11... | collective-permute-start | bytes 196616 | tf_op jit(solution)/shard_map/ppermute | solution.py:278
  11.7 5.2 %collective-permute-start = (bf16[128,256]{1,0:T(8,128)(2,1)S(1)}, bf16[128,256]{1,0:T(8,128)(2,1)S(1)}, u32[]{:S(2)}, u32[]{:S(2)}) collective-permute-start(bf16[128,256]{1,0:T(8,128)(2,1)S(1)} %get-tuple-element.35.refs_1_.refs_0_), channel_id=1, source_target_pairs={{0,8},{4,12},{8,0},{12,4},{1,9},{5,13},{9,1},{13,5},{2,10},{6,14},... | collective-permute-start | bytes 196616 | tf_op jit(solution)/shard_map/ppermute | solution.py:278
  13.0 3.8 %collective-permute-start.9 = (f32[128,128]{1,0:T(8,128)S(1)}, f32[128,128]{1,0:T(8,128)S(1)}, u32[]{:S(2)}, u32[]{:S(2)}) collective-permute-start(f32[128,128]{1,0:T(8,128)S(1)} %get-tuple-element.39.refs_0_), channel_id=1, source_target_pairs={{0,1},{1,0},{2,3},{3,2},{4,5},{5,4},{6,7},{7,6},{8,9},{9,8},{10,11... | collective-permute-start | bytes 196616 | tf_op jit(solution)/shard_map/ppermute | solution.py:278
  13.0 5.0 %collective-permute-start.6 = (bf16[128,256]{1,0:T(8,128)(2,1)S(1)}, bf16[128,256]{1,0:T(8,128)(2,1)S(1)}, u32[]{:S(2)}, u32[]{:S(2)}) collective-permute-start(bf16[128,256]{1,0:T(8,128)(2,1)S(1)} %collective-permute-done.5.refs_6_), channel_id=1, source_target_pairs={{0,1},{1,0},{2,3},{3,2},{4,5},{5,4},{6,7},{7,6},{8,9},{9,8},{10,11... | collective-permute-start | bytes 196616 | tf_op jit(solution)/shard_map/ppermute | solution.py:278
  16.9 1.3 %collective-permute-start.4 = (bf16[128,256]{1,0:T(8,128)(2,1)S(1)}, bf16[128,256]{1,0:T(8,128)(2,1)S(1)}, u32[]{:S(2)}, u32[]{:S(2)}) collective-permute-start(bf16[128,256]{1,0:T(8,128)(2,1)S(1)} %collective-permute-done.3.refs_3_.refs_2_), channel_id=1, source_target_pairs={{0,1},{1,0},{2,3},{3,2},{4,5},{5,4},{6,7},{7,6},{8,9},{9,8},{10,11... | collective-permute-start | bytes 196616 | tf_op jit(solution)/shard_map/ppermute | solution.py:278
  16.9 1.9 %collective-permute-start.1 = (bf16[128,256]{1,0:T(8,128)(2,1)S(1)}, bf16[128,256]{1,0:T(8,128)(2,1)S(1)}, u32[]{:S(2)}, u32[]{:S(2)}) collective-permute-start(bf16[128,256]{1,0:T(8,128)(2,1)S(1)} %collective-permute-done.refs_5_.refs_4_), channel_id=1, source_target_pairs={{0,1},{1,0},{2,3},{3,2},{4,5},{5,4},{6,7},{7,6},{8,9},{9,8},{10,11... | collective-permute-start | bytes 196616 | tf_op jit(solution)/shard_map/ppermute | solution.py:278
  20.7 18.6 %copy-start = (f32[512,512]{1,0:T(8,128)S(1)}, f32[512,512]{1,0:T(8,128)}, u32[]{:S(2)}) copy-start(f32[512,512]{1,0:T(8,128)} %refs_3_.3) | copy-start | bytes 3145732
  20.7 8.1 %collective-permute-start.16 = (bf16[256,256]{1,0:T(8,128)(2,1)S(1)}, bf16[256,256]{1,0:T(8,128)(2,1)S(1)}, u32[]{:S(2)}, u32[]{:S(2)}) collective-permute-start(bf16[256,256]{1,0:T(8,128)(2,1)S(1)} %get-tuple-element.43.refs_10_), channel_id=1, source_target_pairs={{0,2},{2,0},{1,3},{3,1},{4,6},{6,4},{5,7},{7,5},{8,10},{10,8},{9,1... | collective-permute-start | bytes 393224 | tf_op jit(solution)/shard_map/ppermute | solution.py:278
  23.1 4.3 %collective-permute-start.10 = (f32[128,128]{1,0:T(8,128)S(1)}, f32[128,128]{1,0:T(8,128)S(1)}, u32[]{:S(2)}, u32[]{:S(2)}) collective-permute-start(f32[128,128]{1,0:T(8,128)S(1)} %get-tuple-element.41), channel_id=1, source_target_pairs={{0,4},{4,0},{8,12},{12,8},{1,5},{5,1},{9,13},{13,9},{2,6},{6,2},{1... | collective-permute-start | bytes 196616 | tf_op jit(solution)/shard_map/ppermute | solution.py:278
  24.2 12.7 %collective-permute-start.15 = (bf16[256,256]{1,0:T(8,128)(2,1)S(1)}, bf16[256,256]{1,0:T(8,128)(2,1)S(1)}, u32[]{:S(2)}, u32[]{:S(2)}) collective-permute-start(bf16[256,256]{1,0:T(8,128)(2,1)S(1)} %get-tuple-element.45.refs_4_.refs_2_), channel_id=1, source_target_pairs={{0,2},{2,0},{1,3},{3,1},{4,6},{6,4},{5,7},{7,5},{8,10},{10,8},{9,1... | collective-permute-start | bytes 393224 | tf_op jit(solution)/shard_map/ppermute | solution.py:278
  27.4 5.8 %collective-permute-start.11 = (f32[128,128]{1,0:T(8,128)S(1)}, f32[128,128]{1,0:T(8,128)S(1)}, u32[]{:S(2)}, u32[]{:S(2)}) collective-permute-start(f32[128,128]{1,0:T(8,128)S(1)} %add.6), channel_id=1, source_target_pairs={{0,8},{4,12},{8,0},{12,4},{1,9},{5,13},{9,1},{13,5},{2,10},{6,14},... | collective-permute-start | bytes 196616 | tf_op jit(solution)/shard_map/ppermute | solution.py:278
  28.8 12.4 %collective-permute-start.17 = (bf16[256,256]{1,0:T(8,128)(2,1)S(1)}, bf16[256,256]{1,0:T(8,128)(2,1)S(1)}, u32[]{:S(2)}, u32[]{:S(2)}) collective-permute-start(bf16[256,256]{1,0:T(8,128)(2,1)S(1)} %collective-permute-done.16.refs_4_), channel_id=1, source_target_pairs={{0,1},{1,0},{2,3},{3,2},{4,5},{5,4},{6,7},{7,6},{8,9},{9,8},{10,11... | collective-permute-start | bytes 393224 | tf_op jit(solution)/shard_map/ppermute | solution.py:278
  33.3 4.3 %collective-permute-start.12 = (f32[128,128]{1,0:T(8,128)S(1)}, f32[128,128]{1,0:T(8,128)S(1)}, u32[]{:S(2)}, u32[]{:S(2)}) collective-permute-start(f32[128,128]{1,0:T(8,128)S(1)} %add.7.refs_0_.refs_2_), channel_id=1, source_target_pairs={{0,4},{2,6},{4,0},{6,2},{8,12},{10,14},{12,8},{14,10},{1,5},{3,7},... | collective-permute-start | bytes 196616 | tf_op jit(solution)/shard_map/ppermute | solution.py:278
  33.4 5.2 %collective-permute-start.19 = (f32[128,128]{1,0:T(8,128)S(1)}, f32[128,128]{1,0:T(8,128)S(1)}, u32[]{:S(2)}, u32[]{:S(2)}) collective-permute-start(f32[128,128]{1,0:T(8,128)S(1)} %add.7.refs_0_.refs_2_), channel_id=1, source_target_pairs={{0,6},{2,4},{4,2},{6,0},{8,14},{10,12},{12,10},{14,8},{1,7},{3,5},... | collective-permute-start | bytes 196616 | tf_op jit(solution)/shard_map/ppermute | solution.py:278
  35.0 4.3 %collective-permute-start.18 = (f32[128,128]{1,0:T(8,128)S(1)}, f32[128,128]{1,0:T(8,128)S(1)}, u32[]{:S(2)}, u32[]{:S(2)}) collective-permute-start(f32[128,128]{1,0:T(8,128)S(1)} %add.7.refs_0_.refs_2_), channel_id=1, source_target_pairs={{0,2},{2,0},{4,6},{6,4},{8,10},{10,8},{12,14},{14,12},{1,3},{3,1},... | collective-permute-start | bytes 196616 | tf_op jit(solution)/shard_map/ppermute | solution.py:278
  36.8 4.1 %collective-permute-start.13 = (f32[128,128]{1,0:T(8,128)S(1)}, f32[128,128]{1,0:T(8,128)S(1)}, u32[]{:S(2)}, u32[]{:S(2)}) collective-permute-start(f32[128,128]{1,0:T(8,128)S(1)} %add.7.refs_0_.refs_2_), channel_id=1, source_target_pairs={{0,1},{1,0},{2,3},{3,2},{4,5},{5,4},{6,7},{7,6},{8,9},{9,8},{10,11... | collective-permute-start | bytes 196616 | tf_op jit(solution)/shard_map/ppermute | solution.py:278
  37.6 4.9 %collective-permute-start.14 = (f32[128,128]{1,0:T(8,128)S(1)}, f32[128,128]{1,0:T(8,128)S(1)}, u32[]{:S(2)}, u32[]{:S(2)}) collective-permute-start(f32[128,128]{1,0:T(8,128)S(1)} %collective-permute-done.12.refs_1_.refs_4_), channel_id=1, source_target_pairs={{0,1},{1,0},{2,3},{3,2},{4,5},{5,4},{6,7},{7,6},{8,9},{9,8},{10,11... | collective-permute-start | bytes 196616 | tf_op jit(solution)/shard_map/ppermute | solution.py:278
  38.6 4.2 %collective-permute-start.21 = (f32[128,128]{1,0:T(8,128)S(1)}, f32[128,128]{1,0:T(8,128)S(1)}, u32[]{:S(2)}, u32[]{:S(2)}) collective-permute-start(f32[128,128]{1,0:T(8,128)S(1)} %collective-permute-done.19.refs_6_), channel_id=1, source_target_pairs={{0,1},{1,0},{2,3},{3,2},{4,5},{5,4},{6,7},{7,6},{8,9},{9,8},{10,11... | collective-permute-start | bytes 196616 | tf_op jit(solution)/shard_map/ppermute | solution.py:278
  39.3 3.5 %collective-permute-start.20 = (f32[128,128]{1,0:T(8,128)S(1)}, f32[128,128]{1,0:T(8,128)S(1)}, u32[]{:S(2)}, u32[]{:S(2)}) collective-permute-start(f32[128,128]{1,0:T(8,128)S(1)} %collective-permute-done.18.refs_5_), channel_id=1, source_target_pairs={{0,1},{1,0},{2,3},{3,2},{4,5},{5,4},{6,7},{7,6},{8,9},{9,8},{10,11... | collective-permute-start | bytes 196616 | tf_op jit(solution)/shard_map/ppermute | solution.py:278
